TPU v7x, 256 devices: a whole 4x4x8 slice. The times are simulated.
256 devices in a mesh: fsdp: 16 (over y_lo, x, core), ctx: 16 (over y_hi, z).
Axes of the slice: x: 4, y: 4 (y_hi: 2, y_lo: 2; y = y_hi * 2 + y_lo), z: 8, core: 2. Of those that a mesh axis runs over, the one named last changes fastest.
Arguments:
- q_raw: bfloat16 [16, 4096, 1536], P('fsdp', 'ctx')
- k_raw: bfloat16 [16, 4096, 1536], P('fsdp', 'ctx')
- values_in: bfloat16 [16, 4096, 1536], P('fsdp', 'ctx'), may hold values from -6 to 6
- d_out: bfloat16 [16, 4096, 1536], P('fsdp', 'ctx'), may hold values from -6 to 6
- gains: float32 [2, 128], P(None, 'fsdp')
- tile_device: int32 [16], replicated, may hold values from 0 to 15, as said below
- neighbours: int32 [16, 6], replicated, may hold values from -1 to 15, as said below
Outputs:
- attended: bfloat16 [16, 4096, 1536], P('fsdp', 'ctx')
- dq_raw: bfloat16 [16, 4096, 1536], P('fsdp', 'ctx')
- dk_raw: bfloat16 [16, 4096, 1536], P('fsdp', 'ctx')
- value_grad: bfloat16 [16, 4096, 1536], P('fsdp', 'ctx')
Inputs may be any that keep to these rules, and one draw needn't show every extreme that they name: `tile_device`: the entries are a permutation of the ctx indices, and tile t lies on device 2 (t // 2) or 2 (t // 2) + 1, so the two tiles of a grid column sit on one pair of devices and columns follow in order. `neighbours`: row t holds t in slot 0; slots 1 to 5 hold, in an order that differs from row to row, the other tile of t's column and some of the tiles of the adjacent columns, -1 in the other slots.
All inputs are finite; a program needn't handle non-finite values.
Results may differ from a plain program's by a relative error of at most 0.028.
The roundings to bfloat16 on the way count: a program that leaves them out, or rounds other values in their place, can miss the bound.
Values may be sent and summed in bfloat16 or wider, within the bound.
No kernel may reach another device: no remote copies, remote signals or barrier semaphores. Data moves between devices by JAX's collectives and lax.ppermute only.
A program may use at most 192 MiB of HBM per device.

v0:
```python
import math
from functools import partial

import jax
import jax.numpy as jnp
from jax import lax
from jax.experimental import pallas as pl
from jax.experimental.pallas import tpu as pltpu
from jax.sharding import PartitionSpec as P

EPSILON = 1e-06
ROWS = 256
HD = 128
HB = 2
LOW = -1e30
BF = jnp.bfloat16
F32 = jnp.float32

NT = (((1,), (1,)), ((), ()))
TN = (((0,), (0,)), ((), ()))
NN = (((1,), (0,)), ((), ()))


def dot(a, b, dims):
    return lax.dot_general(a, b, dims, preferred_element_type=F32)


def allowed(sc, query_dev, key_dev):
    count = sc[1]
    inside = jnp.logical_and(
        jnp.logical_and(query_dev >= 0, query_dev < count),
        jnp.logical_and(key_dev >= 0, key_dev < count),
    )

    def tile_at(dev):
        first = 2 * (jnp.clip(dev, 0, count - 1) // 2)
        return jnp.where(sc[2 + first] == dev, first, first + 1)

    query_tile, key_tile = tile_at(query_dev), tile_at(key_dev)
    base = 2 + count + query_tile * 6
    hit = sc[base] == key_tile
    for slot in range(1, 6):
        hit = jnp.logical_or(hit, sc[base + slot] == key_tile)
    return jnp.logical_and(inside, hit)


def around(sc):
    me = sc[0]
    odd = me % 2 == 1
    partner = jnp.where(odd, me - 1, me + 1)
    near = jnp.where(odd, me + 1, me - 1)
    far = jnp.where(odd, me + 2, me - 2)
    return me, partner, near, far


def normed(raw, gain_row):
    floats = raw.astype(F32)
    inverse = lax.rsqrt(jnp.mean(floats * floats, axis=1, keepdims=True) + EPSILON)
    return (floats * inverse * gain_row).astype(BF)


def denormed(raw, gain_row, upstream):
    floats = raw.astype(F32)
    inverse = lax.rsqrt(jnp.mean(floats * floats, axis=1, keepdims=True) + EPSILON)
    scaled = upstream * gain_row
    inner = jnp.mean(floats * scaled, axis=1, keepdims=True)
    return (inverse * scaled - floats * (inverse * inverse * inverse * inner)).astype(BF)


def cols(j):
    return slice(j * HD, (j + 1) * HD)


def forward_unit(kn, v, qn, m_ref, l_ref, acc_ref, j, first=False):
    s = dot(kn, qn, NT) * (math.log2(math.e) / math.sqrt(HD))
    top = jnp.max(s, axis=0, keepdims=True)
    if first:
        p = jnp.exp2(s - top)
        m_ref[j] = top
        l_ref[j] = jnp.sum(p, axis=0, keepdims=True)
        acc_ref[cols(j), :] = dot(v, p.astype(BF), TN)
        return
    old = m_ref[j]
    new = jnp.maximum(old, top)
    shrink = jnp.exp2(old - new)
    p = jnp.exp2(s - new)
    m_ref[j] = new
    l_ref[j] = l_ref[j] * shrink + jnp.sum(p, axis=0, keepdims=True)
    acc_ref[cols(j), :] = acc_ref[cols(j), :] * shrink + dot(v, p.astype(BF), TN)


def backward_unit(kn, v, qn, d_out, lse, delta):
    s = dot(kn, qn, NT) * (math.log2(math.e) / math.sqrt(HD))
    p = jnp.exp2(s - lse)
    dp = dot(v, d_out, NT)
    return p, (p * (dp - delta)).astype(BF)


def row(ref, index):
    return ref[pl.ds(index, 1), :]


def partner_forward(sc, g, q, ke, ve, kf, vf, o_ref, ml_ref, kne, knf, qn, m_ref, l_ref, acc_ref):
    step = pl.program_id(0)
    heads = pl.num_programs(0) * HB
    me, partner, near, far = around(sc)
    for j in range(HB):
        qn[:, cols(j)] = normed(q[:, cols(j)], g[0:1, :])
        kne[:, cols(j)] = normed(ke[:, cols(j)], g[1:2, :])
        knf[:, cols(j)] = normed(kf[:, cols(j)], g[1:2, :])
    m_ref[...] = jnp.full_like(m_ref, LOW)
    l_ref[...] = jnp.zeros_like(l_ref)
    acc_ref[...] = jnp.zeros_like(acc_ref)
    for key_dev, kn, v in ((near, kne, ve), (far, knf, vf)):
        @pl.when(allowed(sc, partner, key_dev))
        def _():
            for j in range(HB):
                forward_unit(
                    kn[:, cols(j)], v[:, cols(j)], qn[:, cols(j)], m_ref, l_ref, acc_ref, j
                )
    for j in range(HB):
        total = l_ref[j]
        ml_ref[pl.ds(step * HB + j, 1), :] = m_ref[j]
        ml_ref[pl.ds(heads + step * HB + j, 1), :] = total
        share = jnp.where(total > 0.0, 1.0 / jnp.where(total > 0.0, total, 1.0), 0.0)
        o_ref[cols(j), :] = (acc_ref[cols(j), :] * share).astype(BF)


def own_forward(
    sc, g, q, k, v, kp, vp, kne, ve, knf, vf, acc_ref, ml_ref, qn, knx, knp, m_ref, l_ref
):
    step = pl.program_id(0)
    heads = pl.num_programs(0) * HB
    me, partner, near, far = around(sc)
    for j in range(HB):
        qn[:, cols(j)] = normed(q[:, cols(j)], g[0:1, :])
        knx[:, cols(j)] = normed(k[:, cols(j)], g[1:2, :])
        knp[:, cols(j)] = normed(kp[:, cols(j)], g[1:2, :])
    for j in range(HB):
        forward_unit(
            knx[:, cols(j)], v[:, cols(j)], qn[:, cols(j)], m_ref, l_ref, acc_ref, j, first=True
        )
    for key_dev, kn, val in ((partner, knp, vp), (near, kne, ve), (far, knf, vf)):
        @pl.when(allowed(sc, me, key_dev))
        def _():
            for j in range(HB):
                forward_unit(
                    kn[:, cols(j)], val[:, cols(j)], qn[:, cols(j)], m_ref, l_ref, acc_ref, j
                )
    for j in range(HB):
        ml_ref[pl.ds(step * HB + j, 1), :] = m_ref[j]
        ml_ref[pl.ds(heads + step * HB + j, 1), :] = l_ref[j]


def merge(acc_ref, ml_ref, o_ret, ml_ret, d_out, att_ref, st_ref):
    step = pl.program_id(0)
    heads = pl.num_programs(0) * HB
    for j in range(HB):
        h = step * HB + j
        m1, l1 = row(ml_ref, h), row(ml_ref, heads + h)
        m2, l2 = row(ml_ret, h), row(ml_ret, heads + h)
        m = jnp.maximum(m1, m2)
        a1 = jnp.exp2(m1 - m)
        a2 = jnp.exp2(m2 - m) * l2
        total = l1 * a1 + a2
        inv = 1.0 / total
        out = acc_ref[cols(j), :] * (a1 * inv) + o_ret[cols(j), :].astype(F32) * (a2 * inv)
        low = out.astype(BF)
        att_ref[:, cols(j)] = jnp.transpose(low)
        grads = jnp.transpose(d_out[:, cols(j)]).astype(F32)
        st_ref[pl.ds(h, 1), :] = m + jnp.log2(total)
        st_ref[pl.ds(heads + h, 1), :] = jnp.sum(low.astype(F32) * grads, axis=0, keepdims=True)


def own_query_grads(
    sc, qn, do, st, knx, v, knp, vp, kne, ve, knf, vf, dq_ref, dk_ref, dv_ref
):
    step = pl.program_id(0)
    heads = pl.num_programs(0) * HB
    me, partner, near, far = around(sc)
    for j in range(HB):
        c = cols(j)
        p, ds = backward_unit(
            knx[:, c], v[:, c], qn[:, c], do[:, c],
            row(st, step * HB + j), row(st, heads + step * HB + j),
        )
        dq_ref[c, :] = dot(knx[:, c], ds, TN)
        dk_ref[:, c] = dot(ds, qn[:, c], NN)
        dv_ref[:, c] = dot(p.astype(BF), do[:, c], NN)
    for key_dev, kn, val in ((partner, knp, vp), (near, kne, ve), (far, knf, vf)):
        @pl.when(allowed(sc, me, key_dev))
        def _():
            for j in range(HB):
                c = cols(j)
                p, ds = backward_unit(
                    kn[:, c], val[:, c], qn[:, c], do[:, c],
                    row(st, step * HB + j), row(st, heads + step * HB + j),
                )
                dq_ref[c, :] += dot(kn[:, c], ds, TN)


def partner_query_grads(sc, qn, do, st, kne, ve, knf, vf, dq_ref, acc_ref):
    step = pl.program_id(0)
    heads = pl.num_programs(0) * HB
    me, partner, near, far = around(sc)
    acc_ref[...] = jnp.zeros_like(acc_ref)
    for key_dev, kn, val in ((near, kne, ve), (far, knf, vf)):
        @pl.when(allowed(sc, partner, key_dev))
        def _():
            for j in range(HB):
                c = cols(j)
                p, ds = backward_unit(
                    kn[:, c], val[:, c], qn[:, c], do[:, c],
                    row(st, step * HB + j), row(st, heads + step * HB + j),
                )
                acc_ref[c, :] += dot(kn[:, c], ds, TN)
    dq_ref[...] = acc_ref[...].astype(BF)


def key_units(sc, key_dev, kn, v, queries, dk_ref, dv_ref, step, heads):
    for query_dev, qn, do, st in queries:
        @pl.when(allowed(sc, query_dev, key_dev))
        def _():
            for j in range(HB):
                c = cols(j)
                p, ds = backward_unit(
                    kn[:, c], v[:, c], qn[:, c], do[:, c],
                    row(st, step * HB + j), row(st, heads + step * HB + j),
                )
                dk_ref[:, c] += dot(ds, qn[:, c], NN)
                dv_ref[:, c] += dot(p.astype(BF), do[:, c], NN)


def partner_key_grads(
    sc, g, knp, vp, qe, doe, ste, qf, dof, stf, dk_ref, dv_ref, qne, qnf, dka, dva
):
    step = pl.program_id(0)
    heads = pl.num_programs(0) * HB
    me, partner, near, far = around(sc)
    for j in range(HB):
        qne[:, cols(j)] = normed(qe[:, cols(j)], g[0:1, :])
        qnf[:, cols(j)] = normed(qf[:, cols(j)], g[0:1, :])
    dka[...] = jnp.zeros_like(dka)
    dva[...] = jnp.zeros_like(dva)
    key_units(
        sc, partner, knp, vp, ((near, qne, doe, ste), (far, qnf, dof, stf)), dka, dva, step, heads
    )
    dk_ref[...] = dka[...].astype(BF)
    dv_ref[...] = dva[...].astype(BF)


def own_key_grads(
    sc, knx, v, qnp, dop, stp, qne, doe, ste, qnf, dof, stf, dk0, dv0, dk_ref, dv_ref
):
    step = pl.program_id(0)
    heads = pl.num_programs(0) * HB
    me, partner, near, far = around(sc)
    dk_ref[...] = dk0[...]
    dv_ref[...] = dv0[...]
    key_units(
        sc, me, knx, v,
        ((partner, qnp, dop, stp), (near, qne, doe, ste), (far, qnf, dof, stf)),
        dk_ref, dv_ref, step, heads,
    )


def finish(g, dqt, dqr, dk, dkr, dv, dvr, q, k, dq_out, dk_out, dv_out):
    scale = 1.0 / math.sqrt(HD)
    for j in range(HB):
        c = cols(j)
        dq = jnp.transpose(dqt[c, :] + dqr[c, :].astype(F32)) * scale
        dq_out[:, c] = denormed(q[:, c], g[0:1, :], dq)
        dk_out[:, c] = denormed(k[:, c], g[1:2, :], (dk[:, c] + dkr[:, c].astype(F32)) * scale)
        dv_out[:, c] = (dv[:, c] + dvr[:, c].astype(F32)).astype(BF)


WIDE = "wide"
TALL = "tall"
FULL = "full"


def spec(kind, arr):
    if kind == WIDE:
        return pl.BlockSpec((ROWS, HB * HD), lambda i, *_: (0, i))
    if kind == TALL:
        return pl.BlockSpec((HB * HD, ROWS), lambda i, *_: (i, 0))
    return pl.BlockSpec(arr.shape, lambda i, *_: (0,) * len(arr.shape))


def run(name, body, scalars, ins, outs, scratch=(), units=1):
    features = next(a.shape[1] for kind, a in ins if kind == WIDE)
    shapes = [jax.ShapeDtypeStruct(s, d) for _, s, d in outs]
    grid_spec = pltpu.PrefetchScalarGridSpec(
        num_scalar_prefetch=len(scalars),
        grid=(features // (HB * HD),),
        in_specs=[spec(kind, a) for kind, a in ins],
        out_specs=[spec(o[0], s) for o, s in zip(outs, shapes)],
        scratch_shapes=list(scratch),
    )
    heads = features // HD
    flops = units * heads * 6 * 2 * ROWS * ROWS * HD
    return pl.pallas_call(
        body,
        name=name,
        grid_spec=grid_spec,
        out_shape=shapes,
        cost_estimate=pl.CostEstimate(
            flops=flops, transcendentals=units * heads * ROWS * ROWS, bytes_accessed=4 << 20
        ),
        compiler_params=pltpu.CompilerParams(
            dimension_semantics=("arbitrary",), vmem_limit_bytes=24 << 20
        ),
    )(*scalars, *[a for _, a in ins])


def after(values, *others):
    out = lax.optimization_barrier(tuple(values) + tuple(others))
    return out[: len(values)]


def local(q_raw, k_raw, values_in, d_out, gains, tile_device, neighbours):
    count = lax.axis_size("ctx")
    inner = [(d, d ^ 1) for d in range(count)]
    outer = []
    for d in range(1, count - 1, 2):
        outer += [(d, d + 1), (d + 1, d)]
    q, k, v, do = q_raw[0], k_raw[0], values_in[0], d_out[0]
    features = q.shape[1]
    heads = features // HD

    def across(value):
        return lax.ppermute(value, "ctx", inner)

    def beyond(value):
        return lax.ppermute(value, "ctx", outer)

    kp, vp, ke, ve = across(k), across(v), beyond(k), beyond(v)
    g = lax.all_gather(gains, "fsdp", axis=1, tiled=True)
    scalars = jnp.concatenate(
        [
            jnp.stack([lax.axis_index("ctx"), jnp.int32(count)]).astype(jnp.int32),
            tile_device,
            neighbours.reshape(-1),
        ]
    )
    q1, do1 = after((q, do), kp, vp)
    qp, dop = across(q1), across(do1)
    kf, vf = beyond(kp), beyond(vp)
    q2, do2 = after((q, do), kf, vf)
    qe, doe = beyond(q2), beyond(do2)
    qp3, dop3 = after((qp, dop), qe, doe)
    qf, dof = beyond(qp3), beyond(dop3)

    wide_bf = (WIDE, (ROWS, features), BF)
    wide_f = (WIDE, (ROWS, features), F32)
    tall_bf = (TALL, (features, ROWS), BF)
    tall_f = (TALL, (features, ROWS), F32)
    stats = (FULL, (2 * heads, ROWS), F32)
    rows_scratch = pltpu.VMEM((HB, 1, ROWS), F32)
    acc_t = pltpu.VMEM((HB * HD, ROWS), F32)
    acc_w = pltpu.VMEM((ROWS, HB * HD), F32)

    def wide(*arrays):
        return [(WIDE, a) for a in arrays]

    op, mlp, kne, knf, qnp = run(
        "partner_forward", partner_forward, (scalars,),
        [(FULL, g)] + wide(qp, ke, ve, kf, vf),
        [tall_bf, stats, wide_bf, wide_bf, wide_bf],
        (rows_scratch, rows_scratch, acc_t), 1,
    )
    o_ret, ml_ret = across(op), across(mlp)
    acc, ml, qnx, knx, knp = run(
        "own_forward", own_forward, (scalars,),
        [(FULL, g)] + wide(q, k, v, kp, vp, kne, ve, knf, vf),
        [tall_f, stats, wide_bf, wide_bf, wide_bf],
        (rows_scratch, rows_scratch), 2,
    )
    att, st = run(
        "merge", merge, (),
        [(TALL, acc), (FULL, ml), (TALL, o_ret), (FULL, ml_ret)] + wide(do),
        [wide_bf, stats],
    )
    stp, ste = across(st), beyond(st)
    stf = beyond(stp)
    dqt, dk0, dv0 = run(
        "own_query_grads", own_query_grads, (scalars,),
        wide(qnx, do) + [(FULL, st)] + wide(knx, v, knp, vp, kne, ve, knf, vf),
        [tall_f, wide_f, wide_f], (), 3,
    )
    (dqp,) = run(
        "partner_query_grads", partner_query_grads, (scalars,),
        wide(qnp, dop) + [(FULL, stp)] + wide(kne, ve, knf, vf),
        [tall_bf], (acc_t,), 1,
    )
    dqr = across(dqp)
    dkp, dvp, qne, qnf = run(
        "partner_key_grads", partner_key_grads, (scalars,),
        [(FULL, g)] + wide(knp, vp, qe, doe) + [(FULL, ste)] + wide(qf, dof) + [(FULL, stf)],
        [wide_bf, wide_bf, wide_bf, wide_bf], (acc_w, acc_w), 2,
    )
    dkr, dvr = across(dkp), across(dvp)
    dk1, dv1 = run(
        "own_key_grads", own_key_grads, (scalars,),
        wide(knx, v, qnp, dop) + [(FULL, stp)] + wide(qne, doe) + [(FULL, ste)]
        + wide(qnf, dof) + [(FULL, stf)] + wide(dk0, dv0),
        [wide_f, wide_f], (), 3,
    )
    dq_out, dk_out, dv_out = run(
        "finish", finish, (),
        [(FULL, g), (TALL, dqt), (TALL, dqr)] + wide(dk1, dkr, dv1, dvr, q, k),
        [wide_bf, wide_bf, wide_bf],
    )
    return att[None], dq_out[None], dk_out[None], dv_out[None]


def solution(mesh):
    tokens = P("fsdp", "ctx", None)
    return jax.shard_map(
        local,
        mesh=mesh,
        in_specs=(tokens, tokens, tokens, tokens, P(None, "fsdp"), P(), P()),
        out_specs=(tokens, tokens, tokens, tokens),
        check_vma=False,
    )
```

profile of v0, /device:TPU:16, one launch (start us, length us, event | category | flops | bytes accessed | tf_op | source)
XLA Modules:
  0.0 231.8 jit_solution(10403937678294456937)
XLA Ops:
  0.6 2.0 collective-permute-start
  2.7 18.6 %collective-permute-done.kp = bf16[256,1536]{1,0:T(8,128)(2,1)S(1)} collective-permute-done((bf16[256,1536]{1,0:T(8,128)(2,1)}, bf16[256,1536]{1,0:T(8,128)(2,1)S(1)}, u32[]{:S(2)}, u32[]{:S(2)}) %collective-permute-start) | collective-permute-done | bytes 786464 | tf_op jit(solution)/shard_map/ppermute | solution.py:332
  21.3 7.5 %collective-permute-start.5 = (bf16[256,1536]{1,0:T(8,128)(2,1)S(1)}, bf16[256,1536]{1,0:T(8,128)(2,1)S(1)}, u32[]{:S(2)}, u32[]{:S(2)}) collective-permute-start(bf16[256,1536]{1,0:T(8,128)(2,1)S(1)} %collective-permute-done.kp), channel_id=1, source_target_pairs={{1,2},{2,1},{3,4},{4,3},{5,6},{6,5},{7,8},{8,7},{9,10},{10,9},{11,... | collective-permute-start | bytes 2359304 | tf_op jit(solution)/shard_map/ppermute | solution.py:335
  29.8 7.5 %collective-permute-done.1.vp = bf16[256,1536]{1,0:T(8,128)(2,1)S(1)} collective-permute-done((bf16[256,1536]{1,0:T(8,128)(2,1)}, bf16[256,1536]{1,0:T(8,128)(2,1)S(1)}, u32[]{:S(2)}, u32[]{:S(2)}) %collective-permute-start.1) | collective-permute-done | bytes 786464 | tf_op jit(solution)/shard_map/ppermute | solution.py:332
  37.2 7.3 %collective-permute-start.6 = (bf16[256,1536]{1,0:T(8,128)(2,1)S(1)}, bf16[256,1536]{1,0:T(8,128)(2,1)S(1)}, u32[]{:S(2)}, u32[]{:S(2)}) collective-permute-start(bf16[256,1536]{1,0:T(8,128)(2,1)S(1)} %collective-permute-done.1.vp), channel_id=1, source_target_pairs={{1,2},{2,1},{3,4},{4,3},{5,6},{6,5},{7,8},{8,7},{9,10},{10,9},{11,... | collective-permute-start | bytes 2359304 | tf_op jit(solution)/shard_map/ppermute | solution.py:335
  44.6 2.1 collective-permute-start.3
  46.7 7.4 %collective-permute-start.4 = (bf16[256,1536]{1,0:T(8,128)(2,1)}, bf16[256,1536]{1,0:T(8,128)(2,1)S(1)}, u32[]{:S(2)}, u32[]{:S(2)}) collective-permute-start(bf16[256,1536]{1,0:T(8,128)(2,1)} %bitcast.32), channel_id=1, source_target_pairs={{1,2},{2,1},{3,4},{4,3},{5,6},{6,5},{7,8},{8,7},{9,10},{10,9},{11,... | collective-permute-start | bytes 2359304 | tf_op jit(solution)/shard_map/ppermute | solution.py:335
  55.1 2.0 collective-permute-start.9
  57.1 6.2 %collective-permute-done.6.vf = bf16[256,1536]{1,0:T(8,128)(2,1)S(1)} collective-permute-done((bf16[256,1536]{1,0:T(8,128)(2,1)S(1)}, bf16[256,1536]{1,0:T(8,128)(2,1)S(1)}, u32[]{:S(2)}, u32[]{:S(2)}) %collective-permute-start.6) | collective-permute-done | bytes 786464 | tf_op jit(solution)/shard_map/ppermute | solution.py:335
  63.2 7.3 %collective-permute-start.12 = (bf16[256,1536]{1,0:T(8,128)(2,1)}, bf16[256,1536]{1,0:T(8,128)(2,1)}, u32[]{:S(2)}, u32[]{:S(2)}) collective-permute-start(bf16[256,1536]{1,0:T(8,128)(2,1)} %bitcast.16), channel_id=1, source_target_pairs={{1,2},{2,1},{3,4},{4,3},{5,6},{6,5},{7,8},{8,7},{9,10},{10,9},{11,... | collective-permute-start | bytes 2359304 | tf_op jit(solution)/shard_map/ppermute | solution.py:335
  70.6 9.6 %collective-permute-done.3.ke = bf16[256,1536]{1,0:T(8,128)(2,1)S(1)} collective-permute-done((bf16[256,1536]{1,0:T(8,128)(2,1)}, bf16[256,1536]{1,0:T(8,128)(2,1)S(1)}, u32[]{:S(2)}, u32[]{:S(2)}) %collective-permute-start.3) | collective-permute-done | bytes 786464 | tf_op jit(solution)/shard_map/ppermute | solution.py:335
  81.0 7.3 %collective-permute-start.13 = (bf16[256,1536]{1,0:T(8,128)(2,1)}, bf16[256,1536]{1,0:T(8,128)(2,1)}, u32[]{:S(2)}, u32[]{:S(2)}) collective-permute-start(bf16[256,1536]{1,0:T(8,128)(2,1)} %bitcast.28), channel_id=1, source_target_pairs={{1,2},{2,1},{3,4},{4,3},{5,6},{6,5},{7,8},{8,7},{9,10},{10,9},{11,... | collective-permute-start | bytes 2359304 | tf_op jit(solution)/shard_map/ppermute | solution.py:335
  89.2 20.5 %all-gather = f32[16,8,2]{1,2,0:T(2,128)S(1)} all-gather(f32[1,8,2]{1,2,0:T(2,128)} %bitcast.36), channel_id=1, replica_groups=mesh['fsdp'=16,'ctx'=16] {'fsdp'}, dimensions={0}, use_global_device_ids=true | all-gather | bytes 1088 | tf_op jit(solution)/shard_map/all_gather | solution.py:338
  110.6 1.1 copy-done.7
  111.8 1.1 copy-done.9
  112.9 8.5 %partner_forward.1 = (bf16[1536,256]{1,0:T(8,128)(2,1)S(1)}, f32[24,256]{1,0:T(8,128)S(1)}, bf16[256,1536]{1,0:T(8,128)(2,1)S(1)}, bf16[256,1536]{1,0:T(8,128)(2,1)S(1)}, bf16[256,1536]{1,0:T(8,128)(2,1)S(1)}) custom-call(s32[114]{0:T(128)S(1)} %pad_add_fusion.sc, f32[2,128]{1,0:T(2,128)S(1)} %bitcast.23, bf16[256,1536]{1,0:T(8,128)(2,1)} %collective-permute-done.2.q, ...), custom_call_target="tpu_custom_call" | custom-call | flops 1207959552 | bytes 4194304 | tf_op jit(solution)/shard_map/partner_forward/pallas_call | solution.py:302
  121.5 7.4 %collective-permute-done.13.doe = bf16[256,1536]{1,0:T(8,128)(2,1)} collective-permute-done((bf16[256,1536]{1,0:T(8,128)(2,1)}, bf16[256,1536]{1,0:T(8,128)(2,1)}, u32[]{:S(2)}, u32[]{:S(2)}) %collective-permute-start.13) | collective-permute-done | bytes 786464 | tf_op jit(solution)/shard_map/ppermute | solution.py:335
  129.0 7.1 %collective-permute-start.15 = (bf16[256,1536]{1,0:T(8,128)(2,1)}, bf16[256,1536]{1,0:T(8,128)(2,1)S(1)}, u32[]{:S(2)}, u32[]{:S(2)}) collective-permute-start(bf16[256,1536]{1,0:T(8,128)(2,1)} %collective-permute-done.2.q), channel_id=1, source_target_pairs={{1,2},{2,1},{3,4},{4,3},{5,6},{6,5},{7,8},{8,7},{9,10},{10,9},{11,... | collective-permute-start | bytes 2359304 | tf_op jit(solution)/shard_map/ppermute | solution.py:335
  136.1 2.3 collective-permute-start.16
  138.6 11.5 %own_forward.1 = (f32[1536,256]{1,0:T(8,128)S(1)}, f32[24,256]{1,0:T(8,128)S(1)}, bf16[256,1536]{1,0:T(8,128)(2,1)S(1)}, bf16[256,1536]{1,0:T(8,128)(2,1)S(1)}, bf16[256,1536]{1,0:T(8,128)(2,1)S(1)}) custom-call(s32[114]{0:T(128)S(1)} %pad_add_fusion.sc, f32[2,128]{1,0:T(2,128)S(1)} %bitcast.24, bf16[256,1536]{1,0:T(8,128)(2,1)S(1)} %bitcast.17, ...), custom_call_target="tpu_custom_call" | custom-call | flops 2415919104 | bytes 4194304 | tf_op jit(solution)/shard_map/own_forward/pallas_call | solution.py:302
  150.1 2.7 %merge.1 = (bf16[256,1536]{1,0:T(8,128)(2,1)}, f32[24,256]{1,0:T(8,128)S(1)}) custom-call(f32[1536,256]{1,0:T(8,128)S(1)} %get-tuple-element.37.acc_ref, f32[24,256]{1,0:T(8,128)S(1)} %get-tuple-element.38.ml_ref, bf16[1536,256]{1,0:T(8,128)(2,1)S(1)} %collective-permute-done.7.o_ret, f32[24,256]{1,0:T(8,128)S(1)} %collective-permute-done.8.ml_ret, ...), custom_call_target="tpu_custom_call" | custom-call | flops 1207959552 | bytes 4194304 | tf_op jit(solution)/shard_map/merge/pallas_call | solution.py:302
  152.7 10.3 %collective-permute-start.10 = (f32[24,256]{1,0:T(8,128)S(1)}, f32[24,256]{1,0:T(8,128)S(1)}, u32[]{:S(2)}, u32[]{:S(2)}) collective-permute-start(f32[24,256]{1,0:T(8,128)S(1)} %get-tuple-element.43.st), channel_id=1, source_target_pairs={{0,1},{1,0},{2,3},{3,2},{4,5},{5,4},{6,7},{7,6},{8,9},{9,8},{10,11... | collective-permute-start | bytes 73736 | tf_op jit(solution)/shard_map/ppermute | solution.py:332
  163.0 5.2 %collective-permute-start.14 = (f32[24,256]{1,0:T(8,128)S(1)}, f32[24,256]{1,0:T(8,128)S(1)}, u32[]{:S(2)}, u32[]{:S(2)}) collective-permute-start(f32[24,256]{1,0:T(8,128)S(1)} %get-tuple-element.43.st), channel_id=1, source_target_pairs={{1,2},{2,1},{3,4},{4,3},{5,6},{6,5},{7,8},{8,7},{9,10},{10,9},{11,... | collective-permute-start | bytes 73736 | tf_op jit(solution)/shard_map/ppermute | solution.py:335
  168.2 4.3 %collective-permute-start.17 = (f32[24,256]{1,0:T(8,128)S(1)}, f32[24,256]{1,0:T(8,128)S(1)}, u32[]{:S(2)}, u32[]{:S(2)}) collective-permute-start(f32[24,256]{1,0:T(8,128)S(1)} %collective-permute-done.10.st.stp), channel_id=1, source_target_pairs={{1,2},{2,1},{3,4},{4,3},{5,6},{6,5},{7,8},{8,7},{9,10},{10,9},{11,... | collective-permute-start | bytes 73736 | tf_op jit(solution)/shard_map/ppermute | solution.py:335
  172.5 5.3 %partner_query_grads.1 = bf16[1536,256]{1,0:T(8,128)(2,1)S(1)} custom-call(s32[114]{0:T(128)S(1)} %pad_add_fusion.sc, bf16[256,1536]{1,0:T(8,128)(2,1)S(1)} %get-tuple-element.47.qn.qnp, bf16[256,1536]{1,0:T(8,128)(2,1)S(1)} %collective-permute-done.9.do.dop, f32[24,256]{1,0:T(8,128)S(1)} %collective-permute-done.10.st.stp, ...), custom_call_target="tpu_custom_call" | custom-call | flops 1207959552 | bytes 4194304 | tf_op jit(solution)/shard_map/partner_query_grads/pallas_call | solution.py:302
  177.9 7.5 %partner_key_grads.1 = (bf16[256,1536]{1,0:T(8,128)(2,1)S(1)}, bf16[256,1536]{1,0:T(8,128)(2,1)S(1)}, bf16[256,1536]{1,0:T(8,128)(2,1)S(1)}, bf16[256,1536]{1,0:T(8,128)(2,1)S(1)}) custom-call(s32[114]{0:T(128)S(1)} %pad_add_fusion.sc, f32[2,128]{1,0:T(2,128)S(1)} %bitcast.25, bf16[256,1536]{1,0:T(8,128)(2,1)S(1)} %get-tuple-element.45.knp, ...), custom_call_target="tpu_custom_call" | custom-call | flops 2415919104 | bytes 4194304 | tf_op jit(solution)/shard_map/partner_key_grads/pallas_call | solution.py:302
  185.7 2.0 collective-permute-start.19
  187.7 10.3 %own_query_grads.1 = (f32[1536,256]{1,0:T(8,128)S(1)}, f32[256,1536]{1,0:T(8,128)S(1)}, f32[256,1536]{1,0:T(8,128)S(1)}) custom-call(s32[114]{0:T(128)S(1)} %pad_add_fusion.sc, bf16[256,1536]{1,0:T(8,128)(2,1)S(1)} %get-tuple-element.42.qn, bf16[256,1536]{1,0:T(8,128)(2,1)S(1)} %bitcast.30, f32[24,256]{1,0:T(8,128)S(1)} %get-tuple-element.43.st, ...), custom_call_target="tpu_custom_call" | custom-call | flops 3623878656 | bytes 4194304 | tf_op jit(solution)/shard_map/own_query_grads/pallas_call | solution.py:302
  198.0 13.8 %own_key_grads.1 = (f32[256,1536]{1,0:T(8,128)S(1)}, f32[256,1536]{1,0:T(8,128)S(1)}) custom-call(s32[114]{0:T(128)S(1)} %pad_add_fusion.sc, bf16[256,1536]{1,0:T(8,128)(2,1)S(1)} %get-tuple-element.44.knx, bf16[256,1536]{1,0:T(8,128)(2,1)S(1)} %bitcast.35, bf16[256,1536]{1,0:T(8,128)(2,1)S(1)} %get-tuple-element.47.qn.qnp, ...), custom_call_target="tpu_custom_call" | custom-call | flops 3623878656 | bytes 4194304 | tf_op jit(solution)/shard_map/own_key_grads/pallas_call | solution.py:302
  211.8 3.4 %collective-permute-done.18.dkr = bf16[256,1536]{1,0:T(8,128)(2,1)S(1)} collective-permute-done((bf16[256,1536]{1,0:T(8,128)(2,1)S(1)}, bf16[256,1536]{1,0:T(8,128)(2,1)S(1)}, u32[]{:S(2)}, u32[]{:S(2)}) %collective-permute-start.18) | collective-permute-done | bytes 786464 | tf_op jit(solution)/shard_map/ppermute | solution.py:332
  215.2 12.3 %collective-permute-done.19.dvr = bf16[256,1536]{1,0:T(8,128)(2,1)S(1)} collective-permute-done((bf16[256,1536]{1,0:T(8,128)(2,1)S(1)}, bf16[256,1536]{1,0:T(8,128)(2,1)S(1)}, u32[]{:S(2)}, u32[]{:S(2)}) %collective-permute-start.19) | collective-permute-done | bytes 786464 | tf_op jit(solution)/shard_map/ppermute | solution.py:332
  227.5 4.3 %finish.1 = (bf16[256,1536]{1,0:T(8,128)(2,1)}, bf16[256,1536]{1,0:T(8,128)(2,1)}, bf16[256,1536]{1,0:T(8,128)(2,1)}) custom-call(f32[2,128]{1,0:T(2,128)S(1)} %bitcast.26, f32[1536,256]{1,0:T(8,128)S(1)} %get-tuple-element.46.dqt, bf16[1536,256]{1,0:T(8,128)(2,1)S(1)} %collective-permute-done.11.dqr, f32[256,1536]{1,0:T(8,128)S(1)} %get-tuple-element.57.dk, ...), custom_call_target="tpu_custom_call" | custom-call | flops 1207959552 | bytes 4194304 | tf_op jit(solution)/shard_map/finish/pallas_call | solution.py:302
  (42 shorter events, 5.1 us)
Async XLA Ops:
  0.6 20.7 %collective-permute-start = (bf16[256,1536]{1,0:T(8,128)(2,1)}, bf16[256,1536]{1,0:T(8,128)(2,1)S(1)}, u32[]{:S(2)}, u32[]{:S(2)}) collective-permute-start(bf16[256,1536]{1,0:T(8,128)(2,1)} %bitcast.19), channel_id=1, source_target_pairs={{0,1},{1,0},{2,3},{3,2},{4,5},{5,4},{6,7},{7,6},{8,9},{9,8},{10,11... | collective-permute-start | bytes 2359304 | tf_op jit(solution)/shard_map/ppermute | solution.py:332
  2.6 34.6 %collective-permute-start.1 = (bf16[256,1536]{1,0:T(8,128)(2,1)}, bf16[256,1536]{1,0:T(8,128)(2,1)S(1)}, u32[]{:S(2)}, u32[]{:S(2)}) collective-permute-start(bf16[256,1536]{1,0:T(8,128)(2,1)} %bitcast.31), channel_id=1, source_target_pairs={{0,1},{1,0},{2,3},{3,2},{4,5},{5,4},{6,7},{7,6},{8,9},{9,8},{10,11... | collective-permute-start | bytes 2359304 | tf_op jit(solution)/shard_map/ppermute | solution.py:332
  21.3 32.8 %collective-permute-start.5 = (bf16[256,1536]{1,0:T(8,128)(2,1)S(1)}, bf16[256,1536]{1,0:T(8,128)(2,1)S(1)}, u32[]{:S(2)}, u32[]{:S(2)}) collective-permute-start(bf16[256,1536]{1,0:T(8,128)(2,1)S(1)} %collective-permute-done.kp), channel_id=1, source_target_pairs={{1,2},{2,1},{3,4},{4,3},{5,6},{6,5},{7,8},{8,7},{9,10},{10,9},{11,... | collective-permute-start | bytes 2359304 | tf_op jit(solution)/shard_map/ppermute | solution.py:335
  28.9 0.9 copy-start.4
  37.2 26.0 %collective-permute-start.6 = (bf16[256,1536]{1,0:T(8,128)(2,1)S(1)}, bf16[256,1536]{1,0:T(8,128)(2,1)S(1)}, u32[]{:S(2)}, u32[]{:S(2)}) collective-permute-start(bf16[256,1536]{1,0:T(8,128)(2,1)S(1)} %collective-permute-done.1.vp), channel_id=1, source_target_pairs={{1,2},{2,1},{3,4},{4,3},{5,6},{6,5},{7,8},{8,7},{9,10},{10,9},{11,... | collective-permute-start | bytes 2359304 | tf_op jit(solution)/shard_map/ppermute | solution.py:335
  44.6 35.6 %collective-permute-start.3 = (bf16[256,1536]{1,0:T(8,128)(2,1)}, bf16[256,1536]{1,0:T(8,128)(2,1)S(1)}, u32[]{:S(2)}, u32[]{:S(2)}) collective-permute-start(bf16[256,1536]{1,0:T(8,128)(2,1)} %bitcast.20), channel_id=1, source_target_pairs={{1,2},{2,1},{3,4},{4,3},{5,6},{6,5},{7,8},{8,7},{9,10},{10,9},{11,... | collective-permute-start | bytes 2359304 | tf_op jit(solution)/shard_map/ppermute | solution.py:335
  46.7 63.9 %collective-permute-start.4 = (bf16[256,1536]{1,0:T(8,128)(2,1)}, bf16[256,1536]{1,0:T(8,128)(2,1)S(1)}, u32[]{:S(2)}, u32[]{:S(2)}) collective-permute-start(bf16[256,1536]{1,0:T(8,128)(2,1)} %bitcast.32), channel_id=1, source_target_pairs={{1,2},{2,1},{3,4},{4,3},{5,6},{6,5},{7,8},{8,7},{9,10},{10,9},{11,... | collective-permute-start | bytes 2359304 | tf_op jit(solution)/shard_map/ppermute | solution.py:335
  54.1 56.5 %collective-permute-start.2 = (bf16[256,1536]{1,0:T(8,128)(2,1)}, bf16[256,1536]{1,0:T(8,128)(2,1)}, u32[]{:S(2)}, u32[]{:S(2)}) collective-permute-start(bf16[256,1536]{1,0:T(8,128)(2,1)} %bitcast.15), channel_id=1, source_target_pairs={{0,1},{1,0},{2,3},{3,2},{4,5},{5,4},{6,7},{7,6},{8,9},{9,8},{10,11... | collective-permute-start | bytes 2359304 | tf_op jit(solution)/shard_map/ppermute | solution.py:332
  54.2 0.9 copy-start.6
  55.1 66.5 %collective-permute-start.9 = (bf16[256,1536]{1,0:T(8,128)(2,1)}, bf16[256,1536]{1,0:T(8,128)(2,1)S(1)}, u32[]{:S(2)}, u32[]{:S(2)}) collective-permute-start(bf16[256,1536]{1,0:T(8,128)(2,1)} %bitcast.27), channel_id=1, source_target_pairs={{0,1},{1,0},{2,3},{3,2},{4,5},{5,4},{6,7},{7,6},{8,9},{9,8},{10,11... | collective-permute-start | bytes 2359304 | tf_op jit(solution)/shard_map/ppermute | solution.py:332
  63.2 58.3 %collective-permute-start.12 = (bf16[256,1536]{1,0:T(8,128)(2,1)}, bf16[256,1536]{1,0:T(8,128)(2,1)}, u32[]{:S(2)}, u32[]{:S(2)}) collective-permute-start(bf16[256,1536]{1,0:T(8,128)(2,1)} %bitcast.16), channel_id=1, source_target_pairs={{1,2},{2,1},{3,4},{4,3},{5,6},{6,5},{7,8},{8,7},{9,10},{10,9},{11,... | collective-permute-start | bytes 2359304 | tf_op jit(solution)/shard_map/ppermute | solution.py:335
  80.2 0.9 copy-start.8
  81.0 47.9 %collective-permute-start.13 = (bf16[256,1536]{1,0:T(8,128)(2,1)}, bf16[256,1536]{1,0:T(8,128)(2,1)}, u32[]{:S(2)}, u32[]{:S(2)}) collective-permute-start(bf16[256,1536]{1,0:T(8,128)(2,1)} %bitcast.28), channel_id=1, source_target_pairs={{1,2},{2,1},{3,4},{4,3},{5,6},{6,5},{7,8},{8,7},{9,10},{10,9},{11,... | collective-permute-start | bytes 2359304 | tf_op jit(solution)/shard_map/ppermute | solution.py:335
  110.6 1.1 copy-start.7
  111.8 1.1 copy-start.9
  112.9 25.6 %copy-start = (bf16[1,256,1536]{2,1,0:T(8,128)(2,1)S(1)}, bf16[1,256,1536]{2,1,0:T(8,128)(2,1)}, u32[]{:S(2)}) copy-start(bf16[1,256,1536]{2,1,0:T(8,128)(2,1)} %param.7) | copy-start | bytes 2359300
  112.9 25.6 %copy-start.1 = (bf16[1,256,1536]{2,1,0:T(8,128)(2,1)S(1)}, bf16[1,256,1536]{2,1,0:T(8,128)(2,1)}, u32[]{:S(2)}) copy-start(bf16[1,256,1536]{2,1,0:T(8,128)(2,1)} %param.8) | copy-start | bytes 2359300
  112.9 25.6 %copy-start.3 = (bf16[1,256,1536]{2,1,0:T(8,128)(2,1)S(1)}, bf16[1,256,1536]{2,1,0:T(8,128)(2,1)}, u32[]{:S(2)}) copy-start(bf16[1,256,1536]{2,1,0:T(8,128)(2,1)} %param.9) | copy-start | bytes 2359300
  112.9 25.7 %copy-start.5 = (bf16[256,1536]{1,0:T(8,128)(2,1)S(1)}, bf16[256,1536]{1,0:T(8,128)(2,1)}, u32[]{:S(2)}) copy-start(bf16[256,1536]{1,0:T(8,128)(2,1)} %copy-done.4) | copy-start | bytes 2359300
  121.4 28.6 %collective-permute-start.7 = (bf16[1536,256]{1,0:T(8,128)(2,1)S(1)}, bf16[1536,256]{1,0:T(8,128)(2,1)S(1)}, u32[]{:S(2)}, u32[]{:S(2)}) collective-permute-start(bf16[1536,256]{1,0:T(8,128)(2,1)S(1)} %get-tuple-element.39), channel_id=1, source_target_pairs={{0,1},{1,0},{2,3},{3,2},{4,5},{5,4},{6,7},{7,6},{8,9},{9,8},{10,11... | collective-permute-start | bytes 2359304 | tf_op jit(solution)/shard_map/ppermute | solution.py:332
  129.0 49.0 %collective-permute-start.15 = (bf16[256,1536]{1,0:T(8,128)(2,1)}, bf16[256,1536]{1,0:T(8,128)(2,1)S(1)}, u32[]{:S(2)}, u32[]{:S(2)}) collective-permute-start(bf16[256,1536]{1,0:T(8,128)(2,1)} %collective-permute-done.2.q), channel_id=1, source_target_pairs={{1,2},{2,1},{3,4},{4,3},{5,6},{6,5},{7,8},{8,7},{9,10},{10,9},{11,... | collective-permute-start | bytes 2359304 | tf_op jit(solution)/shard_map/ppermute | solution.py:335
  136.1 41.8 %collective-permute-start.16 = (bf16[256,1536]{1,0:T(8,128)(2,1)S(1)}, bf16[256,1536]{1,0:T(8,128)(2,1)S(1)}, u32[]{:S(2)}, u32[]{:S(2)}) collective-permute-start(bf16[256,1536]{1,0:T(8,128)(2,1)S(1)} %collective-permute-done.9.do.dop), channel_id=1, source_target_pairs={{1,2},{2,1},{3,4},{4,3},{5,6},{6,5},{7,8},{8,7},{9,10},{10,9},{11,... | collective-permute-start | bytes 2359304 | tf_op jit(solution)/shard_map/ppermute | solution.py:335
  138.4 11.6 %collective-permute-start.8 = (f32[24,256]{1,0:T(8,128)S(1)}, f32[24,256]{1,0:T(8,128)S(1)}, u32[]{:S(2)}, u32[]{:S(2)}) collective-permute-start(f32[24,256]{1,0:T(8,128)S(1)} %get-tuple-element.40), channel_id=1, source_target_pairs={{0,1},{1,0},{2,3},{3,2},{4,5},{5,4},{6,7},{7,6},{8,9},{9,8},{10,11... | collective-permute-start | bytes 73736 | tf_op jit(solution)/shard_map/ppermute | solution.py:332
  138.6 11.5 %copy-start.2 = (bf16[1,256,1536]{2,1,0:T(8,128)(2,1)S(1)}, bf16[1,256,1536]{2,1,0:T(8,128)(2,1)}, u32[]{:S(2)}) copy-start(bf16[1,256,1536]{2,1,0:T(8,128)(2,1)} %param.10) | copy-start | bytes 2359300
  152.7 15.4 %collective-permute-start.10 = (f32[24,256]{1,0:T(8,128)S(1)}, f32[24,256]{1,0:T(8,128)S(1)}, u32[]{:S(2)}, u32[]{:S(2)}) collective-permute-start(f32[24,256]{1,0:T(8,128)S(1)} %get-tuple-element.43.st), channel_id=1, source_target_pairs={{0,1},{1,0},{2,3},{3,2},{4,5},{5,4},{6,7},{7,6},{8,9},{9,8},{10,11... | collective-permute-start | bytes 73736 | tf_op jit(solution)/shard_map/ppermute | solution.py:332
  163.0 14.9 %collective-permute-start.14 = (f32[24,256]{1,0:T(8,128)S(1)}, f32[24,256]{1,0:T(8,128)S(1)}, u32[]{:S(2)}, u32[]{:S(2)}) collective-permute-start(f32[24,256]{1,0:T(8,128)S(1)} %get-tuple-element.43.st), channel_id=1, source_target_pairs={{1,2},{2,1},{3,4},{4,3},{5,6},{6,5},{7,8},{8,7},{9,10},{10,9},{11,... | collective-permute-start | bytes 73736 | tf_op jit(solution)/shard_map/ppermute | solution.py:335
  168.2 9.7 %collective-permute-start.17 = (f32[24,256]{1,0:T(8,128)S(1)}, f32[24,256]{1,0:T(8,128)S(1)}, u32[]{:S(2)}, u32[]{:S(2)}) collective-permute-start(f32[24,256]{1,0:T(8,128)S(1)} %collective-permute-done.10.st.stp), channel_id=1, source_target_pairs={{1,2},{2,1},{3,4},{4,3},{5,6},{6,5},{7,8},{8,7},{9,10},{10,9},{11,... | collective-permute-start | bytes 73736 | tf_op jit(solution)/shard_map/ppermute | solution.py:335
  177.8 34.0 %collective-permute-start.11 = (bf16[1536,256]{1,0:T(8,128)(2,1)S(1)}, bf16[1536,256]{1,0:T(8,128)(2,1)S(1)}, u32[]{:S(2)}, u32[]{:S(2)}) collective-permute-start(bf16[1536,256]{1,0:T(8,128)(2,1)S(1)} %partner_query_grads.1), channel_id=1, source_target_pairs={{0,1},{1,0},{2,3},{3,2},{4,5},{5,4},{6,7},{7,6},{8,9},{9,8},{10,11... | collective-permute-start | bytes 2359304 | tf_op jit(solution)/shard_map/ppermute | solution.py:332
  185.4 29.8 %collective-permute-start.18 = (bf16[256,1536]{1,0:T(8,128)(2,1)S(1)}, bf16[256,1536]{1,0:T(8,128)(2,1)S(1)}, u32[]{:S(2)}, u32[]{:S(2)}) collective-permute-start(bf16[256,1536]{1,0:T(8,128)(2,1)S(1)} %get-tuple-element.58), channel_id=1, source_target_pairs={{0,1},{1,0},{2,3},{3,2},{4,5},{5,4},{6,7},{7,6},{8,9},{9,8},{10,11... | collective-permute-start | bytes 2359304 | tf_op jit(solution)/shard_map/ppermute | solution.py:332
  185.7 41.8 %collective-permute-start.19 = (bf16[256,1536]{1,0:T(8,128)(2,1)S(1)}, bf16[256,1536]{1,0:T(8,128)(2,1)S(1)}, u32[]{:S(2)}, u32[]{:S(2)}) collective-permute-start(bf16[256,1536]{1,0:T(8,128)(2,1)S(1)} %get-tuple-element.60), channel_id=1, source_target_pairs={{0,1},{1,0},{2,3},{3,2},{4,5},{5,4},{6,7},{7,6},{8,9},{9,8},{10,11... | collective-permute-start | bytes 2359304 | tf_op jit(solution)/shard_map/ppermute | solution.py:332
where the time goes:
time: 233 us; the launch traced here: 232 us
  starting transfers between devices  75 us (32%)
  waiting for transfers between devices  64.9 us (28%)
  Pallas kernels  63.8 us (27%)
  blocking collectives  20.5 us (9%)
  local copies, waits for them, and re-layouts  5.85 us (3%)
    pallas_call x8, Pallas kernels, run(): pl.pallas_call(body, name=name, grid_spec=grid_spec, out_shape=shapes, co...  63.8 us
    ppermute x10, starting transfers between devices, beyond(): return lax.ppermute(value, 'ctx', outer)  57.9 us
    ppermute x10, waiting for transfers between devices, across(): return lax.ppermute(value, 'ctx', inner)  41.8 us
    ppermute x10, waiting for transfers between devices, beyond(): return lax.ppermute(value, 'ctx', outer)  23.2 us
    all_gather x1, blocking collectives, local(): g = lax.all_gather(gains, 'fsdp', axis=1, tiled=True)  20.5 us
    ppermute x10, starting transfers between devices, across(): return lax.ppermute(value, 'ctx', inner)  17.1 us
    unnamed x22, local copies, waits for them, and re-layouts  5.76 us
  transfers between devices with their start and end apart: 20, of which 7 were waited for; matrix products, arithmetic and copies ran while one was open for 1% of the time, Pallas kernels for 26%

commit v1 on v0

v1 whole, which is shorter than its diff:
```python
import math
from functools import partial

import jax
import jax.numpy as jnp
from jax import lax
from jax.experimental import pallas as pl
from jax.experimental.pallas import tpu as pltpu
from jax.sharding import PartitionSpec as P

EPSILON = 1e-06
ROWS = 256
HD = 128
HB = 4
DEPTH = 1
LOW = -1e30
COST = 20_000_000_000
SCALE = math.log2(math.e) / math.sqrt(128)
BF = jnp.bfloat16
F32 = jnp.float32

NT = (((1,), (1,)), ((), ()))
TN = (((0,), (0,)), ((), ()))
NN = (((1,), (0,)), ((), ()))


def dot(a, b, dims):
    return lax.dot_general(a, b, dims, preferred_element_type=F32)


def allowed(sc, query_dev, key_dev):
    count = sc[1]
    inside = jnp.logical_and(
        jnp.logical_and(query_dev >= 0, query_dev < count),
        jnp.logical_and(key_dev >= 0, key_dev < count),
    )

    def tile_at(dev):
        first = 2 * (jnp.clip(dev, 0, count - 1) // 2)
        return jnp.where(sc[2 + first] == dev, first, first + 1)

    query_tile, key_tile = tile_at(query_dev), tile_at(key_dev)
    base = 2 + count + query_tile * 6
    hit = sc[base] == key_tile
    for slot in range(1, 6):
        hit = jnp.logical_or(hit, sc[base + slot] == key_tile)
    return jnp.logical_and(inside, hit)


def around(sc):
    me = sc[0]
    odd = me % 2 == 1
    partner = jnp.where(odd, me - 1, me + 1)
    near = jnp.where(odd, me + 1, me - 1)
    far = jnp.where(odd, me + 2, me - 2)
    return me, partner, near, far


def normed(raw, gain_row):
    floats = raw.astype(F32)
    inverse = lax.rsqrt(jnp.mean(floats * floats, axis=1, keepdims=True) + EPSILON)
    return (floats * inverse * gain_row).astype(BF)


def denormed(raw, gain_row, upstream):
    floats = raw.astype(F32)
    inverse = lax.rsqrt(jnp.mean(floats * floats, axis=1, keepdims=True) + EPSILON)
    scaled = upstream * gain_row
    inner = jnp.mean(floats * scaled, axis=1, keepdims=True)
    return (inverse * scaled - floats * (inverse * inverse * inverse * inner)).astype(BF)


def cols(j):
    return slice(j * HD, (j + 1) * HD)


def emit(units):
    first, second = {}, {}
    for t in range(len(units) + DEPTH + 1):
        if t < len(units):
            first[t] = units[t][0]()
        u = t - DEPTH - 1
        if u >= 0:
            units[u][2](second.pop(u))
        u = t - DEPTH
        if 0 <= u < len(units):
            second[u] = units[u][1](first.pop(u))


def forward_units(permit, kn, v, qn, m_ref, l_ref, acc_ref):
    units = []
    for j in range(HB):
        def scores(c=cols(j)):
            return dot(kn[:, c], qn[:, c], NT)

        def weights(s, j=j):
            top = jnp.max(s, axis=0, keepdims=True) * SCALE
            if permit is not None:
                top = jnp.where(permit, top, LOW)
            new = jnp.maximum(m_ref[j], top)
            shrink = jnp.exp2(m_ref[j] - new)
            m_ref[j] = new
            if permit is not None:
                new = jnp.where(permit, new, -LOW)
            return shrink, jnp.exp2(s * SCALE - new).astype(BF)

        def mix(found, j=j, c=cols(j)):
            shrink, p = found
            both = jnp.concatenate([v[:, c], jnp.ones((ROWS, HD), BF)], axis=1)
            out = dot(both, p, TN)
            l_ref[j] = l_ref[j] * shrink + out[HD : HD + 1]
            acc_ref[c, :] = acc_ref[c, :] * shrink + out[:HD]

        units.append((scores, weights, mix))
    return units


def backward_units(permit, kn, v, qn, do, st, use, first=None, heads=None, base=0):
    if heads is None:
        heads = pl.num_programs(0) * HB
    if first is None:
        first = pl.program_id(0) * HB
    units = []
    for j in range(HB):
        def scores(c=cols(j)):
            return dot(kn[:, c], qn[:, c], NT), dot(v[:, c], do[:, c], NT)

        def weights(found, h=base + first + j):
            s, dp = found
            lse = st[pl.ds(h, 1), :]
            if permit is not None:
                lse = jnp.where(permit, lse, -LOW)
            p = jnp.exp2(s * SCALE - lse)
            return p.astype(BF), (p * (dp - st[pl.ds(heads + h, 1), :])).astype(BF)

        units.append((scores, weights, partial(use, cols(j))))
    return units


def query_use(kn, dq_ref, c, found):
    dq_ref[c, :] += dot(kn[:, c], found[1], TN)


def key_use(qn, do, dk_ref, dv_ref, c, found):
    dk_ref[:, c] += dot(found[1], qn[:, c], NN)
    dv_ref[:, c] += dot(found[0], do[:, c], NN)


def clear(*refs):
    for ref in refs:
        ref[...] = jnp.zeros_like(ref)


def put_rows(ref, half, rows_ref):
    step = pl.program_id(0)
    heads = pl.num_programs(0) * HB
    for j in range(HB):
        ref[pl.ds(half * heads + step * HB + j, 1), :] = rows_ref[j]


def get_rows(ref, half, rows_ref):
    step = pl.program_id(0)
    heads = pl.num_programs(0) * HB
    for j in range(HB):
        rows_ref[j] = ref[pl.ds(half * heads + step * HB + j, 1), :]


def prepare(g, q, k, do, qn, kn, do_out):
    for j in range(HB):
        c = cols(j)
        qn[:, c] = normed(q[:, c], g[0:1, :])
        kn[:, c] = normed(k[:, c], g[1:2, :])
    do_out[...] = do[...]


def own_forward(
    sc, g, qn, knx, v, kp, vp, ke, ve, do, acc_ref, ml_ref, knp, kne, qn_out, do_out,
    m_ref, l_ref,
):
    me, partner, near, far = around(sc)
    qn_out[...] = qn[...]
    do_out[...] = do[...]
    for j in range(HB):
        c = cols(j)
        knp[:, c] = normed(kp[:, c], g[1:2, :])
        kne[:, c] = normed(ke[:, c], g[1:2, :])
    m_ref[...] = jnp.full_like(m_ref, LOW)
    clear(l_ref, acc_ref)
    emit(
        forward_units(None, knx, v, qn, m_ref, l_ref, acc_ref)
        + forward_units(allowed(sc, me, partner), knp, vp, qn, m_ref, l_ref, acc_ref)
        + forward_units(allowed(sc, me, near), kne, ve, qn, m_ref, l_ref, acc_ref)
    )
    put_rows(ml_ref, 0, m_ref)
    put_rows(ml_ref, 1, l_ref)


def partner_forward(sc, g, qn, kne, ve, kf, vf, o_ref, ml_ref, knf, m_ref, l_ref, acc_ref):
    me, partner, near, far = around(sc)
    for j in range(HB):
        knf[:, cols(j)] = normed(kf[:, cols(j)], g[1:2, :])
    m_ref[...] = jnp.full_like(m_ref, LOW)
    clear(l_ref, acc_ref)
    emit(
        forward_units(allowed(sc, partner, near), kne, ve, qn, m_ref, l_ref, acc_ref)
        + forward_units(allowed(sc, partner, far), knf, vf, qn, m_ref, l_ref, acc_ref)
    )
    put_rows(ml_ref, 0, m_ref)
    put_rows(ml_ref, 1, l_ref)
    for j in range(HB):
        total = l_ref[j]
        share = jnp.where(total > 0.0, 1.0 / jnp.where(total > 0.0, total, 1.0), 0.0)
        o_ref[cols(j), :] = (acc_ref[cols(j), :] * share).astype(BF)


def own_forward_far(sc, qn, knf, vf, acc0, ml0, acc_ref, ml_ref, m_ref, l_ref):
    me, partner, near, far = around(sc)
    get_rows(ml0, 0, m_ref)
    get_rows(ml0, 1, l_ref)
    acc_ref[...] = acc0[...]
    emit(forward_units(allowed(sc, me, far), knf, vf, qn, m_ref, l_ref, acc_ref))
    put_rows(ml_ref, 0, m_ref)
    put_rows(ml_ref, 1, l_ref)


def merge(acc_ref, ml_ref, o_ret, ml_ret, d_out, att_ref, st_ref):
    step = pl.program_id(0)
    heads = pl.num_programs(0) * HB
    for j in range(HB):
        h = step * HB + j
        m1, l1 = ml_ref[pl.ds(h, 1), :], ml_ref[pl.ds(heads + h, 1), :]
        m2, l2 = ml_ret[pl.ds(h, 1), :], ml_ret[pl.ds(heads + h, 1), :]
        m = jnp.maximum(m1, m2)
        a1 = jnp.exp2(m1 - m)
        a2 = jnp.exp2(m2 - m) * l2
        total = l1 * a1 + a2
        inv = 1.0 / total
        out = acc_ref[cols(j), :] * (a1 * inv) + o_ret[cols(j), :].astype(F32) * (a2 * inv)
        low = out.astype(BF)
        att_ref[:, cols(j)] = jnp.transpose(low)
        grads = jnp.transpose(d_out[:, cols(j)]).astype(F32)
        st_ref[pl.ds(h, 1), :] = m + jnp.log2(total)
        st_ref[pl.ds(heads + h, 1), :] = jnp.sum(low.astype(F32) * grads, axis=0, keepdims=True)


def own_query_grads(
    sc, qn, do, st, knx, v, knp, vp, kne, ve, knf, vf, dq_ref, dk_ref, dv_ref
):
    me, partner, near, far = around(sc)
    clear(dq_ref, dk_ref, dv_ref)

    def both(c, found):
        query_use(knx, dq_ref, c, found)
        key_use(qn, do, dk_ref, dv_ref, c, found)

    units = backward_units(None, knx, v, qn, do, st, both)
    for dev, kn, val in ((partner, knp, vp), (near, kne, ve), (far, knf, vf)):
        use = partial(query_use, kn, dq_ref)
        units += backward_units(allowed(sc, me, dev), kn, val, qn, do, st, use)
    emit(units)


def partner_query_grads(sc, qn, do, st, kne, ve, knf, vf, _, dq_ref, *rest):
    acc_ref = rest[-1]
    me, partner, near, far = around(sc)
    for chunk, both in enumerate(rest[:-1]):
        @pl.when(pl.program_id(0) == chunk)
        def _(both=both):
            both[:ROWS] = qn[...]
            both[ROWS:] = do[...]

    clear(acc_ref)
    units = []
    for dev, kn, val in ((near, kne, ve), (far, knf, vf)):
        use = partial(query_use, kn, acc_ref)
        units += backward_units(allowed(sc, partner, dev), kn, val, qn, do, st, use)
    emit(units)
    dq_ref[...] = acc_ref[...].astype(BF)


def near_key_grads(
    sc, knx, v, qnp, dop, stp, knp, vp, qne, doe, ste, dk0, dv0, _,
    dkx, dvx, dkp, dvp,
):
    me, partner, near, far = around(sc)
    dkx[...] = dk0[...]
    dvx[...] = dv0[...]
    clear(dkp, dvp)
    emit(
        backward_units(
            allowed(sc, partner, me), knx, v, qnp, dop, stp, partial(key_use, qnp, dop, dkx, dvx)
        )
        + backward_units(
            allowed(sc, near, me), knx, v, qne, doe, ste, partial(key_use, qne, doe, dkx, dvx)
        )
        + backward_units(
            allowed(sc, near, partner), knp, vp, qne, doe, ste,
            partial(key_use, qne, doe, dkp, dvp),
        )
    )


def partner_far_grads(chunk, heads, sc, knp, vp, both, st, dk0, dv0, _, out, dk, dv):
    me, partner, near, far = around(sc)
    dk[...] = dk0[...]
    dv[...] = dv0[...]
    qn, do = both.at[pl.ds(0, ROWS)], both.at[pl.ds(ROWS, ROWS)]
    emit(
        backward_units(
            allowed(sc, far, partner), knp, vp, qn, do, st, partial(key_use, qn, do, dk, dv),
            chunk * HB, heads, 2 * heads,
        )
    )
    out[:ROWS] = dk[...].astype(BF)
    out[ROWS:] = dv[...].astype(BF)


def own_far_grads(chunk, heads, sc, knx, v, both, st, dk0, dv0, _, dk, dv):
    me, partner, near, far = around(sc)
    dk[...] = dk0[...]
    dv[...] = dv0[...]
    qn, do = both.at[pl.ds(0, ROWS)], both.at[pl.ds(ROWS, ROWS)]
    emit(
        backward_units(
            allowed(sc, far, me), knx, v, qn, do, st, partial(key_use, qn, do, dk, dv),
            chunk * HB, heads, 2 * heads,
        )
    )


def finish_queries(g, dqt, dqr, q, _, dq_out):
    scale = 1.0 / math.sqrt(HD)
    for j in range(HB):
        c = cols(j)
        dq = jnp.transpose(dqt[c, :] + dqr[c, :].astype(F32)) * scale
        dq_out[:, c] = denormed(q[:, c], g[0:1, :], dq)


def finish_keys(g, k, *refs):
    dk_out, dv_out = refs[-2:]
    scale = 1.0 / math.sqrt(HD)
    for chunk in range((len(refs) - 2) // 3):
        dk, dv, back = refs[3 * chunk : 3 * chunk + 3]

        @pl.when(pl.program_id(0) == chunk)
        def _(dk=dk, dv=dv, back=back):
            for j in range(HB):
                c = cols(j)
                total = (dk[:, c] + back[:ROWS, c].astype(F32)) * scale
                dk_out[:, c] = denormed(k[:, c], g[1:2, :], total)
            dv_out[...] = (dv[...] + back[ROWS:].astype(F32)).astype(BF)


WIDE = "wide"
TALL = "tall"
FULL = "full"
ORDER = "order"


def spec(kind, arr):
    if kind == WIDE:
        return pl.BlockSpec((ROWS, HB * HD), lambda i, *_: (0, i))
    if kind == TALL:
        return pl.BlockSpec((HB * HD, ROWS), lambda i, *_: (i, 0))
    if isinstance(kind, int):
        return pl.BlockSpec((ROWS, HB * HD), lambda i, *_: (0, kind))
    if kind == ORDER:
        return pl.BlockSpec(memory_space=pl.ANY)
    return pl.BlockSpec(arr.shape, lambda i, *_: (0,) * len(arr.shape))


def run(body, scalars, ins, outs, scratch=(), steps=None, name=None):
    if steps is None:
        steps = next(a.shape[1] for kind, a in ins if kind == WIDE) // (HB * HD)
    shapes = [jax.ShapeDtypeStruct(s, d) for _, s, d in outs]
    grid_spec = pltpu.PrefetchScalarGridSpec(
        num_scalar_prefetch=len(scalars),
        grid=(steps,),
        in_specs=[spec(kind, a) for kind, a in ins],
        out_specs=[spec(o[0], s) for o, s in zip(outs, shapes)],
        scratch_shapes=list(scratch),
    )
    return pl.pallas_call(
        body,
        name=name or body.__name__,
        grid_spec=grid_spec,
        out_shape=shapes,
        cost_estimate=pl.CostEstimate(flops=COST, transcendentals=0, bytes_accessed=COST),
        compiler_params=pltpu.CompilerParams(
            dimension_semantics=("arbitrary",), vmem_limit_bytes=32 << 20
        ),
    )(*scalars, *[a for _, a in ins])


def local(q_raw, k_raw, values_in, d_out, gains, tile_device, neighbours):
    count = lax.axis_size("ctx")
    inner = [(d, d ^ 1) for d in range(count)]
    outer = []
    for d in range(1, count - 1, 2):
        outer += [(d, d + 1), (d + 1, d)]
    q, k, v, do = q_raw[0], k_raw[0], values_in[0], d_out[0]
    features = q.shape[1]
    heads = features // HD

    def across(*values):
        return [lax.ppermute(value, "ctx", inner) for value in values]

    def beyond(*values):
        return [lax.ppermute(value, "ctx", outer) for value in values]

    wide_bf = (WIDE, (ROWS, features), BF)
    wide_f = (WIDE, (ROWS, features), F32)
    tall_bf = (TALL, (features, ROWS), BF)
    tall_f = (TALL, (features, ROWS), F32)
    stats = (FULL, (2 * heads, ROWS), F32)
    row_s = pltpu.VMEM((HB, 1, ROWS), F32)
    acc_t = pltpu.VMEM((HB * HD, ROWS), F32)
    acc_w = pltpu.VMEM((ROWS, HB * HD), F32)

    def wide(*arrays):
        return [(WIDE, a) for a in arrays]

    kp, vp = across(k, v)
    ke, ve = beyond(k, v)
    g = lax.all_gather(gains, "fsdp", axis=1, tiled=True)
    place = jnp.stack([lax.axis_index("ctx"), jnp.int32(count)]).astype(jnp.int32)
    scalars = (jnp.concatenate([place, tile_device, neighbours.reshape(-1)]),)
    gain = [(FULL, g)]
    chunks = features // (HB * HD)
    pair = (FULL, (2 * ROWS, HB * HD), BF)
    part_f = (FULL, (ROWS, HB * HD), F32)

    qn, knx, do2 = run(prepare, (), gain + wide(q, k, do), [wide_bf] * 3)
    kf, vf = beyond(kp, vp)
    qnp, dop = across(qn, do2)

    acc, ml, knp, kne, qn3, do3 = run(
        own_forward, scalars, gain + wide(qn, knx, v, kp, vp, ke, ve, do),
        [tall_f, stats] + [wide_bf] * 4, (row_s, row_s),
    )
    qne, doe = beyond(qn3, do3)
    op, mlp, knf = run(
        partner_forward, scalars, gain + wide(qnp, kne, ve, kf, vf),
        [tall_bf, stats, wide_bf], (row_s, row_s, acc_t),
    )
    o_ret, ml_ret = across(op, mlp)
    acc, ml = run(
        own_forward_far, scalars,
        wide(qn, knf, vf) + [(TALL, acc), (FULL, ml)], [tall_f, stats], (row_s, row_s),
    )
    att, st = run(
        merge, (), [(TALL, acc), (FULL, ml), (TALL, o_ret), (FULL, ml_ret)] + wide(do),
        [wide_bf, stats],
    )
    (stp,) = across(st)
    (st2,) = beyond(jnp.concatenate([st, stp], axis=0))
    dqt, dk, dv = run(
        own_query_grads, scalars,
        wide(qn, do) + [(FULL, st)] + wide(knx, v, knp, vp, kne, ve, knf, vf),
        [tall_f, wide_f, wide_f],
    )
    dqp, *sent = run(
        partner_query_grads, scalars,
        wide(qnp, dop) + [(FULL, stp)] + wide(kne, ve, knf, vf) + [(ORDER, dqt)],
        [tall_bf] + [pair] * chunks, (acc_t,),
    )
    (dqr,) = across(dqp)
    far = beyond(*sent)
    dk, dv, dkp, dvp = run(
        near_key_grads, scalars,
        wide(knx, v, qnp, dop) + [(FULL, stp)] + wide(knp, vp, qne, doe) + [(FULL, st2)]
        + wide(dk, dv) + [(ORDER, dqp)],
        [wide_f] * 4,
    )
    last, back, own = dkp, [], []
    for i in range(chunks):
        out, _, _ = run(
            partial(partner_far_grads, i, heads), scalars,
            [(i, knp), (i, vp), (FULL, far[i]), (FULL, st2), (i, dkp), (i, dvp), (ORDER, last)],
            [pair, part_f, part_f], (), 1, "partner_far_grads",
        )
        back += across(out)
        dki, dvi = run(
            partial(own_far_grads, i, heads), scalars,
            [(i, knx), (i, v), (FULL, far[i]), (FULL, st2), (i, dk), (i, dv), (ORDER, out)],
            [part_f, part_f], (), 1, "own_far_grads",
        )
        own.append((dki, dvi))
        last = dki
    (dq_out,) = run(
        finish_queries, (), gain + [(TALL, dqt), (TALL, dqr)] + wide(q) + [(ORDER, last)],
        [wide_bf],
    )
    pieces = []
    for i in range(chunks):
        pieces += [(FULL, own[i][0]), (FULL, own[i][1]), (FULL, back[i])]
    dk_out, dv_out = run(finish_keys, (), gain + wide(k) + pieces, [wide_bf] * 2)
    return att[None], dq_out[None], dk_out[None], dv_out[None]


def solution(mesh):
    tokens = P("fsdp", "ctx", None)
    return jax.shard_map(
        local,
        mesh=mesh,
        in_specs=(tokens, tokens, tokens, tokens, P(None, "fsdp"), P(), P()),
        out_specs=(tokens, tokens, tokens, tokens),
        check_vma=False,
    )
```

time: 233 us -> 207 us (0.89)
  starting transfers between devices: 75 us -> 58.2 us
  Pallas kernels: 63.8 us -> 54.6 us
    ppermute x20 -> x21, starting transfers between devices: 75 us -> 58.2 us  [the longest x10 49 us: beyond(): return [lax.ppermute(value, 'ctx', outer) for value in values]]
    pallas_call x8 -> x16, Pallas kernels: 63.8 us -> 54.6 us  [run(): pl.pallas_call(body, name=name or body.__name__, grid_spec=grid_spec, out...]
    unnamed x22 -> x32, local copies, waits for them, and re-layouts: 5.76 us -> 7.62 us
    ppermute x20 -> x21, waiting for transfers between devices: 64.9 us -> 64.7 us  [the longest x11 43.7 us: across(): return [lax.ppermute(value, 'ctx', inner) for value in values]]
  transfers between devices with their start and end apart: 20 -> 21, of which waited for: 7 -> 6; matrix products, arithmetic and copies ran while one was open for 1% -> 0% of each run, Pallas kernels for 26% -> 25%
where the time goes in v1:
time: 207 us; the launch traced here: 206 us
  waiting for transfers between devices  64.7 us (31%)
  starting transfers between devices  58.2 us (28%)
  Pallas kernels  54.6 us (26%)
  blocking collectives  19.6 us (9%)
  local copies, waits for them, and re-layouts  7.71 us (4%)
    pallas_call x16, Pallas kernels, run(): pl.pallas_call(body, name=name or body.__name__, grid_spec=grid_spec, out...  54.6 us
    ppermute x10, starting transfers between devices, beyond(): return [lax.ppermute(value, 'ctx', outer) for value in values]  49 us
    ppermute x11, waiting for transfers between devices, across(): return [lax.ppermute(value, 'ctx', inner) for value in values]  43.7 us
    ppermute x10, waiting for transfers between devices, beyond(): return [lax.ppermute(value, 'ctx', outer) for value in values]  21.1 us
    all_gather x1, blocking collectives, local(): g = lax.all_gather(gains, 'fsdp', axis=1, tiled=True)  19.6 us
    ppermute x11, starting transfers between devices, across(): return [lax.ppermute(value, 'ctx', inner) for value in values]  9.19 us
    unnamed x32, local copies, waits for them, and re-layouts  7.62 us
  transfers between devices with their start and end apart: 21, of which 6 were waited for; matrix products, arithmetic and copies ran while one was open for 0% of the time, Pallas kernels for 25%

profile of v1, /device:TPU:16, one launch (start us, length us, event | category | flops | bytes accessed | tf_op | source)
XLA Modules:
  0.0 206.0 jit_solution(9138227113694592625)
XLA Ops:
  0.6 7.5 %collective-permute-start.3 = (bf16[256,1536]{1,0:T(8,128)(2,1)}, bf16[256,1536]{1,0:T(8,128)(2,1)}, u32[]{:S(2)}, u32[]{:S(2)}) collective-permute-start(bf16[256,1536]{1,0:T(8,128)(2,1)} %bitcast.34), channel_id=1, source_target_pairs={{1,2},{2,1},{3,4},{4,3},{5,6},{6,5},{7,8},{8,7},{9,10},{10,9},{11,... | collective-permute-start | bytes 2359304 | tf_op jit(solution)/shard_map/ppermute | solution.py:409
  8.3 3.9 %collective-permute-start.4 = (bf16[256,1536]{1,0:T(8,128)(2,1)}, bf16[256,1536]{1,0:T(8,128)(2,1)}, u32[]{:S(2)}, u32[]{:S(2)}) collective-permute-start(bf16[256,1536]{1,0:T(8,128)(2,1)} %bitcast.24), channel_id=1, source_target_pairs={{1,2},{2,1},{3,4},{4,3},{5,6},{6,5},{7,8},{8,7},{9,10},{10,9},{11,... | collective-permute-start | bytes 2359304 | tf_op jit(solution)/shard_map/ppermute | solution.py:409
  13.5 19.6 %all-gather = f32[16,8,2]{1,2,0:T(2,128)S(1)} all-gather(f32[1,8,2]{1,2,0:T(2,128)} %bitcast.38), channel_id=1, replica_groups=mesh['fsdp'=16,'ctx'=16] {'fsdp'}, dimensions={0}, use_global_device_ids=true | all-gather | bytes 1088 | tf_op jit(solution)/shard_map/all_gather | solution.py:425
  36.6 2.3 %prepare.1 = (bf16[256,1536]{1,0:T(8,128)(2,1)S(1)}, bf16[256,1536]{1,0:T(8,128)(2,1)S(1)}, bf16[256,1536]{1,0:T(8,128)(2,1)}) custom-call(f32[2,128]{1,0:T(2,128)S(1)} %bitcast.15, bf16[256,1536]{1,0:T(8,128)(2,1)S(1)} %bitcast.32, bf16[256,1536]{1,0:T(8,128)(2,1)S(1)} %bitcast.36, bf16[256,1536]{1,0:T(8,128)(2,1)S(1)} %bitcast.20), custom_call_target="tpu_custom_call" | custom-call | flops 20000000000 | bytes 20000000000 | tf_op jit(solution)/shard_map/prepare/pallas_call | solution.py:383
  43.1 4.6 %collective-permute-start.5 = (bf16[256,1536]{1,0:T(8,128)(2,1)}, bf16[256,1536]{1,0:T(8,128)(2,1)S(1)}, u32[]{:S(2)}, u32[]{:S(2)}) collective-permute-start(bf16[256,1536]{1,0:T(8,128)(2,1)} %collective-permute-done.1.kp), channel_id=1, source_target_pairs={{1,2},{2,1},{3,4},{4,3},{5,6},{6,5},{7,8},{8,7},{9,10},{10,9},{11,... | collective-permute-start | bytes 2359304 | tf_op jit(solution)/shard_map/ppermute | solution.py:409
  47.7 4.8 %collective-permute-start.6 = (bf16[256,1536]{1,0:T(8,128)(2,1)S(1)}, bf16[256,1536]{1,0:T(8,128)(2,1)S(1)}, u32[]{:S(2)}, u32[]{:S(2)}) collective-permute-start(bf16[256,1536]{1,0:T(8,128)(2,1)S(1)} %collective-permute-done.2.vp), channel_id=1, source_target_pairs={{1,2},{2,1},{3,4},{4,3},{5,6},{6,5},{7,8},{8,7},{9,10},{10,9},{11,... | collective-permute-start | bytes 2359304 | tf_op jit(solution)/shard_map/ppermute | solution.py:409
  54.8 6.9 %own_forward.1 = (f32[1536,256]{1,0:T(8,128)S(1)}, f32[24,256]{1,0:T(8,128)S(1)}, bf16[256,1536]{1,0:T(8,128)(2,1)S(1)}, bf16[256,1536]{1,0:T(8,128)(2,1)S(1)}, ...) custom-call(s32[114]{0:T(128)S(1)} %pad_add_fusion.sc, f32[2,128]{1,0:T(2,128)S(1)} %bitcast.16, ...), custom_call_target="tpu_custom_call" | custom-call | flops 20000000000 | bytes 20000000000 | tf_op jit(solution)/shard_map/own_forward/pallas_call | solution.py:383
  61.8 4.7 %collective-permute-start.14 = (bf16[256,1536]{1,0:T(8,128)(2,1)S(1)}, bf16[256,1536]{1,0:T(8,128)(2,1)S(1)}, u32[]{:S(2)}, u32[]{:S(2)}) collective-permute-start(bf16[256,1536]{1,0:T(8,128)(2,1)S(1)} %get-tuple-element.59), channel_id=1, source_target_pairs={{1,2},{2,1},{3,4},{4,3},{5,6},{6,5},{7,8},{8,7},{9,10},{10,9},{11,... | collective-permute-start | bytes 2359304 | tf_op jit(solution)/shard_map/ppermute | solution.py:409
  66.4 11.6 %collective-permute-done.qn.qnp = bf16[256,1536]{1,0:T(8,128)(2,1)S(1)} collective-permute-done((bf16[256,1536]{1,0:T(8,128)(2,1)}, bf16[256,1536]{1,0:T(8,128)(2,1)S(1)}, u32[]{:S(2)}, u32[]{:S(2)}) %collective-permute-start) | collective-permute-done | bytes 786464 | tf_op jit(solution)/shard_map/ppermute | solution.py:406
  78.0 4.4 %collective-permute-start.15 = (bf16[256,1536]{1,0:T(8,128)(2,1)S(1)}, bf16[256,1536]{1,0:T(8,128)(2,1)S(1)}, u32[]{:S(2)}, u32[]{:S(2)}) collective-permute-start(bf16[256,1536]{1,0:T(8,128)(2,1)S(1)} %get-tuple-element.60), channel_id=1, source_target_pairs={{1,2},{2,1},{3,4},{4,3},{5,6},{6,5},{7,8},{8,7},{9,10},{10,9},{11,... | collective-permute-start | bytes 2359304 | tf_op jit(solution)/shard_map/ppermute | solution.py:409
  82.5 3.6 %collective-permute-done.6.vf = bf16[256,1536]{1,0:T(8,128)(2,1)S(1)} collective-permute-done((bf16[256,1536]{1,0:T(8,128)(2,1)S(1)}, bf16[256,1536]{1,0:T(8,128)(2,1)S(1)}, u32[]{:S(2)}, u32[]{:S(2)}) %collective-permute-start.6) | collective-permute-done | bytes 786464 | tf_op jit(solution)/shard_map/ppermute | solution.py:409
  86.1 5.2 %partner_forward.1 = (bf16[1536,256]{1,0:T(8,128)(2,1)S(1)}, f32[24,256]{1,0:T(8,128)S(1)}, bf16[256,1536]{1,0:T(8,128)(2,1)S(1)}) custom-call(s32[114]{0:T(128)S(1)} %pad_add_fusion.sc, f32[2,128]{1,0:T(2,128)S(1)} %bitcast.17, bf16[256,1536]{1,0:T(8,128)(2,1)S(1)} %collective-permute-done.qn.qnp, bf16[256,1536]{1,0:T(8,128)(2,1)S(1)} %get-tuple-element.44.kne, ...), custom_call_target="tpu_custom_call" | custom-call | flops 20000000000 | bytes 20000000000 | tf_op jit(solution)/shard_map/partner_forward/pallas_call | solution.py:383
  91.4 2.0 collective-permute-start.7
  93.4 2.8 %own_forward_far.1 = (f32[1536,256]{1,0:T(8,128)S(1)}, f32[24,256]{1,0:T(8,128)S(1)}) custom-call(s32[114]{0:T(128)S(1)} %pad_add_fusion.sc, bf16[256,1536]{1,0:T(8,128)(2,1)S(1)} %copy-done.8, bf16[256,1536]{1,0:T(8,128)(2,1)S(1)} %get-tuple-element.45.knf, bf16[256,1536]{1,0:T(8,128)(2,1)S(1)} %collective-permute-done.6.vf, ...), custom_call_target="tpu_custom_call" | custom-call | flops 20000000000 | bytes 20000000000 | tf_op jit(solution)/shard_map/own_forward_far/pallas_call | solution.py:383
  96.2 12.8 %collective-permute-done.7.o_ret = bf16[1536,256]{1,0:T(8,128)(2,1)S(1)} collective-permute-done((bf16[1536,256]{1,0:T(8,128)(2,1)S(1)}, bf16[1536,256]{1,0:T(8,128)(2,1)S(1)}, u32[]{:S(2)}, u32[]{:S(2)}) %collective-permute-start.7) | collective-permute-done | bytes 786464 | tf_op jit(solution)/shard_map/ppermute | solution.py:406
  109.0 1.9 merge.1
  112.4 7.8 %own_query_grads.1 = (f32[1536,256]{1,0:T(8,128)S(1)}, f32[256,1536]{1,0:T(8,128)S(1)}, f32[256,1536]{1,0:T(8,128)S(1)}) custom-call(s32[114]{0:T(128)S(1)} %pad_add_fusion.sc, bf16[256,1536]{1,0:T(8,128)(2,1)S(1)} %copy-done.9, bf16[256,1536]{1,0:T(8,128)(2,1)S(1)} %bitcast.23, f32[24,256]{1,0:T(8,128)S(1)} %get-tuple-element.53.st, ...), custom_call_target="tpu_custom_call" | custom-call | flops 20000000000 | bytes 20000000000 | tf_op jit(solution)/shard_map/own_query_grads/pallas_call | solution.py:383
  120.3 5.4 %collective-permute-start.13 = (f32[48,256]{1,0:T(8,128)S(1)}, f32[48,256]{1,0:T(8,128)S(1)}, u32[]{:S(2)}, u32[]{:S(2)}) collective-permute-start(f32[48,256]{1,0:T(8,128)S(1)} %pad_maximum_fusion), channel_id=1, source_target_pairs={{1,2},{2,1},{3,4},{4,3},{5,6},{6,5},{7,8},{8,7},{9,10},{10,9},{11,... | collective-permute-start | bytes 147464 | tf_op jit(solution)/shard_map/ppermute | solution.py:409
  125.7 4.8 %partner_query_grads.1 = (bf16[1536,256]{1,0:T(8,128)(2,1)S(1)}, bf16[512,512]{1,0:T(8,128)(2,1)S(1)}, bf16[512,512]{1,0:T(8,128)(2,1)S(1)}, bf16[512,512]{1,0:T(8,128)(2,1)S(1)}) custom-call(s32[114]{0:T(128)S(1)} %pad_add_fusion.sc, bf16[256,1536]{1,0:T(8,128)(2,1)S(1)} %collective-permute-done.qn.qnp, ...), custom_call_target="tpu_custom_call" | custom-call | flops 20000000000 | bytes 20000000000 | tf_op jit(solution)/shard_map/partner_query_grads/pallas_call | solution.py:383
  130.5 4.2 %collective-permute-start.12 = (bf16[512,512]{1,0:T(8,128)(2,1)S(1)}, bf16[512,512]{1,0:T(8,128)(2,1)S(1)}, u32[]{:S(2)}, u32[]{:S(2)}) collective-permute-start(bf16[512,512]{1,0:T(8,128)(2,1)S(1)} %get-tuple-element.58), channel_id=1, source_target_pairs={{1,2},{2,1},{3,4},{4,3},{5,6},{6,5},{7,8},{8,7},{9,10},{10,9},{11,... | collective-permute-start | bytes 1572872 | tf_op jit(solution)/shard_map/ppermute | solution.py:409
  134.7 5.2 %collective-permute-start.16 = (bf16[512,512]{1,0:T(8,128)(2,1)S(1)}, bf16[512,512]{1,0:T(8,128)(2,1)S(1)}, u32[]{:S(2)}, u32[]{:S(2)}) collective-permute-start(bf16[512,512]{1,0:T(8,128)(2,1)S(1)} %get-tuple-element.67), channel_id=1, source_target_pairs={{1,2},{2,1},{3,4},{4,3},{5,6},{6,5},{7,8},{8,7},{9,10},{10,9},{11,... | collective-permute-start | bytes 1572872 | tf_op jit(solution)/shard_map/ppermute | solution.py:409
  140.0 4.2 %collective-permute-start.17 = (bf16[512,512]{1,0:T(8,128)(2,1)S(1)}, bf16[512,512]{1,0:T(8,128)(2,1)S(1)}, u32[]{:S(2)}, u32[]{:S(2)}) collective-permute-start(bf16[512,512]{1,0:T(8,128)(2,1)S(1)} %get-tuple-element.68), channel_id=1, source_target_pairs={{1,2},{2,1},{3,4},{4,3},{5,6},{6,5},{7,8},{8,7},{9,10},{10,9},{11,... | collective-permute-start | bytes 1572872 | tf_op jit(solution)/shard_map/ppermute | solution.py:409
  144.3 7.3 %near_key_grads.1 = (f32[256,1536]{1,0:T(8,128)S(1)}, f32[256,1536]{1,0:T(8,128)S(1)}, f32[256,1536]{1,0:T(8,128)S(1)}, f32[256,1536]{1,0:T(8,128)S(1)}) custom-call(s32[114]{0:T(128)S(1)} %pad_add_fusion.sc, bf16[256,1536]{1,0:T(8,128)(2,1)S(1)} %copy-done.12, bf16[256,1536]{1,0:T(8,128)(2,1)S(1)} %bitcast.28, ...), custom_call_target="tpu_custom_call" | custom-call | flops 20000000000 | bytes 20000000000 | tf_op jit(solution)/shard_map/near_key_grads/pallas_call | solution.py:383
  151.6 17.4 %collective-permute-done.17.both = bf16[512,512]{1,0:T(8,128)(2,1)S(1)} collective-permute-done((bf16[512,512]{1,0:T(8,128)(2,1)S(1)}, bf16[512,512]{1,0:T(8,128)(2,1)S(1)}, u32[]{:S(2)}, u32[]{:S(2)}) %collective-permute-start.17) | collective-permute-done | bytes 524320 | tf_op jit(solution)/shard_map/ppermute | solution.py:409
  169.1 2.2 %partner_far_grads.3 = (bf16[512,512]{1,0:T(8,128)(2,1)S(1)}, f32[256,512]{1,0:T(8,128)}, f32[256,512]{1,0:T(8,128)}) custom-call(s32[114]{0:T(128)S(1)} %pad_add_fusion.sc, bf16[256,1536]{1,0:T(8,128)(2,1)S(1)} %get-tuple-element.54.knp, bf16[256,1536]{1,0:T(8,128)(2,1)S(1)} %collective-permute-done.2.vp, ...), custom_call_target="tpu_custom_call" | custom-call | flops 20000000000 | bytes 20000000000 | tf_op jit(solution)/shard_map/partner_far_grads/pallas_call | solution.py:383
  172.6 2.2 %partner_far_grads.4 = (bf16[512,512]{1,0:T(8,128)(2,1)S(1)}, f32[256,512]{1,0:T(8,128)}, f32[256,512]{1,0:T(8,128)}) custom-call(s32[114]{0:T(128)S(1)} %pad_add_fusion.sc, bf16[256,1536]{1,0:T(8,128)(2,1)S(1)} %get-tuple-element.54.knp, bf16[256,1536]{1,0:T(8,128)(2,1)S(1)} %collective-permute-done.2.vp, ...), custom_call_target="tpu_custom_call" | custom-call | flops 20000000000 | bytes 20000000000 | tf_op jit(solution)/shard_map/partner_far_grads/pallas_call | solution.py:383
  174.8 2.0 collective-permute-start.19
  178.1 2.2 %partner_far_grads.5 = (bf16[512,512]{1,0:T(8,128)(2,1)S(1)}, f32[256,512]{1,0:T(8,128)}, f32[256,512]{1,0:T(8,128)}) custom-call(s32[114]{0:T(128)S(1)} %pad_add_fusion.sc, bf16[256,1536]{1,0:T(8,128)(2,1)S(1)} %get-tuple-element.54.knp, bf16[256,1536]{1,0:T(8,128)(2,1)S(1)} %collective-permute-done.2.vp, ...), custom_call_target="tpu_custom_call" | custom-call | flops 20000000000 | bytes 20000000000 | tf_op jit(solution)/shard_map/partner_far_grads/pallas_call | solution.py:383
  181.6 2.5 %finish_queries.1 = bf16[256,1536]{1,0:T(8,128)(2,1)} custom-call(f32[2,128]{1,0:T(2,128)S(1)} %bitcast.18, f32[1536,256]{1,0:T(8,128)S(1)} %get-tuple-element.55._.dqt, bf16[1536,256]{1,0:T(8,128)(2,1)S(1)} %collective-permute-done.11.dqr, bf16[256,1536]{1,0:T(8,128)(2,1)S(1)} %bitcast.33, f32[256,512]{1,0:T(8,128)S(1)} %get-tuple-element.74._.refs_6_), custom_call_target="tpu_custom_call" | custom-call | flops 20000000000 | bytes 20000000000 | tf_op jit(solution)/shard_map/finish_queries/pallas_call | solution.py:383
  184.1 2.0 collective-permute-done.18.refs_2_
  186.1 17.3 %collective-permute-done.20.refs_8_ = bf16[512,512]{1,0:T(8,128)(2,1)S(1)} collective-permute-done((bf16[512,512]{1,0:T(8,128)(2,1)S(1)}, bf16[512,512]{1,0:T(8,128)(2,1)S(1)}, u32[]{:S(2)}, u32[]{:S(2)}) %collective-permute-start.20) | collective-permute-done | bytes 524320 | tf_op jit(solution)/shard_map/ppermute | solution.py:406
  203.4 2.6 %finish_keys.1 = (bf16[256,1536]{1,0:T(8,128)(2,1)}, bf16[256,1536]{1,0:T(8,128)(2,1)}) custom-call(f32[2,128]{1,0:T(2,128)S(1)} %bitcast.19, bf16[256,1536]{1,0:T(8,128)(2,1)S(1)} %bitcast.37, f32[256,512]{1,0:T(8,128)S(1)} %get-tuple-element.70._.refs_0_, f32[256,512]{1,0:T(8,128)S(1)} %get-tuple-element.75.refs_1_, ...), custom_call_target="tpu_custom_call" | custom-call | flops 20000000000 | bytes 20000000000 | tf_op jit(solution)/shard_map/finish_keys/pallas_call | solution.py:383
  (63 shorter events, 16.8 us)
Async XLA Ops:
  0.6 42.0 %collective-permute-start.3 = (bf16[256,1536]{1,0:T(8,128)(2,1)}, bf16[256,1536]{1,0:T(8,128)(2,1)}, u32[]{:S(2)}, u32[]{:S(2)}) collective-permute-start(bf16[256,1536]{1,0:T(8,128)(2,1)} %bitcast.34), channel_id=1, source_target_pairs={{1,2},{2,1},{3,4},{4,3},{5,6},{6,5},{7,8},{8,7},{9,10},{10,9},{11,... | collective-permute-start | bytes 2359304 | tf_op jit(solution)/shard_map/ppermute | solution.py:409
  8.2 34.9 %collective-permute-start.1 = (bf16[256,1536]{1,0:T(8,128)(2,1)}, bf16[256,1536]{1,0:T(8,128)(2,1)}, u32[]{:S(2)}, u32[]{:S(2)}) collective-permute-start(bf16[256,1536]{1,0:T(8,128)(2,1)} %bitcast.35), channel_id=1, source_target_pairs={{0,1},{1,0},{2,3},{3,2},{4,5},{5,4},{6,7},{7,6},{8,9},{9,8},{10,11... | collective-permute-start | bytes 2359304 | tf_op jit(solution)/shard_map/ppermute | solution.py:406
  8.3 44.2 %collective-permute-start.4 = (bf16[256,1536]{1,0:T(8,128)(2,1)}, bf16[256,1536]{1,0:T(8,128)(2,1)}, u32[]{:S(2)}, u32[]{:S(2)}) collective-permute-start(bf16[256,1536]{1,0:T(8,128)(2,1)} %bitcast.24), channel_id=1, source_target_pairs={{1,2},{2,1},{3,4},{4,3},{5,6},{6,5},{7,8},{8,7},{9,10},{10,9},{11,... | collective-permute-start | bytes 2359304 | tf_op jit(solution)/shard_map/ppermute | solution.py:409
  12.2 35.5 %collective-permute-start.2 = (bf16[256,1536]{1,0:T(8,128)(2,1)}, bf16[256,1536]{1,0:T(8,128)(2,1)S(1)}, u32[]{:S(2)}, u32[]{:S(2)}) collective-permute-start(bf16[256,1536]{1,0:T(8,128)(2,1)} %bitcast.25), channel_id=1, source_target_pairs={{0,1},{1,0},{2,3},{3,2},{4,5},{5,4},{6,7},{7,6},{8,9},{9,8},{10,11... | collective-permute-start | bytes 2359304 | tf_op jit(solution)/shard_map/ppermute | solution.py:406
  33.2 1.1 copy-start
  34.4 1.1 copy-start.3
  36.6 5.8 %copy-start.13 = (s32[16,6]{0,1:T(8,128)S(1)}, s32[16,6]{0,1:T(8,128)}, u32[]{:S(2)}) copy-start(s32[16,6]{0,1:T(8,128)} %param.13) | copy-start | bytes 1156
  36.6 5.9 %copy-start.14 = (s32[16]{0:T(128)S(1)}, s32[16]{0:T(128)}, u32[]{:S(2)}) copy-start(s32[16]{0:T(128)} %param.12) | copy-start | bytes 196
  36.6 15.9 %copy-start.1 = (bf16[1,256,1536]{2,1,0:T(8,128)(2,1)S(1)}, bf16[1,256,1536]{2,1,0:T(8,128)(2,1)}, u32[]{:S(2)}) copy-start(bf16[1,256,1536]{2,1,0:T(8,128)(2,1)} %param.10) | copy-start | bytes 2359300
  36.6 15.9 %copy-start.2 = (bf16[1,256,1536]{2,1,0:T(8,128)(2,1)S(1)}, bf16[1,256,1536]{2,1,0:T(8,128)(2,1)}, u32[]{:S(2)}) copy-start(bf16[1,256,1536]{2,1,0:T(8,128)(2,1)} %param.9) | copy-start | bytes 2359300
  40.7 85.0 %collective-permute-start.9 = (bf16[256,1536]{1,0:T(8,128)(2,1)}, bf16[256,1536]{1,0:T(8,128)(2,1)S(1)}, u32[]{:S(2)}, u32[]{:S(2)}) collective-permute-start(bf16[256,1536]{1,0:T(8,128)(2,1)} %get-tuple-element.56), channel_id=1, source_target_pairs={{0,1},{1,0},{2,3},{3,2},{4,5},{5,4},{6,7},{7,6},{8,9},{9,8},{10,11... | collective-permute-start | bytes 2359304 | tf_op jit(solution)/shard_map/ppermute | solution.py:406
  42.7 35.4 %collective-permute-start = (bf16[256,1536]{1,0:T(8,128)(2,1)}, bf16[256,1536]{1,0:T(8,128)(2,1)S(1)}, u32[]{:S(2)}, u32[]{:S(2)}) collective-permute-start(bf16[256,1536]{1,0:T(8,128)(2,1)} %copy-done.7), channel_id=1, source_target_pairs={{0,1},{1,0},{2,3},{3,2},{4,5},{5,4},{6,7},{7,6},{8,9},{9,8},{10,11... | collective-permute-start | bytes 2359304 | tf_op jit(solution)/shard_map/ppermute | solution.py:406
  43.1 39.4 %collective-permute-start.5 = (bf16[256,1536]{1,0:T(8,128)(2,1)}, bf16[256,1536]{1,0:T(8,128)(2,1)S(1)}, u32[]{:S(2)}, u32[]{:S(2)}) collective-permute-start(bf16[256,1536]{1,0:T(8,128)(2,1)} %collective-permute-done.1.kp), channel_id=1, source_target_pairs={{1,2},{2,1},{3,4},{4,3},{5,6},{6,5},{7,8},{8,7},{9,10},{10,9},{11,... | collective-permute-start | bytes 2359304 | tf_op jit(solution)/shard_map/ppermute | solution.py:409
  47.7 38.3 %collective-permute-start.6 = (bf16[256,1536]{1,0:T(8,128)(2,1)S(1)}, bf16[256,1536]{1,0:T(8,128)(2,1)S(1)}, u32[]{:S(2)}, u32[]{:S(2)}) collective-permute-start(bf16[256,1536]{1,0:T(8,128)(2,1)S(1)} %collective-permute-done.2.vp), channel_id=1, source_target_pairs={{1,2},{2,1},{3,4},{4,3},{5,6},{6,5},{7,8},{8,7},{9,10},{10,9},{11,... | collective-permute-start | bytes 2359304 | tf_op jit(solution)/shard_map/ppermute | solution.py:409
  52.6 1.1 copy-start.8
  61.8 78.2 %collective-permute-start.14 = (bf16[256,1536]{1,0:T(8,128)(2,1)S(1)}, bf16[256,1536]{1,0:T(8,128)(2,1)S(1)}, u32[]{:S(2)}, u32[]{:S(2)}) collective-permute-start(bf16[256,1536]{1,0:T(8,128)(2,1)S(1)} %get-tuple-element.59), channel_id=1, source_target_pairs={{1,2},{2,1},{3,4},{4,3},{5,6},{6,5},{7,8},{8,7},{9,10},{10,9},{11,... | collective-permute-start | bytes 2359304 | tf_op jit(solution)/shard_map/ppermute | solution.py:409
  78.0 66.1 %collective-permute-start.15 = (bf16[256,1536]{1,0:T(8,128)(2,1)S(1)}, bf16[256,1536]{1,0:T(8,128)(2,1)S(1)}, u32[]{:S(2)}, u32[]{:S(2)}) collective-permute-start(bf16[256,1536]{1,0:T(8,128)(2,1)S(1)} %get-tuple-element.60), channel_id=1, source_target_pairs={{1,2},{2,1},{3,4},{4,3},{5,6},{6,5},{7,8},{8,7},{9,10},{10,9},{11,... | collective-permute-start | bytes 2359304 | tf_op jit(solution)/shard_map/ppermute | solution.py:409
  91.3 4.9 %collective-permute-start.8 = (f32[24,256]{1,0:T(8,128)S(1)}, f32[24,256]{1,0:T(8,128)S(1)}, u32[]{:S(2)}, u32[]{:S(2)}) collective-permute-start(f32[24,256]{1,0:T(8,128)S(1)} %get-tuple-element.51), channel_id=1, source_target_pairs={{0,1},{1,0},{2,3},{3,2},{4,5},{5,4},{6,7},{7,6},{8,9},{9,8},{10,11... | collective-permute-start | bytes 73736 | tf_op jit(solution)/shard_map/ppermute | solution.py:406
  91.4 17.6 %collective-permute-start.7 = (bf16[1536,256]{1,0:T(8,128)(2,1)S(1)}, bf16[1536,256]{1,0:T(8,128)(2,1)S(1)}, u32[]{:S(2)}, u32[]{:S(2)}) collective-permute-start(bf16[1536,256]{1,0:T(8,128)(2,1)S(1)} %get-tuple-element.50), channel_id=1, source_target_pairs={{0,1},{1,0},{2,3},{3,2},{4,5},{5,4},{6,7},{7,6},{8,9},{9,8},{10,11... | collective-permute-start | bytes 2359304 | tf_op jit(solution)/shard_map/ppermute | solution.py:406
  109.0 3.4 %copy-start.9 = (bf16[256,1536]{1,0:T(8,128)(2,1)S(1)}, bf16[256,1536]{1,0:T(8,128)(2,1)}, u32[]{:S(2)}) copy-start(bf16[256,1536]{1,0:T(8,128)(2,1)} %copy-done.7) | copy-start | bytes 2359300
  109.0 3.4 %copy-start.12 = (bf16[256,1536]{1,0:T(8,128)(2,1)S(1)}, bf16[256,1536]{1,0:T(8,128)(2,1)}, u32[]{:S(2)}) copy-start(bf16[256,1536]{1,0:T(8,128)(2,1)} %copy-done.10) | copy-start | bytes 2359300
  110.9 9.3 %collective-permute-start.10 = (f32[24,256]{1,0:T(8,128)S(1)}, f32[24,256]{1,0:T(8,128)S(1)}, u32[]{:S(2)}, u32[]{:S(2)}) collective-permute-start(f32[24,256]{1,0:T(8,128)S(1)} %get-tuple-element.53.st), channel_id=1, source_target_pairs={{0,1},{1,0},{2,3},{3,2},{4,5},{5,4},{6,7},{7,6},{8,9},{9,8},{10,11... | collective-permute-start | bytes 73736 | tf_op jit(solution)/shard_map/ppermute | solution.py:406
  120.3 24.0 %collective-permute-start.13 = (f32[48,256]{1,0:T(8,128)S(1)}, f32[48,256]{1,0:T(8,128)S(1)}, u32[]{:S(2)}, u32[]{:S(2)}) collective-permute-start(f32[48,256]{1,0:T(8,128)S(1)} %pad_maximum_fusion), channel_id=1, source_target_pairs={{1,2},{2,1},{3,4},{4,3},{5,6},{6,5},{7,8},{8,7},{9,10},{10,9},{11,... | collective-permute-start | bytes 147464 | tf_op jit(solution)/shard_map/ppermute | solution.py:409
  130.5 47.6 %collective-permute-start.12 = (bf16[512,512]{1,0:T(8,128)(2,1)S(1)}, bf16[512,512]{1,0:T(8,128)(2,1)S(1)}, u32[]{:S(2)}, u32[]{:S(2)}) collective-permute-start(bf16[512,512]{1,0:T(8,128)(2,1)S(1)} %get-tuple-element.58), channel_id=1, source_target_pairs={{1,2},{2,1},{3,4},{4,3},{5,6},{6,5},{7,8},{8,7},{9,10},{10,9},{11,... | collective-permute-start | bytes 1572872 | tf_op jit(solution)/shard_map/ppermute | solution.py:409
  134.7 37.9 %collective-permute-start.16 = (bf16[512,512]{1,0:T(8,128)(2,1)S(1)}, bf16[512,512]{1,0:T(8,128)(2,1)S(1)}, u32[]{:S(2)}, u32[]{:S(2)}) collective-permute-start(bf16[512,512]{1,0:T(8,128)(2,1)S(1)} %get-tuple-element.67), channel_id=1, source_target_pairs={{1,2},{2,1},{3,4},{4,3},{5,6},{6,5},{7,8},{8,7},{9,10},{10,9},{11,... | collective-permute-start | bytes 1572872 | tf_op jit(solution)/shard_map/ppermute | solution.py:409
  140.0 29.1 %collective-permute-start.17 = (bf16[512,512]{1,0:T(8,128)(2,1)S(1)}, bf16[512,512]{1,0:T(8,128)(2,1)S(1)}, u32[]{:S(2)}, u32[]{:S(2)}) collective-permute-start(bf16[512,512]{1,0:T(8,128)(2,1)S(1)} %get-tuple-element.68), channel_id=1, source_target_pairs={{1,2},{2,1},{3,4},{4,3},{5,6},{6,5},{7,8},{8,7},{9,10},{10,9},{11,... | collective-permute-start | bytes 1572872 | tf_op jit(solution)/shard_map/ppermute | solution.py:409
  144.2 37.4 %collective-permute-start.11 = (bf16[1536,256]{1,0:T(8,128)(2,1)S(1)}, bf16[1536,256]{1,0:T(8,128)(2,1)S(1)}, u32[]{:S(2)}, u32[]{:S(2)}) collective-permute-start(bf16[1536,256]{1,0:T(8,128)(2,1)S(1)} %get-tuple-element.57._), channel_id=1, source_target_pairs={{0,1},{1,0},{2,3},{3,2},{4,5},{5,4},{6,7},{7,6},{8,9},{9,8},{10,11... | collective-permute-start | bytes 2359304 | tf_op jit(solution)/shard_map/ppermute | solution.py:406
  171.3 14.9 %collective-permute-start.18 = (bf16[512,512]{1,0:T(8,128)(2,1)S(1)}, bf16[512,512]{1,0:T(8,128)(2,1)S(1)}, u32[]{:S(2)}, u32[]{:S(2)}) collective-permute-start(bf16[512,512]{1,0:T(8,128)(2,1)S(1)} %get-tuple-element.69._), channel_id=1, source_target_pairs={{0,1},{1,0},{2,3},{3,2},{4,5},{5,4},{6,7},{7,6},{8,9},{9,8},{10,11... | collective-permute-start | bytes 1572872 | tf_op jit(solution)/shard_map/ppermute | solution.py:406
  174.8 28.6 %collective-permute-start.19 = (bf16[512,512]{1,0:T(8,128)(2,1)S(1)}, bf16[512,512]{1,0:T(8,128)(2,1)S(1)}, u32[]{:S(2)}, u32[]{:S(2)}) collective-permute-start(bf16[512,512]{1,0:T(8,128)(2,1)S(1)} %get-tuple-element.71._), channel_id=1, source_target_pairs={{0,1},{1,0},{2,3},{3,2},{4,5},{5,4},{6,7},{7,6},{8,9},{9,8},{10,11... | collective-permute-start | bytes 1572872 | tf_op jit(solution)/shard_map/ppermute | solution.py:406
  180.3 1.3 copy-start.4
  180.3 23.1 %collective-permute-start.20 = (bf16[512,512]{1,0:T(8,128)(2,1)S(1)}, bf16[512,512]{1,0:T(8,128)(2,1)S(1)}, u32[]{:S(2)}, u32[]{:S(2)}) collective-permute-start(bf16[512,512]{1,0:T(8,128)(2,1)S(1)} %get-tuple-element.73._), channel_id=1, source_target_pairs={{0,1},{1,0},{2,3},{3,2},{4,5},{5,4},{6,7},{7,6},{8,9},{9,8},{10,11... | collective-permute-start | bytes 1572872 | tf_op jit(solution)/shard_map/ppermute | solution.py:406
  181.6 21.8 %copy-start.6 = (bf16[1,256,1536]{2,1,0:T(8,128)(2,1)S(1)}, bf16[1,256,1536]{2,1,0:T(8,128)(2,1)}, u32[]{:S(2)}) copy-start(bf16[1,256,1536]{2,1,0:T(8,128)(2,1)} %param.8) | copy-start | bytes 2359300
  (4 other events, 4.0 us)

commit v2 on v1

--- a/solution.py
+++ b/solution.py
@@ -14,7 +14,17 @@
 HB = 4
 DEPTH = 1
 LOW = -1e30
-COST = 20_000_000_000
+COST = dict.fromkeys(
+    (
+        "partner_forward",
+        "own_forward_far",
+        "merge_stats",
+        "partner_query_grads",
+        "own_query_grads",
+    ),
+    0,
+)
+OTHER = 20_000_000_000
 SCALE = math.log2(math.e) / math.sqrt(128)
 BF = jnp.bfloat16
 F32 = jnp.float32
@@ -115,11 +125,12 @@
     return units
 
 
-def backward_units(permit, kn, v, qn, do, st, use, first=None, heads=None, base=0):
+def backward_units(permit, kn, v, qn, do, st, use, half=0, first=None, heads=None):
     if heads is None:
         heads = pl.num_programs(0) * HB
     if first is None:
         first = pl.program_id(0) * HB
+    base = 2 * half * heads
     units = []
     for j in range(HB):
         def scores(c=cols(j)):
@@ -195,7 +206,13 @@
     put_rows(ml_ref, 1, l_ref)
 
 
-def partner_forward(sc, g, qn, kne, ve, kf, vf, o_ref, ml_ref, knf, m_ref, l_ref, acc_ref):
+def delta_row(out, do):
+    return jnp.sum(out * jnp.transpose(do).astype(F32), axis=0, keepdims=True)
+
+
+def partner_forward(
+    sc, g, qn, kne, ve, kf, vf, do, o_ref, ml_ref, knf, m_ref, l_ref, d_ref, acc_ref
+):
     me, partner, near, far = around(sc)
     for j in range(HB):
         knf[:, cols(j)] = normed(kf[:, cols(j)], g[1:2, :])
@@ -205,48 +222,87 @@
         forward_units(allowed(sc, partner, near), kne, ve, qn, m_ref, l_ref, acc_ref)
         + forward_units(allowed(sc, partner, far), knf, vf, qn, m_ref, l_ref, acc_ref)
     )
-    put_rows(ml_ref, 0, m_ref)
-    put_rows(ml_ref, 1, l_ref)
     for j in range(HB):
         total = l_ref[j]
         share = jnp.where(total > 0.0, 1.0 / jnp.where(total > 0.0, total, 1.0), 0.0)
-        o_ref[cols(j), :] = (acc_ref[cols(j), :] * share).astype(BF)
-
-
-def own_forward_far(sc, qn, knf, vf, acc0, ml0, acc_ref, ml_ref, m_ref, l_ref):
-    me, partner, near, far = around(sc)
+        out = acc_ref[cols(j), :] * share
+        o_ref[cols(j), :] = out.astype(BF)
+        d_ref[j] = delta_row(out, do[:, cols(j)])
+    for index, rows in enumerate((m_ref, l_ref, d_ref)):
+        put_rows(ml_ref, index, rows)
+
+
+def own_forward_far(
+    sc, qn, knf, vf, do, acc0, ml0, mlp, acc_ref, st_ref, m_ref, l_ref, d_ref
+):
+    me, partner, near, far = around(sc)
+
+    @pl.when(pl.program_id(0) == 0)
+    def _():
+        st_ref[mlp.shape[0] :, :] = mlp[...]
+
     get_rows(ml0, 0, m_ref)
     get_rows(ml0, 1, l_ref)
     acc_ref[...] = acc0[...]
     emit(forward_units(allowed(sc, me, far), knf, vf, qn, m_ref, l_ref, acc_ref))
-    put_rows(ml_ref, 0, m_ref)
-    put_rows(ml_ref, 1, l_ref)
-
-
-def merge(acc_ref, ml_ref, o_ret, ml_ret, d_out, att_ref, st_ref):
+    for j in range(HB):
+        d_ref[j] = delta_row(acc_ref[cols(j), :] * (1.0 / l_ref[j]), do[:, cols(j)])
+    for index, rows in enumerate((m_ref, l_ref, d_ref)):
+        put_rows(st_ref, index, rows)
+
+
+def weights_of(first, second, heads):
+    m1, l1 = first[:heads], first[heads : 2 * heads]
+    m2, l2 = second[:heads], second[heads : 2 * heads]
+    m = jnp.maximum(m1, m2)
+    w1, w2 = l1 * jnp.exp2(m1 - m), l2 * jnp.exp2(m2 - m)
+    total = w1 + w2
+    return w1 / total, w2 / total, m + jnp.log2(total)
+
+
+def merge_stats(mine, got, o_ref, st_ref, sh_ref, o_out):
+    o_out[...] = o_ref[...]
+
+    @pl.when(pl.program_id(0) == 0)
+    def _():
+        size = mine.shape[0] // 2
+        heads = size // 3
+        both = ((mine[:size], got[size:]), (got[:size], mine[size:]))
+        for half, (first, second) in enumerate(both):
+            w1, w2, lse = weights_of(first, second, heads)
+            base = 2 * half * heads
+            st_ref[base : base + heads] = lse
+            st_ref[base + heads : base + 2 * heads] = (
+                w1 * first[2 * heads :] + w2 * second[2 * heads :]
+            )
+            if half == 0:
+                total = first[heads : 2 * heads]
+                sh_ref[:heads] = w1 / total
+                sh_ref[heads:] = w2
+
+
+def merge(acc_ref, sh, o_ret, _, att_ref):
     step = pl.program_id(0)
     heads = pl.num_programs(0) * HB
     for j in range(HB):
-        h = step * HB + j
-        m1, l1 = ml_ref[pl.ds(h, 1), :], ml_ref[pl.ds(heads + h, 1), :]
-        m2, l2 = ml_ret[pl.ds(h, 1), :], ml_ret[pl.ds(heads + h, 1), :]
-        m = jnp.maximum(m1, m2)
-        a1 = jnp.exp2(m1 - m)
-        a2 = jnp.exp2(m2 - m) * l2
-        total = l1 * a1 + a2
-        inv = 1.0 / total
-        out = acc_ref[cols(j), :] * (a1 * inv) + o_ret[cols(j), :].astype(F32) * (a2 * inv)
-        low = out.astype(BF)
-        att_ref[:, cols(j)] = jnp.transpose(low)
-        grads = jnp.transpose(d_out[:, cols(j)]).astype(F32)
-        st_ref[pl.ds(h, 1), :] = m + jnp.log2(total)
-        st_ref[pl.ds(heads + h, 1), :] = jnp.sum(low.astype(F32) * grads, axis=0, keepdims=True)
+        c, h = cols(j), step * HB + j
+        w1, w2 = sh[pl.ds(h, 1), :], sh[pl.ds(heads + h, 1), :]
+        out = acc_ref[c, :] * w1 + o_ret[c, :].astype(F32) * w2
+        att_ref[:, c] = jnp.transpose(out.astype(BF))
+
+
+def stack(both, qn, do):
+    @pl.when(pl.program_id(0) == 0)
+    def _():
+        both[:ROWS] = qn[...]
+        both[ROWS:] = do[...]
 
 
 def own_query_grads(
-    sc, qn, do, st, knx, v, knp, vp, kne, ve, knf, vf, dq_ref, dk_ref, dv_ref
+    sc, qn, do, st, knx, v, knp, vp, kne, ve, knf, vf, qs, ds, _, dq_ref, dk_ref, dv_ref, both_out
 ):
     me, partner, near, far = around(sc)
+    stack(both_out, qs, ds)
     clear(dq_ref, dk_ref, dv_ref)
 
     def both(c, found):
@@ -260,43 +316,36 @@
     emit(units)
 
 
-def partner_query_grads(sc, qn, do, st, kne, ve, knf, vf, _, dq_ref, *rest):
-    acc_ref = rest[-1]
-    me, partner, near, far = around(sc)
-    for chunk, both in enumerate(rest[:-1]):
-        @pl.when(pl.program_id(0) == chunk)
-        def _(both=both):
-            both[:ROWS] = qn[...]
-            both[ROWS:] = do[...]
-
+def partner_query_grads(
+    sc, qn, do, st, kne, ve, knf, vf, qs, ds, dq_ref, both_out, acc_ref
+):
+    me, partner, near, far = around(sc)
+    stack(both_out, qs, ds)
     clear(acc_ref)
     units = []
     for dev, kn, val in ((near, kne, ve), (far, knf, vf)):
         use = partial(query_use, kn, acc_ref)
-        units += backward_units(allowed(sc, partner, dev), kn, val, qn, do, st, use)
+        units += backward_units(allowed(sc, partner, dev), kn, val, qn, do, st, use, 1)
     emit(units)
     dq_ref[...] = acc_ref[...].astype(BF)
 
 
 def near_key_grads(
-    sc, knx, v, qnp, dop, stp, knp, vp, qne, doe, ste, dk0, dv0, _,
-    dkx, dvx, dkp, dvp,
+    sc, knx, v, qnp, dop, st, knp, vp, qne, doe, ste, dk0, dv0, qs, ds, _,
+    dkx, dvx, dkp, dvp, both_out,
 ):
     me, partner, near, far = around(sc)
+    stack(both_out, qs, ds)
     dkx[...] = dk0[...]
     dvx[...] = dv0[...]
     clear(dkp, dvp)
+    own = partial(key_use, qnp, dop, dkx, dvx)
+    use = partial(key_use, qne, doe, dkx, dvx)
+    back = partial(key_use, qne, doe, dkp, dvp)
     emit(
-        backward_units(
-            allowed(sc, partner, me), knx, v, qnp, dop, stp, partial(key_use, qnp, dop, dkx, dvx)
-        )
-        + backward_units(
-            allowed(sc, near, me), knx, v, qne, doe, ste, partial(key_use, qne, doe, dkx, dvx)
-        )
-        + backward_units(
-            allowed(sc, near, partner), knp, vp, qne, doe, ste,
-            partial(key_use, qne, doe, dkp, dvp),
-        )
+        backward_units(allowed(sc, partner, me), knx, v, qnp, dop, st, own, 1)
+        + backward_units(allowed(sc, near, me), knx, v, qne, doe, ste, use)
+        + backward_units(allowed(sc, near, partner), knp, vp, qne, doe, ste, back)
     )
 
 
@@ -308,7 +357,7 @@
     emit(
         backward_units(
             allowed(sc, far, partner), knp, vp, qn, do, st, partial(key_use, qn, do, dk, dv),
-            chunk * HB, heads, 2 * heads,
+            1, chunk * HB, heads,
         )
     )
     out[:ROWS] = dk[...].astype(BF)
@@ -323,7 +372,7 @@
     emit(
         backward_units(
             allowed(sc, far, me), knx, v, qn, do, st, partial(key_use, qn, do, dk, dv),
-            chunk * HB, heads, 2 * heads,
+            1, chunk * HB, heads,
         )
     )
 
@@ -385,7 +434,11 @@
         name=name or body.__name__,
         grid_spec=grid_spec,
         out_shape=shapes,
-        cost_estimate=pl.CostEstimate(flops=COST, transcendentals=0, bytes_accessed=COST),
+        cost_estimate=pl.CostEstimate(
+            flops=COST.get(name or body.__name__, OTHER),
+            transcendentals=0,
+            bytes_accessed=COST.get(name or body.__name__, OTHER),
+        ),
         compiler_params=pltpu.CompilerParams(
             dimension_semantics=("arbitrary",), vmem_limit_bytes=32 << 20
         ),
@@ -439,58 +492,70 @@
         [tall_f, stats] + [wide_bf] * 4, (row_s, row_s),
     )
     qne, doe = beyond(qn3, do3)
+    parts = (FULL, (3 * heads, ROWS), F32)
     op, mlp, knf = run(
-        partner_forward, scalars, gain + wide(qnp, kne, ve, kf, vf),
-        [tall_bf, stats, wide_bf], (row_s, row_s, acc_t),
-    )
-    o_ret, ml_ret = across(op, mlp)
-    acc, ml = run(
+        partner_forward, scalars, gain + wide(qnp, kne, ve, kf, vf, dop),
+        [tall_bf, parts, wide_bf], (row_s, row_s, row_s, acc_t),
+    )
+    acc, mine = run(
         own_forward_far, scalars,
-        wide(qn, knf, vf) + [(TALL, acc), (FULL, ml)], [tall_f, stats], (row_s, row_s),
-    )
-    att, st = run(
-        merge, (), [(TALL, acc), (FULL, ml), (TALL, o_ret), (FULL, ml_ret)] + wide(do),
-        [wide_bf, stats],
-    )
-    (stp,) = across(st)
-    (st2,) = beyond(jnp.concatenate([st, stp], axis=0))
-    dqt, dk, dv = run(
+        wide(qn, knf, vf, do) + [(TALL, acc), (FULL, ml), (FULL, mlp)],
+        [tall_f, (FULL, (6 * heads, ROWS), F32)], (row_s, row_s, row_s),
+    )
+    (got,) = across(mine)
+    st, shares, op = run(
+        merge_stats, (), [(FULL, mine), (FULL, got), (TALL, op)],
+        [(FULL, (4 * heads, ROWS), F32), stats, tall_bf], (), chunks,
+    )
+    (ste,) = beyond(st)
+    (o_ret,) = across(op)
+
+    def send(i):
+        return [(i, qnp), (i, dop)]
+
+    dqp, sent0 = run(
+        partner_query_grads, scalars,
+        wide(qnp, dop) + [(FULL, st)] + wide(kne, ve, knf, vf) + send(0),
+        [tall_bf, pair], (acc_t,),
+    )
+    (dqr,) = across(dqp)
+    dqt, dk, dv, sent1 = run(
         own_query_grads, scalars,
-        wide(qn, do) + [(FULL, st)] + wide(knx, v, knp, vp, kne, ve, knf, vf),
-        [tall_f, wide_f, wide_f],
-    )
-    dqp, *sent = run(
-        partner_query_grads, scalars,
-        wide(qnp, dop) + [(FULL, stp)] + wide(kne, ve, knf, vf) + [(ORDER, dqt)],
-        [tall_bf] + [pair] * chunks, (acc_t,),
-    )
-    (dqr,) = across(dqp)
-    far = beyond(*sent)
-    dk, dv, dkp, dvp = run(
+        wide(qn, do) + [(FULL, st)] + wide(knx, v, knp, vp, kne, ve, knf, vf) + send(1)
+        + [(ORDER, dqp)],
+        [tall_f, wide_f, wide_f, pair],
+    )
+    dk, dv, dkp, dvp, sent2 = run(
         near_key_grads, scalars,
-        wide(knx, v, qnp, dop) + [(FULL, stp)] + wide(knp, vp, qne, doe) + [(FULL, st2)]
-        + wide(dk, dv) + [(ORDER, dqp)],
-        [wide_f] * 4,
-    )
-    last, back, own = dkp, [], []
+        wide(knx, v, qnp, dop) + [(FULL, st)] + wide(knp, vp, qne, doe) + [(FULL, ste)]
+        + wide(dk, dv) + send(2) + [(ORDER, dqt)],
+        [wide_f] * 4 + [pair],
+    )
+    far = beyond(sent0, sent1, sent2)
+    (att,) = run(
+        merge, (), [(TALL, acc), (FULL, shares), (TALL, o_ret), (ORDER, dkp)], [wide_bf], (), chunks,
+    )
+    last, back, own = att, [], []
     for i in range(chunks):
         out, _, _ = run(
             partial(partner_far_grads, i, heads), scalars,
-            [(i, knp), (i, vp), (FULL, far[i]), (FULL, st2), (i, dkp), (i, dvp), (ORDER, last)],
+            [(i, knp), (i, vp), (FULL, far[i]), (FULL, ste), (i, dkp), (i, dvp), (ORDER, last)],
             [pair, part_f, part_f], (), 1, "partner_far_grads",
         )
         back += across(out)
         dki, dvi = run(
             partial(own_far_grads, i, heads), scalars,
-            [(i, knx), (i, v), (FULL, far[i]), (FULL, st2), (i, dk), (i, dv), (ORDER, out)],
+            [(i, knx), (i, v), (FULL, far[i]), (FULL, ste), (i, dk), (i, dv), (ORDER, out)],
             [part_f, part_f], (), 1, "own_far_grads",
         )
         own.append((dki, dvi))
         last = dki
-    (dq_out,) = run(
-        finish_queries, (), gain + [(TALL, dqt), (TALL, dqr)] + wide(q) + [(ORDER, last)],
-        [wide_bf],
-    )
+        if i == 0:
+            (dq_out,) = run(
+                finish_queries, (),
+                gain + [(TALL, dqt), (TALL, dqr)] + wide(q) + [(ORDER, last)], [wide_bf],
+            )
+            last = dq_out
     pieces = []
     for i in range(chunks):
         pieces += [(FULL, own[i][0]), (FULL, own[i][1]), (FULL, back[i])]

time: 207 us -> 180 us (0.87)
  waiting for transfers between devices: 64.7 us -> 34.7 us
  Pallas kernels: 54.6 us -> 57.2 us
    ppermute x11 -> x10, waiting for transfers between devices: 43.7 us -> 27.5 us  [across(): return [lax.ppermute(value, 'ctx', inner) for value in values]]
    ppermute x10, waiting for transfers between devices: 21.1 us -> 7.14 us  [beyond(): return [lax.ppermute(value, 'ctx', outer) for value in values]]
    pallas_call x16 -> x17, Pallas kernels: 54.6 us -> 57.2 us  [run(): pl.pallas_call(body, name=name or body.__name__, grid_spec=grid_spec, out...]
    ppermute x11 -> x10, starting transfers between devices: 9.19 us -> 7.97 us  [across(): return [lax.ppermute(value, 'ctx', inner) for value in values]]
  transfers between devices with their start and end apart: 21 -> 20, of which waited for: 6 -> 4; matrix products, arithmetic and copies ran while one was open for 0% -> 0% of each run, Pallas kernels for 25% -> 31%
where the time goes in v2:
time: 180 us; the launch traced here: 179 us
  starting transfers between devices  57.2 us (32%)
  Pallas kernels  57.2 us (32%)
  waiting for transfers between devices  34.7 us (19%)
  blocking collectives  19.6 us (11%)
  local copies, waits for them, and re-layouts  9.09 us (5%)
    pallas_call x17, Pallas kernels, run(): pl.pallas_call(body, name=name or body.__name__, grid_spec=grid_spec, out...  57.2 us
    ppermute x10, starting transfers between devices, beyond(): return [lax.ppermute(value, 'ctx', outer) for value in values]  49.3 us
    ppermute x10, waiting for transfers between devices, across(): return [lax.ppermute(value, 'ctx', inner) for value in values]  27.5 us
    all_gather x1, blocking collectives, local(): g = lax.all_gather(gains, 'fsdp', axis=1, tiled=True)  19.6 us
    unnamed x32, local copies, waits for them, and re-layouts  9 us
    ppermute x10, starting transfers between devices, across(): return [lax.ppermute(value, 'ctx', inner) for value in values]  7.97 us
    ppermute x10, waiting for transfers between devices, beyond(): return [lax.ppermute(value, 'ctx', outer) for value in values]  7.14 us
  transfers between devices with their start and end apart: 20, of which 4 were waited for; matrix products, arithmetic and copies ran while one was open for 0% of the time, Pallas kernels for 31%

profile of v2, /device:TPU:16, one launch (start us, length us, event | category | flops | bytes accessed | tf_op | source)
XLA Modules:
  0.0 178.9 jit_solution(5066781227284428403)
XLA Ops:
  0.6 7.5 %collective-permute-start.3 = (bf16[256,1536]{1,0:T(8,128)(2,1)}, bf16[256,1536]{1,0:T(8,128)(2,1)}, u32[]{:S(2)}, u32[]{:S(2)}) collective-permute-start(bf16[256,1536]{1,0:T(8,128)(2,1)} %bitcast.34), channel_id=1, source_target_pairs={{1,2},{2,1},{3,4},{4,3},{5,6},{6,5},{7,8},{8,7},{9,10},{10,9},{11,... | collective-permute-start | bytes 2359304 | tf_op jit(solution)/shard_map/ppermute | solution.py:462
  8.3 3.9 %collective-permute-start.4 = (bf16[256,1536]{1,0:T(8,128)(2,1)}, bf16[256,1536]{1,0:T(8,128)(2,1)S(1)}, u32[]{:S(2)}, u32[]{:S(2)}) collective-permute-start(bf16[256,1536]{1,0:T(8,128)(2,1)} %bitcast.19), channel_id=1, source_target_pairs={{1,2},{2,1},{3,4},{4,3},{5,6},{6,5},{7,8},{8,7},{9,10},{10,9},{11,... | collective-permute-start | bytes 2359304 | tf_op jit(solution)/shard_map/ppermute | solution.py:462
  12.2 1.3 collective-permute-start.2
  13.5 19.6 %all-gather = f32[16,8,2]{1,2,0:T(2,128)S(1)} all-gather(f32[1,8,2]{1,2,0:T(2,128)} %bitcast.40), channel_id=1, replica_groups=mesh['fsdp'=16,'ctx'=16] {'fsdp'}, dimensions={0}, use_global_device_ids=true | all-gather | bytes 1088 | tf_op jit(solution)/shard_map/all_gather | solution.py:478
  36.6 2.3 %prepare.1 = (bf16[256,1536]{1,0:T(8,128)(2,1)S(1)}, bf16[256,1536]{1,0:T(8,128)(2,1)S(1)}, bf16[256,1536]{1,0:T(8,128)(2,1)}) custom-call(f32[2,128]{1,0:T(2,128)S(1)} %bitcast.27, bf16[256,1536]{1,0:T(8,128)(2,1)S(1)} %bitcast.32, bf16[256,1536]{1,0:T(8,128)(2,1)S(1)} %bitcast.36, bf16[256,1536]{1,0:T(8,128)(2,1)S(1)} %bitcast.15), custom_call_target="tpu_custom_call" | custom-call | flops 20000000000 | bytes 20000000000 | tf_op jit(solution)/shard_map/prepare/pallas_call | solution.py:432
  39.8 1.7 collective-permute-start.7
  42.2 4.6 %collective-permute-start.5 = (bf16[256,1536]{1,0:T(8,128)(2,1)}, bf16[256,1536]{1,0:T(8,128)(2,1)S(1)}, u32[]{:S(2)}, u32[]{:S(2)}) collective-permute-start(bf16[256,1536]{1,0:T(8,128)(2,1)} %collective-permute-done.1.kp), channel_id=1, source_target_pairs={{1,2},{2,1},{3,4},{4,3},{5,6},{6,5},{7,8},{8,7},{9,10},{10,9},{11,... | collective-permute-start | bytes 2359304 | tf_op jit(solution)/shard_map/ppermute | solution.py:462
  46.8 4.8 %collective-permute-start.6 = (bf16[256,1536]{1,0:T(8,128)(2,1)}, bf16[256,1536]{1,0:T(8,128)(2,1)S(1)}, u32[]{:S(2)}, u32[]{:S(2)}) collective-permute-start(bf16[256,1536]{1,0:T(8,128)(2,1)} %collective-permute-done.2.vp), channel_id=1, source_target_pairs={{1,2},{2,1},{3,4},{4,3},{5,6},{6,5},{7,8},{8,7},{9,10},{10,9},{11,... | collective-permute-start | bytes 2359304 | tf_op jit(solution)/shard_map/ppermute | solution.py:462
  53.9 6.9 %own_forward.1 = (f32[1536,256]{1,0:T(8,128)S(1)}, f32[24,256]{1,0:T(8,128)S(1)}, bf16[256,1536]{1,0:T(8,128)(2,1)S(1)}, bf16[256,1536]{1,0:T(8,128)(2,1)S(1)}, ...) custom-call(s32[114]{0:T(128)S(1)} %pad_add_fusion.sc, f32[2,128]{1,0:T(2,128)S(1)} %bitcast.28, ...), custom_call_target="tpu_custom_call" | custom-call | flops 20000000000 | bytes 20000000000 | tf_op jit(solution)/shard_map/own_forward/pallas_call | solution.py:432
  60.8 4.7 %collective-permute-start.10 = (bf16[256,1536]{1,0:T(8,128)(2,1)S(1)}, bf16[256,1536]{1,0:T(8,128)(2,1)S(1)}, u32[]{:S(2)}, u32[]{:S(2)}) collective-permute-start(bf16[256,1536]{1,0:T(8,128)(2,1)S(1)} %get-tuple-element.58), channel_id=1, source_target_pairs={{1,2},{2,1},{3,4},{4,3},{5,6},{6,5},{7,8},{8,7},{9,10},{10,9},{11,... | collective-permute-start | bytes 2359304 | tf_op jit(solution)/shard_map/ppermute | solution.py:462
  65.5 4.8 %collective-permute-start.11 = (bf16[256,1536]{1,0:T(8,128)(2,1)S(1)}, bf16[256,1536]{1,0:T(8,128)(2,1)S(1)}, u32[]{:S(2)}, u32[]{:S(2)}) collective-permute-start(bf16[256,1536]{1,0:T(8,128)(2,1)S(1)} %get-tuple-element.59), channel_id=1, source_target_pairs={{1,2},{2,1},{3,4},{4,3},{5,6},{6,5},{7,8},{8,7},{9,10},{10,9},{11,... | collective-permute-start | bytes 2359304 | tf_op jit(solution)/shard_map/ppermute | solution.py:462
  70.3 7.7 %collective-permute-done.qn.qs.qnp = bf16[256,1536]{1,0:T(8,128)(2,1)S(1)} collective-permute-done((bf16[256,1536]{1,0:T(8,128)(2,1)S(1)}, bf16[256,1536]{1,0:T(8,128)(2,1)S(1)}, u32[]{:S(2)}, u32[]{:S(2)}) %collective-permute-start) | collective-permute-done | bytes 786464 | tf_op jit(solution)/shard_map/ppermute | solution.py:459
  78.0 7.1 %collective-permute-done.6.vf = bf16[256,1536]{1,0:T(8,128)(2,1)S(1)} collective-permute-done((bf16[256,1536]{1,0:T(8,128)(2,1)}, bf16[256,1536]{1,0:T(8,128)(2,1)S(1)}, u32[]{:S(2)}, u32[]{:S(2)}) %collective-permute-start.6) | collective-permute-done | bytes 786464 | tf_op jit(solution)/shard_map/ppermute | solution.py:462
  85.2 4.6 %partner_forward.1 = (bf16[1536,256]{1,0:T(8,128)(2,1)S(1)}, f32[36,256]{1,0:T(8,128)S(1)}, bf16[256,1536]{1,0:T(8,128)(2,1)S(1)}) custom-call(s32[114]{0:T(128)S(1)} %pad_add_fusion.sc, f32[2,128]{1,0:T(2,128)S(1)} %bitcast.29, bf16[256,1536]{1,0:T(8,128)(2,1)S(1)} %collective-permute-done.qn.qs.qnp, bf16[256,1536]{1,0:T(8,128)(2,1)S(1)} %get-tuple-element.45.kne, ...), custom_call_target="tpu_custom_call" | custom-call | tf_op jit(solution)/shard_map/partner_forward/pallas_call | solution.py:432
  89.7 3.0 %own_forward_far.1 = (f32[1536,256]{1,0:T(8,128)S(1)}, f32[72,256]{1,0:T(8,128)S(1)}) custom-call(s32[114]{0:T(128)S(1)} %pad_add_fusion.sc, bf16[256,1536]{1,0:T(8,128)(2,1)S(1)} %get-tuple-element.43.qn, bf16[256,1536]{1,0:T(8,128)(2,1)S(1)} %get-tuple-element.47.knf, bf16[256,1536]{1,0:T(8,128)(2,1)S(1)} %collective-permute-done.6.vf, ...), custom_call_target="tpu_custom_call" | custom-call | tf_op jit(solution)/shard_map/own_forward_far/pallas_call | solution.py:432
  92.8 4.3 %collective-permute-done.8.got = f32[72,256]{1,0:T(8,128)S(1)} collective-permute-done((f32[72,256]{1,0:T(8,128)S(1)}, f32[72,256]{1,0:T(8,128)S(1)}, u32[]{:S(2)}, u32[]{:S(2)}) %collective-permute-start.8) | collective-permute-done | bytes 73760 | tf_op jit(solution)/shard_map/ppermute | solution.py:459
  97.3 4.6 %collective-permute-start.12 = (f32[48,256]{1,0:T(8,128)S(1)}, f32[48,256]{1,0:T(8,128)S(1)}, u32[]{:S(2)}, u32[]{:S(2)}) collective-permute-start(f32[48,256]{1,0:T(8,128)S(1)} %get-tuple-element.56.st), channel_id=1, source_target_pairs={{1,2},{2,1},{3,4},{4,3},{5,6},{6,5},{7,8},{8,7},{9,10},{10,9},{11,... | collective-permute-start | bytes 147464 | tf_op jit(solution)/shard_map/ppermute | solution.py:462
  102.1 4.0 %partner_query_grads.1 = (bf16[1536,256]{1,0:T(8,128)(2,1)S(1)}, bf16[512,512]{1,0:T(8,128)(2,1)S(1)}) custom-call(s32[114]{0:T(128)S(1)} %pad_add_fusion.sc, bf16[256,1536]{1,0:T(8,128)(2,1)S(1)} %collective-permute-done.qn.qs.qnp, bf16[256,1536]{1,0:T(8,128)(2,1)S(1)} %collective-permute-done.7.do.ds.dop, f32[48,256]{1,0:T(8,128)S(1)} %get-tuple-element.56.st, ...), custom_call_target="tpu_custom_call" | custom-call | tf_op jit(solution)/shard_map/partner_query_grads/pallas_call | solution.py:432
  106.1 2.3 %collective-permute-start.13 = (bf16[1536,256]{1,0:T(8,128)(2,1)S(1)}, bf16[1536,256]{1,0:T(8,128)(2,1)S(1)}, u32[]{:S(2)}, u32[]{:S(2)}) collective-permute-start(bf16[1536,256]{1,0:T(8,128)(2,1)S(1)} %get-tuple-element.60._), channel_id=1, source_target_pairs={{0,1},{1,0},{2,3},{3,2},{4,5},{5,4},{6,7},{7,6},{8,9},{9,8},{10,11... | collective-permute-start | bytes 2359304 | tf_op jit(solution)/shard_map/ppermute | solution.py:459
  108.4 7.9 %own_query_grads.1 = (f32[1536,256]{1,0:T(8,128)S(1)}, f32[256,1536]{1,0:T(8,128)S(1)}, f32[256,1536]{1,0:T(8,128)S(1)}, bf16[512,512]{1,0:T(8,128)(2,1)S(1)}) custom-call(s32[114]{0:T(128)S(1)} %pad_add_fusion.sc, bf16[256,1536]{1,0:T(8,128)(2,1)S(1)} %get-tuple-element.43.qn, bf16[256,1536]{1,0:T(8,128)(2,1)S(1)} %bitcast.18, ...), custom_call_target="tpu_custom_call" | custom-call | tf_op jit(solution)/shard_map/own_query_grads/pallas_call | solution.py:432
  116.3 4.8 %collective-permute-start.14 = (bf16[512,512]{1,0:T(8,128)(2,1)S(1)}, bf16[512,512]{1,0:T(8,128)(2,1)S(1)}, u32[]{:S(2)}, u32[]{:S(2)}) collective-permute-start(bf16[512,512]{1,0:T(8,128)(2,1)S(1)} %get-tuple-element.65), channel_id=1, source_target_pairs={{1,2},{2,1},{3,4},{4,3},{5,6},{6,5},{7,8},{8,7},{9,10},{10,9},{11,... | collective-permute-start | bytes 1572872 | tf_op jit(solution)/shard_map/ppermute | solution.py:462
  121.1 4.6 %collective-permute-start.16 = (bf16[512,512]{1,0:T(8,128)(2,1)S(1)}, bf16[512,512]{1,0:T(8,128)(2,1)S(1)}, u32[]{:S(2)}, u32[]{:S(2)}) collective-permute-start(bf16[512,512]{1,0:T(8,128)(2,1)S(1)} %get-tuple-element.72), channel_id=1, source_target_pairs={{1,2},{2,1},{3,4},{4,3},{5,6},{6,5},{7,8},{8,7},{9,10},{10,9},{11,... | collective-permute-start | bytes 1572872 | tf_op jit(solution)/shard_map/ppermute | solution.py:462
  125.8 7.9 %near_key_grads.1 = (f32[256,1536]{1,0:T(8,128)S(1)}, f32[256,1536]{1,0:T(8,128)S(1)}, f32[256,1536]{1,0:T(8,128)S(1)}, f32[256,1536]{1,0:T(8,128)S(1)}, bf16[512,512]{1,0:T(8,128)(2,1)S(1)}) custom-call(s32[114]{0:T(128)S(1)} %pad_add_fusion.sc, bf16[256,1536]{1,0:T(8,128)(2,1)S(1)} %copy-done.6, bf16[256,1536]{1,0:T(8,128)(2,1)S(1)} %bitcast.23, ...), custom_call_target="tpu_custom_call" | custom-call | flops 20000000000 | bytes 20000000000 | tf_op jit(solution)/shard_map/near_key_grads/pallas_call | solution.py:432
  133.7 4.8 %collective-permute-start.18 = (bf16[512,512]{1,0:T(8,128)(2,1)S(1)}, bf16[512,512]{1,0:T(8,128)(2,1)S(1)}, u32[]{:S(2)}, u32[]{:S(2)}) collective-permute-start(bf16[512,512]{1,0:T(8,128)(2,1)S(1)} %get-tuple-element.76), channel_id=1, source_target_pairs={{1,2},{2,1},{3,4},{4,3},{5,6},{6,5},{7,8},{8,7},{9,10},{10,9},{11,... | collective-permute-start | bytes 1572872 | tf_op jit(solution)/shard_map/ppermute | solution.py:462
  138.5 1.7 merge.1._
  141.4 3.3 %partner_far_grads.3 = (bf16[512,512]{1,0:T(8,128)(2,1)S(1)}, f32[256,512]{1,0:T(8,128)}, f32[256,512]{1,0:T(8,128)}) custom-call(s32[114]{0:T(128)S(1)} %pad_add_fusion.sc, bf16[256,1536]{1,0:T(8,128)(2,1)S(1)} %get-tuple-element.57.knp, bf16[256,1536]{1,0:T(8,128)(2,1)} %collective-permute-done.2.vp, bf16[512,512]{1,0:T(8,128)(2,1)S(1)} %collective-permute-done.14.both, ...), custom_call_target="tpu_custom_call" | custom-call | flops 20000000000 | bytes 20000000000 | tf_op jit(solution)/shard_map/partner_far_grads/pallas_call | solution.py:432
  145.9 2.5 %finish_queries.1._ = bf16[256,1536]{1,0:T(8,128)(2,1)} custom-call(f32[2,128]{1,0:T(2,128)S(1)} %bitcast.30, f32[1536,256]{1,0:T(8,128)S(1)} %get-tuple-element.63._.dqt, bf16[1536,256]{1,0:T(8,128)(2,1)S(1)} %collective-permute-done.13.dqr, bf16[256,1536]{1,0:T(8,128)(2,1)S(1)} %bitcast.33, f32[256,512]{1,0:T(8,128)S(1)} %get-tuple-element.70._.refs_0_), custom_call_target="tpu_custom_call" | custom-call | flops 20000000000 | bytes 20000000000 | tf_op jit(solution)/shard_map/finish_queries/pallas_call | solution.py:432
  149.6 3.3 %partner_far_grads.4 = (bf16[512,512]{1,0:T(8,128)(2,1)S(1)}, f32[256,512]{1,0:T(8,128)}, f32[256,512]{1,0:T(8,128)}) custom-call(s32[114]{0:T(128)S(1)} %pad_add_fusion.sc, bf16[256,1536]{1,0:T(8,128)(2,1)S(1)} %get-tuple-element.57.knp, bf16[256,1536]{1,0:T(8,128)(2,1)} %collective-permute-done.2.vp, bf16[512,512]{1,0:T(8,128)(2,1)S(1)} %collective-permute-done.16.both, ...), custom_call_target="tpu_custom_call" | custom-call | flops 20000000000 | bytes 20000000000 | tf_op jit(solution)/shard_map/partner_far_grads/pallas_call | solution.py:432
  152.9 2.0 %collective-permute-start.17 = (bf16[512,512]{1,0:T(8,128)(2,1)S(1)}, bf16[512,512]{1,0:T(8,128)(2,1)S(1)}, u32[]{:S(2)}, u32[]{:S(2)}) collective-permute-start(bf16[512,512]{1,0:T(8,128)(2,1)S(1)} %get-tuple-element.73._), channel_id=1, source_target_pairs={{0,1},{1,0},{2,3},{3,2},{4,5},{5,4},{6,7},{7,6},{8,9},{9,8},{10,11... | collective-permute-start | bytes 1572872 | tf_op jit(solution)/shard_map/ppermute | solution.py:459
  156.2 3.3 %partner_far_grads.5 = (bf16[512,512]{1,0:T(8,128)(2,1)S(1)}, f32[256,512]{1,0:T(8,128)}, f32[256,512]{1,0:T(8,128)}) custom-call(s32[114]{0:T(128)S(1)} %pad_add_fusion.sc, bf16[256,1536]{1,0:T(8,128)(2,1)S(1)} %get-tuple-element.57.knp, bf16[256,1536]{1,0:T(8,128)(2,1)} %collective-permute-done.2.vp, bf16[512,512]{1,0:T(8,128)(2,1)S(1)} %collective-permute-done.18.both, ...), custom_call_target="tpu_custom_call" | custom-call | flops 20000000000 | bytes 20000000000 | tf_op jit(solution)/shard_map/partner_far_grads/pallas_call | solution.py:432
  160.8 15.5 %collective-permute-done.19.refs_8_ = bf16[512,512]{1,0:T(8,128)(2,1)S(1)} collective-permute-done((bf16[512,512]{1,0:T(8,128)(2,1)S(1)}, bf16[512,512]{1,0:T(8,128)(2,1)S(1)}, u32[]{:S(2)}, u32[]{:S(2)}) %collective-permute-start.19) | collective-permute-done | bytes 524320 | tf_op jit(solution)/shard_map/ppermute | solution.py:459
  176.3 2.6 %finish_keys.1 = (bf16[256,1536]{1,0:T(8,128)(2,1)}, bf16[256,1536]{1,0:T(8,128)(2,1)}) custom-call(f32[2,128]{1,0:T(2,128)S(1)} %bitcast.31, bf16[256,1536]{1,0:T(8,128)(2,1)S(1)} %bitcast.37, f32[256,512]{1,0:T(8,128)S(1)} %get-tuple-element.70._.refs_0_, f32[256,512]{1,0:T(8,128)S(1)} %get-tuple-element.71.refs_1_, ...), custom_call_target="tpu_custom_call" | custom-call | flops 20000000000 | bytes 20000000000 | tf_op jit(solution)/shard_map/finish_keys/pallas_call | solution.py:432
  (61 shorter events, 13.9 us)
Async XLA Ops:
  0.6 41.1 %collective-permute-start.3 = (bf16[256,1536]{1,0:T(8,128)(2,1)}, bf16[256,1536]{1,0:T(8,128)(2,1)}, u32[]{:S(2)}, u32[]{:S(2)}) collective-permute-start(bf16[256,1536]{1,0:T(8,128)(2,1)} %bitcast.34), channel_id=1, source_target_pairs={{1,2},{2,1},{3,4},{4,3},{5,6},{6,5},{7,8},{8,7},{9,10},{10,9},{11,... | collective-permute-start | bytes 2359304 | tf_op jit(solution)/shard_map/ppermute | solution.py:462
  8.2 34.0 %collective-permute-start.1 = (bf16[256,1536]{1,0:T(8,128)(2,1)}, bf16[256,1536]{1,0:T(8,128)(2,1)}, u32[]{:S(2)}, u32[]{:S(2)}) collective-permute-start(bf16[256,1536]{1,0:T(8,128)(2,1)} %bitcast.35), channel_id=1, source_target_pairs={{0,1},{1,0},{2,3},{3,2},{4,5},{5,4},{6,7},{7,6},{8,9},{9,8},{10,11... | collective-permute-start | bytes 2359304 | tf_op jit(solution)/shard_map/ppermute | solution.py:459
  8.3 43.3 %collective-permute-start.4 = (bf16[256,1536]{1,0:T(8,128)(2,1)}, bf16[256,1536]{1,0:T(8,128)(2,1)S(1)}, u32[]{:S(2)}, u32[]{:S(2)}) collective-permute-start(bf16[256,1536]{1,0:T(8,128)(2,1)} %bitcast.19), channel_id=1, source_target_pairs={{1,2},{2,1},{3,4},{4,3},{5,6},{6,5},{7,8},{8,7},{9,10},{10,9},{11,... | collective-permute-start | bytes 2359304 | tf_op jit(solution)/shard_map/ppermute | solution.py:462
  12.2 34.6 %collective-permute-start.2 = (bf16[256,1536]{1,0:T(8,128)(2,1)}, bf16[256,1536]{1,0:T(8,128)(2,1)}, u32[]{:S(2)}, u32[]{:S(2)}) collective-permute-start(bf16[256,1536]{1,0:T(8,128)(2,1)} %bitcast.20), channel_id=1, source_target_pairs={{0,1},{1,0},{2,3},{3,2},{4,5},{5,4},{6,7},{7,6},{8,9},{9,8},{10,11... | collective-permute-start | bytes 2359304 | tf_op jit(solution)/shard_map/ppermute | solution.py:459
  33.2 1.1 copy-start
  34.4 1.1 copy-start.7
  36.6 4.9 %copy-start.13 = (s32[16,6]{0,1:T(8,128)S(1)}, s32[16,6]{0,1:T(8,128)}, u32[]{:S(2)}) copy-start(s32[16,6]{0,1:T(8,128)} %param.13) | copy-start | bytes 1156
  36.6 5.0 %copy-start.14 = (s32[16]{0:T(128)S(1)}, s32[16]{0:T(128)}, u32[]{:S(2)}) copy-start(s32[16]{0:T(128)} %param.12) | copy-start | bytes 196
  36.6 15.0 %copy-start.1 = (bf16[1,256,1536]{2,1,0:T(8,128)(2,1)S(1)}, bf16[1,256,1536]{2,1,0:T(8,128)(2,1)}, u32[]{:S(2)}) copy-start(bf16[1,256,1536]{2,1,0:T(8,128)(2,1)} %param.10) | copy-start | bytes 2359300
  39.8 25.7 %collective-permute-start.7 = (bf16[256,1536]{1,0:T(8,128)(2,1)}, bf16[256,1536]{1,0:T(8,128)(2,1)S(1)}, u32[]{:S(2)}, u32[]{:S(2)}) collective-permute-start(bf16[256,1536]{1,0:T(8,128)(2,1)} %get-tuple-element.46), channel_id=1, source_target_pairs={{0,1},{1,0},{2,3},{3,2},{4,5},{5,4},{6,7},{7,6},{8,9},{9,8},{10,11... | collective-permute-start | bytes 2359304 | tf_op jit(solution)/shard_map/ppermute | solution.py:459
  41.8 36.3 %collective-permute-start = (bf16[256,1536]{1,0:T(8,128)(2,1)S(1)}, bf16[256,1536]{1,0:T(8,128)(2,1)S(1)}, u32[]{:S(2)}, u32[]{:S(2)}) collective-permute-start(bf16[256,1536]{1,0:T(8,128)(2,1)S(1)} %get-tuple-element.43.qn), channel_id=1, source_target_pairs={{0,1},{1,0},{2,3},{3,2},{4,5},{5,4},{6,7},{7,6},{8,9},{9,8},{10,11... | collective-permute-start | bytes 2359304 | tf_op jit(solution)/shard_map/ppermute | solution.py:459
  42.2 35.9 %collective-permute-start.5 = (bf16[256,1536]{1,0:T(8,128)(2,1)}, bf16[256,1536]{1,0:T(8,128)(2,1)S(1)}, u32[]{:S(2)}, u32[]{:S(2)}) collective-permute-start(bf16[256,1536]{1,0:T(8,128)(2,1)} %collective-permute-done.1.kp), channel_id=1, source_target_pairs={{1,2},{2,1},{3,4},{4,3},{5,6},{6,5},{7,8},{8,7},{9,10},{10,9},{11,... | collective-permute-start | bytes 2359304 | tf_op jit(solution)/shard_map/ppermute | solution.py:462
  46.8 38.3 %collective-permute-start.6 = (bf16[256,1536]{1,0:T(8,128)(2,1)}, bf16[256,1536]{1,0:T(8,128)(2,1)S(1)}, u32[]{:S(2)}, u32[]{:S(2)}) collective-permute-start(bf16[256,1536]{1,0:T(8,128)(2,1)} %collective-permute-done.2.vp), channel_id=1, source_target_pairs={{1,2},{2,1},{3,4},{4,3},{5,6},{6,5},{7,8},{8,7},{9,10},{10,9},{11,... | collective-permute-start | bytes 2359304 | tf_op jit(solution)/shard_map/ppermute | solution.py:462
  51.6 1.1 copy-start.2
  60.8 55.4 %collective-permute-start.10 = (bf16[256,1536]{1,0:T(8,128)(2,1)S(1)}, bf16[256,1536]{1,0:T(8,128)(2,1)S(1)}, u32[]{:S(2)}, u32[]{:S(2)}) collective-permute-start(bf16[256,1536]{1,0:T(8,128)(2,1)S(1)} %get-tuple-element.58), channel_id=1, source_target_pairs={{1,2},{2,1},{3,4},{4,3},{5,6},{6,5},{7,8},{8,7},{9,10},{10,9},{11,... | collective-permute-start | bytes 2359304 | tf_op jit(solution)/shard_map/ppermute | solution.py:462
  65.5 55.6 %collective-permute-start.11 = (bf16[256,1536]{1,0:T(8,128)(2,1)S(1)}, bf16[256,1536]{1,0:T(8,128)(2,1)S(1)}, u32[]{:S(2)}, u32[]{:S(2)}) collective-permute-start(bf16[256,1536]{1,0:T(8,128)(2,1)S(1)} %get-tuple-element.59), channel_id=1, source_target_pairs={{1,2},{2,1},{3,4},{4,3},{5,6},{6,5},{7,8},{8,7},{9,10},{10,9},{11,... | collective-permute-start | bytes 2359304 | tf_op jit(solution)/shard_map/ppermute | solution.py:462
  92.7 4.4 %collective-permute-start.8 = (f32[72,256]{1,0:T(8,128)S(1)}, f32[72,256]{1,0:T(8,128)S(1)}, u32[]{:S(2)}, u32[]{:S(2)}) collective-permute-start(f32[72,256]{1,0:T(8,128)S(1)} %get-tuple-element.52.mine), channel_id=1, source_target_pairs={{0,1},{1,0},{2,3},{3,2},{4,5},{5,4},{6,7},{7,6},{8,9},{9,8},{10,11... | collective-permute-start | bytes 221192 | tf_op jit(solution)/shard_map/ppermute | solution.py:459
  97.3 28.4 %collective-permute-start.12 = (f32[48,256]{1,0:T(8,128)S(1)}, f32[48,256]{1,0:T(8,128)S(1)}, u32[]{:S(2)}, u32[]{:S(2)}) collective-permute-start(f32[48,256]{1,0:T(8,128)S(1)} %get-tuple-element.56.st), channel_id=1, source_target_pairs={{1,2},{2,1},{3,4},{4,3},{5,6},{6,5},{7,8},{8,7},{9,10},{10,9},{11,... | collective-permute-start | bytes 147464 | tf_op jit(solution)/shard_map/ppermute | solution.py:462
  102.0 6.4 %copy-start.3 = (bf16[1,256,1536]{2,1,0:T(8,128)(2,1)S(1)}, bf16[1,256,1536]{2,1,0:T(8,128)(2,1)}, u32[]{:S(2)}) copy-start(bf16[1,256,1536]{2,1,0:T(8,128)(2,1)} %param.9) | copy-start | bytes 2359300
  102.0 6.4 %copy-start.6 = (bf16[256,1536]{1,0:T(8,128)(2,1)S(1)}, bf16[256,1536]{1,0:T(8,128)(2,1)}, u32[]{:S(2)}) copy-start(bf16[256,1536]{1,0:T(8,128)(2,1)} %copy-done.4) | copy-start | bytes 2359300
  102.0 36.6 %collective-permute-start.9 = (bf16[1536,256]{1,0:T(8,128)(2,1)S(1)}, bf16[1536,256]{1,0:T(8,128)(2,1)S(1)}, u32[]{:S(2)}, u32[]{:S(2)}) collective-permute-start(bf16[1536,256]{1,0:T(8,128)(2,1)S(1)} %get-tuple-element.55), channel_id=1, source_target_pairs={{0,1},{1,0},{2,3},{3,2},{4,5},{5,4},{6,7},{7,6},{8,9},{9,8},{10,11... | collective-permute-start | bytes 2359304 | tf_op jit(solution)/shard_map/ppermute | solution.py:459
  106.1 39.8 %collective-permute-start.13 = (bf16[1536,256]{1,0:T(8,128)(2,1)S(1)}, bf16[1536,256]{1,0:T(8,128)(2,1)S(1)}, u32[]{:S(2)}, u32[]{:S(2)}) collective-permute-start(bf16[1536,256]{1,0:T(8,128)(2,1)S(1)} %get-tuple-element.60._), channel_id=1, source_target_pairs={{0,1},{1,0},{2,3},{3,2},{4,5},{5,4},{6,7},{7,6},{8,9},{9,8},{10,11... | collective-permute-start | bytes 2359304 | tf_op jit(solution)/shard_map/ppermute | solution.py:459
  116.3 24.0 %collective-permute-start.14 = (bf16[512,512]{1,0:T(8,128)(2,1)S(1)}, bf16[512,512]{1,0:T(8,128)(2,1)S(1)}, u32[]{:S(2)}, u32[]{:S(2)}) collective-permute-start(bf16[512,512]{1,0:T(8,128)(2,1)S(1)} %get-tuple-element.65), channel_id=1, source_target_pairs={{1,2},{2,1},{3,4},{4,3},{5,6},{6,5},{7,8},{8,7},{9,10},{10,9},{11,... | collective-permute-start | bytes 1572872 | tf_op jit(solution)/shard_map/ppermute | solution.py:462
  121.1 27.3 %collective-permute-start.16 = (bf16[512,512]{1,0:T(8,128)(2,1)S(1)}, bf16[512,512]{1,0:T(8,128)(2,1)S(1)}, u32[]{:S(2)}, u32[]{:S(2)}) collective-permute-start(bf16[512,512]{1,0:T(8,128)(2,1)S(1)} %get-tuple-element.72), channel_id=1, source_target_pairs={{1,2},{2,1},{3,4},{4,3},{5,6},{6,5},{7,8},{8,7},{9,10},{10,9},{11,... | collective-permute-start | bytes 1572872 | tf_op jit(solution)/shard_map/ppermute | solution.py:462
  133.7 22.5 %collective-permute-start.18 = (bf16[512,512]{1,0:T(8,128)(2,1)S(1)}, bf16[512,512]{1,0:T(8,128)(2,1)S(1)}, u32[]{:S(2)}, u32[]{:S(2)}) collective-permute-start(bf16[512,512]{1,0:T(8,128)(2,1)S(1)} %get-tuple-element.76), channel_id=1, source_target_pairs={{1,2},{2,1},{3,4},{4,3},{5,6},{6,5},{7,8},{8,7},{9,10},{10,9},{11,... | collective-permute-start | bytes 1572872 | tf_op jit(solution)/shard_map/ppermute | solution.py:462
  140.3 1.1 copy-start.11
  144.6 16.2 %collective-permute-start.15 = (bf16[512,512]{1,0:T(8,128)(2,1)S(1)}, bf16[512,512]{1,0:T(8,128)(2,1)S(1)}, u32[]{:S(2)}, u32[]{:S(2)}) collective-permute-start(bf16[512,512]{1,0:T(8,128)(2,1)S(1)} %get-tuple-element.69._), channel_id=1, source_target_pairs={{0,1},{1,0},{2,3},{3,2},{4,5},{5,4},{6,7},{7,6},{8,9},{9,8},{10,11... | collective-permute-start | bytes 1572872 | tf_op jit(solution)/shard_map/ppermute | solution.py:459
  144.6 1.3 copy-start.8
  148.5 1.1 copy-start.12
  152.9 23.4 %collective-permute-start.17 = (bf16[512,512]{1,0:T(8,128)(2,1)S(1)}, bf16[512,512]{1,0:T(8,128)(2,1)S(1)}, u32[]{:S(2)}, u32[]{:S(2)}) collective-permute-start(bf16[512,512]{1,0:T(8,128)(2,1)S(1)} %get-tuple-element.73._), channel_id=1, source_target_pairs={{0,1},{1,0},{2,3},{3,2},{4,5},{5,4},{6,7},{7,6},{8,9},{9,8},{10,11... | collective-permute-start | bytes 1572872 | tf_op jit(solution)/shard_map/ppermute | solution.py:459
  159.5 16.8 %copy-start.10 = (bf16[1,256,1536]{2,1,0:T(8,128)(2,1)S(1)}, bf16[1,256,1536]{2,1,0:T(8,128)(2,1)}, u32[]{:S(2)}) copy-start(bf16[1,256,1536]{2,1,0:T(8,128)(2,1)} %param.8) | copy-start | bytes 2359300
  159.5 16.8 %collective-permute-start.19 = (bf16[512,512]{1,0:T(8,128)(2,1)S(1)}, bf16[512,512]{1,0:T(8,128)(2,1)S(1)}, u32[]{:S(2)}, u32[]{:S(2)}) collective-permute-start(bf16[512,512]{1,0:T(8,128)(2,1)S(1)} %get-tuple-element.77._), channel_id=1, source_target_pairs={{0,1},{1,0},{2,3},{3,2},{4,5},{5,4},{6,7},{7,6},{8,9},{9,8},{10,11... | collective-permute-start | bytes 1572872 | tf_op jit(solution)/shard_map/ppermute | solution.py:459
  (3 other events, 3.1 us)

commit v3 on v2

--- a/solution.py
+++ b/solution.py
@@ -330,51 +330,51 @@
     dq_ref[...] = acc_ref[...].astype(BF)
 
 
-def near_key_grads(
-    sc, knx, v, qnp, dop, st, knp, vp, qne, doe, ste, dk0, dv0, qs, ds, _,
-    dkx, dvx, dkp, dvp, both_out,
+def partner_near_grads(
+    sc, knp, vp, qne, doe, ste, qs, ds, _, dk_ref, dv_ref, both_out, dk, dv
 ):
     me, partner, near, far = around(sc)
     stack(both_out, qs, ds)
-    dkx[...] = dk0[...]
-    dvx[...] = dv0[...]
-    clear(dkp, dvp)
-    own = partial(key_use, qnp, dop, dkx, dvx)
-    use = partial(key_use, qne, doe, dkx, dvx)
-    back = partial(key_use, qne, doe, dkp, dvp)
+    clear(dk, dv)
+    back = partial(key_use, qne, doe, dk, dv)
+    emit(backward_units(allowed(sc, near, partner), knp, vp, qne, doe, ste, back))
+    dk_ref[...] = dk[...].astype(BF)
+    dv_ref[...] = dv[...].astype(BF)
+
+
+def partner_far_grads(chunk, heads, sc, knp, vp, both, st, dk0, dv0, _, out, dk, dv):
+    me, partner, near, far = around(sc)
+    dk[...] = dk0[...].astype(F32)
+    dv[...] = dv0[...].astype(F32)
+    qn, do = both.at[pl.ds(0, ROWS)], both.at[pl.ds(ROWS, ROWS)]
+    use = partial(key_use, qn, do, dk, dv)
+    emit(
+        backward_units(
+            allowed(sc, far, partner), knp, vp, qn, do, st, use, 1, chunk * HB, heads
+        )
+    )
+    out[:ROWS] = dk[...].astype(BF)
+    out[ROWS:] = dv[...].astype(BF)
+
+
+def own_key_grads(sc, knx, v, qnp, dop, st, qne, doe, ste, dk0, dv0, *refs):
+    dk, dv = refs[-2:]
+    chunks = refs[:-3]
+    me, partner, near, far = around(sc)
+    dk[...] = dk0[...]
+    dv[...] = dv0[...]
+    own = partial(key_use, qnp, dop, dk, dv)
+    use = partial(key_use, qne, doe, dk, dv)
     emit(
         backward_units(allowed(sc, partner, me), knx, v, qnp, dop, st, own, 1)
         + backward_units(allowed(sc, near, me), knx, v, qne, doe, ste, use)
-        + backward_units(allowed(sc, near, partner), knp, vp, qne, doe, ste, back)
-    )
-
-
-def partner_far_grads(chunk, heads, sc, knp, vp, both, st, dk0, dv0, _, out, dk, dv):
-    me, partner, near, far = around(sc)
-    dk[...] = dk0[...]
-    dv[...] = dv0[...]
-    qn, do = both.at[pl.ds(0, ROWS)], both.at[pl.ds(ROWS, ROWS)]
-    emit(
-        backward_units(
-            allowed(sc, far, partner), knp, vp, qn, do, st, partial(key_use, qn, do, dk, dv),
-            1, chunk * HB, heads,
-        )
-    )
-    out[:ROWS] = dk[...].astype(BF)
-    out[ROWS:] = dv[...].astype(BF)
-
-
-def own_far_grads(chunk, heads, sc, knx, v, both, st, dk0, dv0, _, dk, dv):
-    me, partner, near, far = around(sc)
-    dk[...] = dk0[...]
-    dv[...] = dv0[...]
-    qn, do = both.at[pl.ds(0, ROWS)], both.at[pl.ds(ROWS, ROWS)]
-    emit(
-        backward_units(
-            allowed(sc, far, me), knx, v, qn, do, st, partial(key_use, qn, do, dk, dv),
-            1, chunk * HB, heads,
-        )
-    )
+    )
+    for chunk, both in enumerate(chunks):
+        @pl.when(pl.program_id(0) == chunk)
+        def _(both=both):
+            qn, do = both.at[pl.ds(0, ROWS)], both.at[pl.ds(ROWS, ROWS)]
+            last = partial(key_use, qn, do, dk, dv)
+            emit(backward_units(allowed(sc, far, me), knx, v, qn, do, ste, last, 1))
 
 
 def finish_queries(g, dqt, dqr, q, _, dq_out):
@@ -385,14 +385,12 @@
         dq_out[:, c] = denormed(q[:, c], g[0:1, :], dq)
 
 
-def finish_keys(g, k, *refs):
+def finish_keys(g, k, dk, dv, *refs):
     dk_out, dv_out = refs[-2:]
     scale = 1.0 / math.sqrt(HD)
-    for chunk in range((len(refs) - 2) // 3):
-        dk, dv, back = refs[3 * chunk : 3 * chunk + 3]
-
+    for chunk, back in enumerate(refs[:-2]):
         @pl.when(pl.program_id(0) == chunk)
-        def _(dk=dk, dv=dv, back=back):
+        def _(back=back):
             for j in range(HB):
                 c = cols(j)
                 total = (dk[:, c] + back[:ROWS, c].astype(F32)) * scale
@@ -481,7 +479,6 @@
     gain = [(FULL, g)]
     chunks = features // (HB * HD)
     pair = (FULL, (2 * ROWS, HB * HD), BF)
-    part_f = (FULL, (ROWS, HB * HD), F32)
 
     qn, knx, do2 = run(prepare, (), gain + wide(q, k, do), [wide_bf] * 3)
     kf, vf = beyond(kp, vp)
@@ -525,41 +522,36 @@
         + [(ORDER, dqp)],
         [tall_f, wide_f, wide_f, pair],
     )
-    dk, dv, dkp, dvp, sent2 = run(
-        near_key_grads, scalars,
-        wide(knx, v, qnp, dop) + [(FULL, st)] + wide(knp, vp, qne, doe) + [(FULL, ste)]
-        + wide(dk, dv) + send(2) + [(ORDER, dqt)],
-        [wide_f] * 4 + [pair],
+    dkp, dvp, sent2 = run(
+        partner_near_grads, scalars,
+        wide(knp, vp, qne, doe) + [(FULL, ste)] + send(2) + [(ORDER, dqt)],
+        [wide_bf, wide_bf, pair], (acc_w, acc_w),
     )
     far = beyond(sent0, sent1, sent2)
     (att,) = run(
         merge, (), [(TALL, acc), (FULL, shares), (TALL, o_ret), (ORDER, dkp)], [wide_bf], (), chunks,
     )
-    last, back, own = att, [], []
+    last, back = att, []
     for i in range(chunks):
-        out, _, _ = run(
+        (last,) = run(
             partial(partner_far_grads, i, heads), scalars,
             [(i, knp), (i, vp), (FULL, far[i]), (FULL, ste), (i, dkp), (i, dvp), (ORDER, last)],
-            [pair, part_f, part_f], (), 1, "partner_far_grads",
+            [pair], (acc_w, acc_w), 1, "partner_far_grads",
         )
-        back += across(out)
-        dki, dvi = run(
-            partial(own_far_grads, i, heads), scalars,
-            [(i, knx), (i, v), (FULL, far[i]), (FULL, ste), (i, dk), (i, dv), (ORDER, out)],
-            [part_f, part_f], (), 1, "own_far_grads",
-        )
-        own.append((dki, dvi))
-        last = dki
-        if i == 0:
-            (dq_out,) = run(
-                finish_queries, (),
-                gain + [(TALL, dqt), (TALL, dqr)] + wide(q) + [(ORDER, last)], [wide_bf],
-            )
-            last = dq_out
-    pieces = []
-    for i in range(chunks):
-        pieces += [(FULL, own[i][0]), (FULL, own[i][1]), (FULL, back[i])]
-    dk_out, dv_out = run(finish_keys, (), gain + wide(k) + pieces, [wide_bf] * 2)
+        back += across(last)
+    dk, dv = run(
+        own_key_grads, scalars,
+        wide(knx, v, qnp, dop) + [(FULL, st)] + wide(qne, doe) + [(FULL, ste)]
+        + wide(dk, dv) + [(FULL, part) for part in far] + [(ORDER, last)],
+        [wide_f, wide_f],
+    )
+    (dq_out,) = run(
+        finish_queries, (), gain + [(TALL, dqt), (TALL, dqr)] + wide(q) + [(ORDER, dk)],
+        [wide_bf],
+    )
+    dk_out, dv_out = run(
+        finish_keys, (), gain + wide(k, dk, dv) + [(FULL, part) for part in back], [wide_bf] * 2
+    )
     return att[None], dq_out[None], dk_out[None], dv_out[None]
 
 

time: 180 us -> 176 us (0.978)
  Pallas kernels: 57.2 us -> 53.2 us
  starting transfers between devices: 57.2 us -> 55.4 us
    ppermute x10, waiting for transfers between devices: 7.14 us -> 20.9 us  [beyond(): return [lax.ppermute(value, 'ctx', outer) for value in values]]
    ppermute x10, waiting for transfers between devices: 27.5 us -> 14.7 us  [across(): return [lax.ppermute(value, 'ctx', inner) for value in values]]
    pallas_call x17 -> x15, Pallas kernels: 57.2 us -> 53.2 us  [run(): pl.pallas_call(body, name=name or body.__name__, grid_spec=grid_spec, out...]
  transfers between devices with their start and end apart: 20 -> 20, of which waited for: 4 -> 7; matrix products, arithmetic and copies ran while one was open for 0% -> 0% of each run, Pallas kernels for 31% -> 29%
where the time goes in v3:
time: 176 us; the launch traced here: 175 us
  starting transfers between devices  55.4 us (31%)
  Pallas kernels  53.2 us (30%)
  waiting for transfers between devices  35.6 us (20%)
  blocking collectives  20.6 us (12%)
  local copies, waits for them, and re-layouts  8.84 us (5%)
    pallas_call x15, Pallas kernels, run(): pl.pallas_call(body, name=name or body.__name__, grid_spec=grid_spec, out...  53.2 us
    ppermute x10, starting transfers between devices, beyond(): return [lax.ppermute(value, 'ctx', outer) for value in values]  48.3 us
    ppermute x10, waiting for transfers between devices, beyond(): return [lax.ppermute(value, 'ctx', outer) for value in values]  20.9 us
    all_gather x1, blocking collectives, local(): g = lax.all_gather(gains, 'fsdp', axis=1, tiled=True)  20.6 us
    ppermute x10, waiting for transfers between devices, across(): return [lax.ppermute(value, 'ctx', inner) for value in values]  14.7 us
    unnamed x32, local copies, waits for them, and re-layouts  8.75 us
    ppermute x10, starting transfers between devices, across(): return [lax.ppermute(value, 'ctx', inner) for value in values]  7.11 us
  transfers between devices with their start and end apart: 20, of which 7 were waited for; matrix products, arithmetic and copies ran while one was open for 0% of the time, Pallas kernels for 29%

profile of v3, /device:TPU:16, one launch (start us, length us, event | category | flops | bytes accessed | tf_op | source)
XLA Modules:
  0.0 174.7 jit_solution(14149459335347024713)
XLA Ops:
  0.6 2.0 %collective-permute-start.2 = (bf16[256,1536]{1,0:T(8,128)(2,1)}, bf16[256,1536]{1,0:T(8,128)(2,1)}, u32[]{:S(2)}, u32[]{:S(2)}) collective-permute-start(bf16[256,1536]{1,0:T(8,128)(2,1)} %bitcast.19), channel_id=1, source_target_pairs={{0,1},{1,0},{2,3},{3,2},{4,5},{5,4},{6,7},{7,6},{8,9},{9,8},{10,11... | collective-permute-start | bytes 2359304 | tf_op jit(solution)/shard_map/ppermute | solution.py:457
  2.6 6.6 %collective-permute-start.4 = (bf16[256,1536]{1,0:T(8,128)(2,1)}, bf16[256,1536]{1,0:T(8,128)(2,1)S(1)}, u32[]{:S(2)}, u32[]{:S(2)}) collective-permute-start(bf16[256,1536]{1,0:T(8,128)(2,1)} %bitcast.20), channel_id=1, source_target_pairs={{1,2},{2,1},{3,4},{4,3},{5,6},{6,5},{7,8},{8,7},{9,10},{10,9},{11,... | collective-permute-start | bytes 2359304 | tf_op jit(solution)/shard_map/ppermute | solution.py:460
  9.4 3.9 %collective-permute-start.3 = (bf16[256,1536]{1,0:T(8,128)(2,1)}, bf16[256,1536]{1,0:T(8,128)(2,1)}, u32[]{:S(2)}, u32[]{:S(2)}) collective-permute-start(bf16[256,1536]{1,0:T(8,128)(2,1)} %bitcast.32), channel_id=1, source_target_pairs={{1,2},{2,1},{3,4},{4,3},{5,6},{6,5},{7,8},{8,7},{9,10},{10,9},{11,... | collective-permute-start | bytes 2359304 | tf_op jit(solution)/shard_map/ppermute | solution.py:460
  13.3 20.6 %all-gather = f32[16,8,2]{1,2,0:T(2,128)S(1)} all-gather(f32[1,8,2]{1,2,0:T(2,128)} %bitcast.36), channel_id=1, replica_groups=mesh['fsdp'=16,'ctx'=16] {'fsdp'}, dimensions={0}, use_global_device_ids=true | all-gather | bytes 1088 | tf_op jit(solution)/shard_map/all_gather | solution.py:476
  41.1 1.7 collective-permute-start.7
  42.9 4.9 %collective-permute-start.6 = (bf16[256,1536]{1,0:T(8,128)(2,1)}, bf16[256,1536]{1,0:T(8,128)(2,1)S(1)}, u32[]{:S(2)}, u32[]{:S(2)}) collective-permute-start(bf16[256,1536]{1,0:T(8,128)(2,1)} %collective-permute-done.2.vp), channel_id=1, source_target_pairs={{1,2},{2,1},{3,4},{4,3},{5,6},{6,5},{7,8},{8,7},{9,10},{10,9},{11,... | collective-permute-start | bytes 2359304 | tf_op jit(solution)/shard_map/ppermute | solution.py:460
  47.8 4.5 %collective-permute-start.5 = (bf16[256,1536]{1,0:T(8,128)(2,1)}, bf16[256,1536]{1,0:T(8,128)(2,1)S(1)}, u32[]{:S(2)}, u32[]{:S(2)}) collective-permute-start(bf16[256,1536]{1,0:T(8,128)(2,1)} %collective-permute-done.1.kp), channel_id=1, source_target_pairs={{1,2},{2,1},{3,4},{4,3},{5,6},{6,5},{7,8},{8,7},{9,10},{10,9},{11,... | collective-permute-start | bytes 2359304 | tf_op jit(solution)/shard_map/ppermute | solution.py:460
  54.6 7.0 %own_forward.1 = (f32[1536,256]{1,0:T(8,128)S(1)}, f32[24,256]{1,0:T(8,128)S(1)}, bf16[256,1536]{1,0:T(8,128)(2,1)S(1)}, bf16[256,1536]{1,0:T(8,128)(2,1)S(1)}, ...) custom-call(s32[114]{0:T(128)S(1)} %pad_add_fusion.sc, f32[2,128]{1,0:T(2,128)S(1)} %bitcast.25, ...), custom_call_target="tpu_custom_call" | custom-call | flops 20000000000 | bytes 20000000000 | tf_op jit(solution)/shard_map/own_forward/pallas_call | solution.py:430
  61.6 5.0 %collective-permute-start.10 = (bf16[256,1536]{1,0:T(8,128)(2,1)S(1)}, bf16[256,1536]{1,0:T(8,128)(2,1)S(1)}, u32[]{:S(2)}, u32[]{:S(2)}) collective-permute-start(bf16[256,1536]{1,0:T(8,128)(2,1)S(1)} %get-tuple-element.48), channel_id=1, source_target_pairs={{1,2},{2,1},{3,4},{4,3},{5,6},{6,5},{7,8},{8,7},{9,10},{10,9},{11,... | collective-permute-start | bytes 2359304 | tf_op jit(solution)/shard_map/ppermute | solution.py:460
  66.6 4.5 %collective-permute-start.11 = (bf16[256,1536]{1,0:T(8,128)(2,1)S(1)}, bf16[256,1536]{1,0:T(8,128)(2,1)S(1)}, u32[]{:S(2)}, u32[]{:S(2)}) collective-permute-start(bf16[256,1536]{1,0:T(8,128)(2,1)S(1)} %get-tuple-element.49), channel_id=1, source_target_pairs={{1,2},{2,1},{3,4},{4,3},{5,6},{6,5},{7,8},{8,7},{9,10},{10,9},{11,... | collective-permute-start | bytes 2359304 | tf_op jit(solution)/shard_map/ppermute | solution.py:460
  71.1 6.1 %collective-permute-done.7.do.ds.dop = bf16[256,1536]{1,0:T(8,128)(2,1)S(1)} collective-permute-done((bf16[256,1536]{1,0:T(8,128)(2,1)}, bf16[256,1536]{1,0:T(8,128)(2,1)S(1)}, u32[]{:S(2)}, u32[]{:S(2)}) %collective-permute-start.7) | collective-permute-done | bytes 786464 | tf_op jit(solution)/shard_map/ppermute | solution.py:457
  77.1 8.7 %collective-permute-done.5.kf = bf16[256,1536]{1,0:T(8,128)(2,1)S(1)} collective-permute-done((bf16[256,1536]{1,0:T(8,128)(2,1)}, bf16[256,1536]{1,0:T(8,128)(2,1)S(1)}, u32[]{:S(2)}, u32[]{:S(2)}) %collective-permute-start.5) | collective-permute-done | bytes 786464 | tf_op jit(solution)/shard_map/ppermute | solution.py:460
  85.9 4.6 %partner_forward.1 = (bf16[1536,256]{1,0:T(8,128)(2,1)S(1)}, f32[36,256]{1,0:T(8,128)S(1)}, bf16[256,1536]{1,0:T(8,128)(2,1)S(1)}) custom-call(s32[114]{0:T(128)S(1)} %pad_add_fusion.sc, f32[2,128]{1,0:T(2,128)S(1)} %bitcast.26, bf16[256,1536]{1,0:T(8,128)(2,1)S(1)} %collective-permute-done.qn.qs.qnp, bf16[256,1536]{1,0:T(8,128)(2,1)S(1)} %get-tuple-element.36.kne, ...), custom_call_target="tpu_custom_call" | custom-call | tf_op jit(solution)/shard_map/partner_forward/pallas_call | solution.py:430
  90.4 3.0 %own_forward_far.1 = (f32[1536,256]{1,0:T(8,128)S(1)}, f32[72,256]{1,0:T(8,128)S(1)}) custom-call(s32[114]{0:T(128)S(1)} %pad_add_fusion.sc, bf16[256,1536]{1,0:T(8,128)(2,1)S(1)} %get-tuple-element.34.qn, bf16[256,1536]{1,0:T(8,128)(2,1)S(1)} %get-tuple-element.38.knf, bf16[256,1536]{1,0:T(8,128)(2,1)S(1)} %collective-permute-done.6.vf, ...), custom_call_target="tpu_custom_call" | custom-call | tf_op jit(solution)/shard_map/own_forward_far/pallas_call | solution.py:430
  93.6 4.3 %collective-permute-done.8.got = f32[72,256]{1,0:T(8,128)S(1)} collective-permute-done((f32[72,256]{1,0:T(8,128)S(1)}, f32[72,256]{1,0:T(8,128)S(1)}, u32[]{:S(2)}, u32[]{:S(2)}) %collective-permute-start.8) | collective-permute-done | bytes 73760 | tf_op jit(solution)/shard_map/ppermute | solution.py:457
  98.0 5.0 %collective-permute-start.12 = (f32[48,256]{1,0:T(8,128)S(1)}, f32[48,256]{1,0:T(8,128)S(1)}, u32[]{:S(2)}, u32[]{:S(2)}) collective-permute-start(f32[48,256]{1,0:T(8,128)S(1)} %get-tuple-element.50.st), channel_id=1, source_target_pairs={{1,2},{2,1},{3,4},{4,3},{5,6},{6,5},{7,8},{8,7},{9,10},{10,9},{11,... | collective-permute-start | bytes 147464 | tf_op jit(solution)/shard_map/ppermute | solution.py:460
  103.1 4.0 %partner_query_grads.1 = (bf16[1536,256]{1,0:T(8,128)(2,1)S(1)}, bf16[512,512]{1,0:T(8,128)(2,1)S(1)}) custom-call(s32[114]{0:T(128)S(1)} %pad_add_fusion.sc, bf16[256,1536]{1,0:T(8,128)(2,1)S(1)} %collective-permute-done.qn.qs.qnp, bf16[256,1536]{1,0:T(8,128)(2,1)S(1)} %collective-permute-done.7.do.ds.dop, f32[48,256]{1,0:T(8,128)S(1)} %get-tuple-element.50.st, ...), custom_call_target="tpu_custom_call" | custom-call | tf_op jit(solution)/shard_map/partner_query_grads/pallas_call | solution.py:430
  107.2 2.3 %collective-permute-start.13 = (bf16[1536,256]{1,0:T(8,128)(2,1)S(1)}, bf16[1536,256]{1,0:T(8,128)(2,1)S(1)}, u32[]{:S(2)}, u32[]{:S(2)}) collective-permute-start(bf16[1536,256]{1,0:T(8,128)(2,1)S(1)} %get-tuple-element.51._), channel_id=1, source_target_pairs={{0,1},{1,0},{2,3},{3,2},{4,5},{5,4},{6,7},{7,6},{8,9},{9,8},{10,11... | collective-permute-start | bytes 2359304 | tf_op jit(solution)/shard_map/ppermute | solution.py:457
  109.5 7.9 %own_query_grads.1 = (f32[1536,256]{1,0:T(8,128)S(1)}, f32[256,1536]{1,0:T(8,128)S(1)}, f32[256,1536]{1,0:T(8,128)S(1)}, bf16[512,512]{1,0:T(8,128)(2,1)S(1)}) custom-call(s32[114]{0:T(128)S(1)} %pad_add_fusion.sc, bf16[256,1536]{1,0:T(8,128)(2,1)S(1)} %get-tuple-element.34.qn, bf16[256,1536]{1,0:T(8,128)(2,1)S(1)} %bitcast.18, ...), custom_call_target="tpu_custom_call" | custom-call | tf_op jit(solution)/shard_map/own_query_grads/pallas_call | solution.py:430
  117.3 4.5 %collective-permute-start.14 = (bf16[512,512]{1,0:T(8,128)(2,1)S(1)}, bf16[512,512]{1,0:T(8,128)(2,1)S(1)}, u32[]{:S(2)}, u32[]{:S(2)}) collective-permute-start(bf16[512,512]{1,0:T(8,128)(2,1)S(1)} %get-tuple-element.56), channel_id=1, source_target_pairs={{1,2},{2,1},{3,4},{4,3},{5,6},{6,5},{7,8},{8,7},{9,10},{10,9},{11,... | collective-permute-start | bytes 1572872 | tf_op jit(solution)/shard_map/ppermute | solution.py:460
  121.9 5.0 %collective-permute-start.15 = (bf16[512,512]{1,0:T(8,128)(2,1)S(1)}, bf16[512,512]{1,0:T(8,128)(2,1)S(1)}, u32[]{:S(2)}, u32[]{:S(2)}) collective-permute-start(bf16[512,512]{1,0:T(8,128)(2,1)S(1)} %get-tuple-element.57), channel_id=1, source_target_pairs={{1,2},{2,1},{3,4},{4,3},{5,6},{6,5},{7,8},{8,7},{9,10},{10,9},{11,... | collective-permute-start | bytes 1572872 | tf_op jit(solution)/shard_map/ppermute | solution.py:460
  126.8 4.1 %partner_near_grads.1 = (bf16[256,1536]{1,0:T(8,128)(2,1)S(1)}, bf16[256,1536]{1,0:T(8,128)(2,1)S(1)}, bf16[512,512]{1,0:T(8,128)(2,1)S(1)}) custom-call(s32[114]{0:T(128)S(1)} %pad_add_fusion.sc, bf16[256,1536]{1,0:T(8,128)(2,1)S(1)} %get-tuple-element.47.knp, bf16[256,1536]{1,0:T(8,128)(2,1)} %collective-permute-done.2.vp, ...), custom_call_target="tpu_custom_call" | custom-call | flops 20000000000 | bytes 20000000000 | tf_op jit(solution)/shard_map/partner_near_grads/pallas_call | solution.py:430
  130.9 4.5 %collective-permute-start.16 = (bf16[512,512]{1,0:T(8,128)(2,1)S(1)}, bf16[512,512]{1,0:T(8,128)(2,1)S(1)}, u32[]{:S(2)}, u32[]{:S(2)}) collective-permute-start(bf16[512,512]{1,0:T(8,128)(2,1)S(1)} %get-tuple-element.58), channel_id=1, source_target_pairs={{1,2},{2,1},{3,4},{4,3},{5,6},{6,5},{7,8},{8,7},{9,10},{10,9},{11,... | collective-permute-start | bytes 1572872 | tf_op jit(solution)/shard_map/ppermute | solution.py:460
  138.8 2.2 %partner_far_grads.3._ = bf16[512,512]{1,0:T(8,128)(2,1)S(1)} custom-call(s32[114]{0:T(128)S(1)} %pad_add_fusion.sc, bf16[256,1536]{1,0:T(8,128)(2,1)S(1)} %get-tuple-element.47.knp, bf16[256,1536]{1,0:T(8,128)(2,1)} %collective-permute-done.2.vp, bf16[512,512]{1,0:T(8,128)(2,1)S(1)} %collective-permute-done.14.both.refs_0_, ...), custom_call_target="tpu_custom_call" | custom-call | flops 20000000000 | bytes 20000000000 | tf_op jit(solution)/shard_map/partner_far_grads/pallas_call | solution.py:430
  141.2 7.8 %collective-permute-done.15.both.refs_1_ = bf16[512,512]{1,0:T(8,128)(2,1)S(1)} collective-permute-done((bf16[512,512]{1,0:T(8,128)(2,1)S(1)}, bf16[512,512]{1,0:T(8,128)(2,1)S(1)}, u32[]{:S(2)}, u32[]{:S(2)}) %collective-permute-start.15) | collective-permute-done | bytes 524320 | tf_op jit(solution)/shard_map/ppermute | solution.py:460
  148.9 2.2 %partner_far_grads.4._ = bf16[512,512]{1,0:T(8,128)(2,1)S(1)} custom-call(s32[114]{0:T(128)S(1)} %pad_add_fusion.sc, bf16[256,1536]{1,0:T(8,128)(2,1)S(1)} %get-tuple-element.47.knp, bf16[256,1536]{1,0:T(8,128)(2,1)} %collective-permute-done.2.vp, bf16[512,512]{1,0:T(8,128)(2,1)S(1)} %collective-permute-done.15.both.refs_1_, ...), custom_call_target="tpu_custom_call" | custom-call | flops 20000000000 | bytes 20000000000 | tf_op jit(solution)/shard_map/partner_far_grads/pallas_call | solution.py:430
  151.3 3.8 %collective-permute-done.16.both.refs_2_ = bf16[512,512]{1,0:T(8,128)(2,1)S(1)} collective-permute-done((bf16[512,512]{1,0:T(8,128)(2,1)S(1)}, bf16[512,512]{1,0:T(8,128)(2,1)S(1)}, u32[]{:S(2)}, u32[]{:S(2)}) %collective-permute-start.16) | collective-permute-done | bytes 524320 | tf_op jit(solution)/shard_map/ppermute | solution.py:460
  155.1 2.2 %partner_far_grads.5.refs_3_ = bf16[512,512]{1,0:T(8,128)(2,1)S(1)} custom-call(s32[114]{0:T(128)S(1)} %pad_add_fusion.sc, bf16[256,1536]{1,0:T(8,128)(2,1)S(1)} %get-tuple-element.47.knp, bf16[256,1536]{1,0:T(8,128)(2,1)} %collective-permute-done.2.vp, bf16[512,512]{1,0:T(8,128)(2,1)S(1)} %collective-permute-done.16.both.refs_2_, ...), custom_call_target="tpu_custom_call" | custom-call | flops 20000000000 | bytes 20000000000 | tf_op jit(solution)/shard_map/partner_far_grads/pallas_call | solution.py:430
  157.7 7.5 %own_key_grads.1 = (f32[256,1536]{1,0:T(8,128)S(1)}, f32[256,1536]{1,0:T(8,128)S(1)}) custom-call(s32[114]{0:T(128)S(1)} %pad_add_fusion.sc, bf16[256,1536]{1,0:T(8,128)(2,1)S(1)} %copy-done.6, bf16[256,1536]{1,0:T(8,128)(2,1)S(1)} %bitcast.23, bf16[256,1536]{1,0:T(8,128)(2,1)S(1)} %collective-permute-done.qn.qs.qnp, ...), custom_call_target="tpu_custom_call" | custom-call | flops 20000000000 | bytes 20000000000 | tf_op jit(solution)/shard_map/own_key_grads/pallas_call | solution.py:430
  165.2 2.5 %finish_queries.1 = bf16[256,1536]{1,0:T(8,128)(2,1)} custom-call(f32[2,128]{1,0:T(2,128)S(1)} %bitcast.27, f32[1536,256]{1,0:T(8,128)S(1)} %get-tuple-element.52._.dqt, bf16[1536,256]{1,0:T(8,128)(2,1)S(1)} %collective-permute-done.13.dqr, bf16[256,1536]{1,0:T(8,128)(2,1)S(1)} %bitcast.30, f32[256,1536]{1,0:T(8,128)S(1)} %get-tuple-element.60._.dk), custom_call_target="tpu_custom_call" | custom-call | flops 20000000000 | bytes 20000000000 | tf_op jit(solution)/shard_map/finish_queries/pallas_call | solution.py:430
  167.7 4.3 %collective-permute-done.19.refs_2_ = bf16[512,512]{1,0:T(8,128)(2,1)S(1)} collective-permute-done((bf16[512,512]{1,0:T(8,128)(2,1)S(1)}, bf16[512,512]{1,0:T(8,128)(2,1)S(1)}, u32[]{:S(2)}, u32[]{:S(2)}) %collective-permute-start.19) | collective-permute-done | bytes 524320 | tf_op jit(solution)/shard_map/ppermute | solution.py:457
  172.0 2.7 %finish_keys.1 = (bf16[256,1536]{1,0:T(8,128)(2,1)}, bf16[256,1536]{1,0:T(8,128)(2,1)}) custom-call(f32[2,128]{1,0:T(2,128)S(1)} %bitcast.28, bf16[256,1536]{1,0:T(8,128)(2,1)S(1)} %bitcast.34, f32[256,1536]{1,0:T(8,128)S(1)} %get-tuple-element.60._.dk, f32[256,1536]{1,0:T(8,128)S(1)} %get-tuple-element.61.dv, ...), custom_call_target="tpu_custom_call" | custom-call | flops 20000000000 | bytes 20000000000 | tf_op jit(solution)/shard_map/finish_keys/pallas_call | solution.py:430
  (59 shorter events, 13.9 us)
Async XLA Ops:
  0.6 40.5 %collective-permute-start.2 = (bf16[256,1536]{1,0:T(8,128)(2,1)}, bf16[256,1536]{1,0:T(8,128)(2,1)}, u32[]{:S(2)}, u32[]{:S(2)}) collective-permute-start(bf16[256,1536]{1,0:T(8,128)(2,1)} %bitcast.19), channel_id=1, source_target_pairs={{0,1},{1,0},{2,3},{3,2},{4,5},{5,4},{6,7},{7,6},{8,9},{9,8},{10,11... | collective-permute-start | bytes 2359304 | tf_op jit(solution)/shard_map/ppermute | solution.py:457
  2.6 40.2 %collective-permute-start.4 = (bf16[256,1536]{1,0:T(8,128)(2,1)}, bf16[256,1536]{1,0:T(8,128)(2,1)S(1)}, u32[]{:S(2)}, u32[]{:S(2)}) collective-permute-start(bf16[256,1536]{1,0:T(8,128)(2,1)} %bitcast.20), channel_id=1, source_target_pairs={{1,2},{2,1},{3,4},{4,3},{5,6},{6,5},{7,8},{8,7},{9,10},{10,9},{11,... | collective-permute-start | bytes 2359304 | tf_op jit(solution)/shard_map/ppermute | solution.py:460
  9.3 38.5 %collective-permute-start.1 = (bf16[256,1536]{1,0:T(8,128)(2,1)}, bf16[256,1536]{1,0:T(8,128)(2,1)}, u32[]{:S(2)}, u32[]{:S(2)}) collective-permute-start(bf16[256,1536]{1,0:T(8,128)(2,1)} %bitcast.31), channel_id=1, source_target_pairs={{0,1},{1,0},{2,3},{3,2},{4,5},{5,4},{6,7},{7,6},{8,9},{9,8},{10,11... | collective-permute-start | bytes 2359304 | tf_op jit(solution)/shard_map/ppermute | solution.py:457
  9.4 43.0 %collective-permute-start.3 = (bf16[256,1536]{1,0:T(8,128)(2,1)}, bf16[256,1536]{1,0:T(8,128)(2,1)}, u32[]{:S(2)}, u32[]{:S(2)}) collective-permute-start(bf16[256,1536]{1,0:T(8,128)(2,1)} %bitcast.32), channel_id=1, source_target_pairs={{1,2},{2,1},{3,4},{4,3},{5,6},{6,5},{7,8},{8,7},{9,10},{10,9},{11,... | collective-permute-start | bytes 2359304 | tf_op jit(solution)/shard_map/ppermute | solution.py:460
  33.9 1.1 copy-start
  35.1 1.1 copy-start.7
  36.2 1.1 copy-start.9
  37.3 3.6 %copy-start.13 = (s32[16,6]{0,1:T(8,128)S(1)}, s32[16,6]{0,1:T(8,128)}, u32[]{:S(2)}) copy-start(s32[16,6]{0,1:T(8,128)} %param.13) | copy-start | bytes 1156
  37.3 3.7 %copy-start.14 = (s32[16]{0:T(128)S(1)}, s32[16]{0:T(128)}, u32[]{:S(2)}) copy-start(s32[16]{0:T(128)} %param.12) | copy-start | bytes 196
  37.3 15.0 %copy-start.1 = (bf16[1,256,1536]{2,1,0:T(8,128)(2,1)S(1)}, bf16[1,256,1536]{2,1,0:T(8,128)(2,1)}, u32[]{:S(2)}) copy-start(bf16[1,256,1536]{2,1,0:T(8,128)(2,1)} %param.10) | copy-start | bytes 2359300
  40.5 26.0 %collective-permute-start = (bf16[256,1536]{1,0:T(8,128)(2,1)S(1)}, bf16[256,1536]{1,0:T(8,128)(2,1)S(1)}, u32[]{:S(2)}, u32[]{:S(2)}) collective-permute-start(bf16[256,1536]{1,0:T(8,128)(2,1)S(1)} %get-tuple-element.34.qn), channel_id=1, source_target_pairs={{0,1},{1,0},{2,3},{3,2},{4,5},{5,4},{6,7},{7,6},{8,9},{9,8},{10,11... | collective-permute-start | bytes 2359304 | tf_op jit(solution)/shard_map/ppermute | solution.py:457
  41.1 36.0 %collective-permute-start.7 = (bf16[256,1536]{1,0:T(8,128)(2,1)}, bf16[256,1536]{1,0:T(8,128)(2,1)S(1)}, u32[]{:S(2)}, u32[]{:S(2)}) collective-permute-start(bf16[256,1536]{1,0:T(8,128)(2,1)} %copy-done.11), channel_id=1, source_target_pairs={{0,1},{1,0},{2,3},{3,2},{4,5},{5,4},{6,7},{7,6},{8,9},{9,8},{10,11... | collective-permute-start | bytes 2359304 | tf_op jit(solution)/shard_map/ppermute | solution.py:457
  42.9 34.3 %collective-permute-start.6 = (bf16[256,1536]{1,0:T(8,128)(2,1)}, bf16[256,1536]{1,0:T(8,128)(2,1)S(1)}, u32[]{:S(2)}, u32[]{:S(2)}) collective-permute-start(bf16[256,1536]{1,0:T(8,128)(2,1)} %collective-permute-done.2.vp), channel_id=1, source_target_pairs={{1,2},{2,1},{3,4},{4,3},{5,6},{6,5},{7,8},{8,7},{9,10},{10,9},{11,... | collective-permute-start | bytes 2359304 | tf_op jit(solution)/shard_map/ppermute | solution.py:460
  47.8 38.0 %collective-permute-start.5 = (bf16[256,1536]{1,0:T(8,128)(2,1)}, bf16[256,1536]{1,0:T(8,128)(2,1)S(1)}, u32[]{:S(2)}, u32[]{:S(2)}) collective-permute-start(bf16[256,1536]{1,0:T(8,128)(2,1)} %collective-permute-done.1.kp), channel_id=1, source_target_pairs={{1,2},{2,1},{3,4},{4,3},{5,6},{6,5},{7,8},{8,7},{9,10},{10,9},{11,... | collective-permute-start | bytes 2359304 | tf_op jit(solution)/shard_map/ppermute | solution.py:460
  52.3 1.1 copy-start.2
  61.6 55.7 %collective-permute-start.10 = (bf16[256,1536]{1,0:T(8,128)(2,1)S(1)}, bf16[256,1536]{1,0:T(8,128)(2,1)S(1)}, u32[]{:S(2)}, u32[]{:S(2)}) collective-permute-start(bf16[256,1536]{1,0:T(8,128)(2,1)S(1)} %get-tuple-element.48), channel_id=1, source_target_pairs={{1,2},{2,1},{3,4},{4,3},{5,6},{6,5},{7,8},{8,7},{9,10},{10,9},{11,... | collective-permute-start | bytes 2359304 | tf_op jit(solution)/shard_map/ppermute | solution.py:460
  66.6 55.3 %collective-permute-start.11 = (bf16[256,1536]{1,0:T(8,128)(2,1)S(1)}, bf16[256,1536]{1,0:T(8,128)(2,1)S(1)}, u32[]{:S(2)}, u32[]{:S(2)}) collective-permute-start(bf16[256,1536]{1,0:T(8,128)(2,1)S(1)} %get-tuple-element.49), channel_id=1, source_target_pairs={{1,2},{2,1},{3,4},{4,3},{5,6},{6,5},{7,8},{8,7},{9,10},{10,9},{11,... | collective-permute-start | bytes 2359304 | tf_op jit(solution)/shard_map/ppermute | solution.py:460
  93.5 4.4 %collective-permute-start.8 = (f32[72,256]{1,0:T(8,128)S(1)}, f32[72,256]{1,0:T(8,128)S(1)}, u32[]{:S(2)}, u32[]{:S(2)}) collective-permute-start(f32[72,256]{1,0:T(8,128)S(1)} %get-tuple-element.43.mine), channel_id=1, source_target_pairs={{0,1},{1,0},{2,3},{3,2},{4,5},{5,4},{6,7},{7,6},{8,9},{9,8},{10,11... | collective-permute-start | bytes 221192 | tf_op jit(solution)/shard_map/ppermute | solution.py:457
  98.0 28.8 %collective-permute-start.12 = (f32[48,256]{1,0:T(8,128)S(1)}, f32[48,256]{1,0:T(8,128)S(1)}, u32[]{:S(2)}, u32[]{:S(2)}) collective-permute-start(f32[48,256]{1,0:T(8,128)S(1)} %get-tuple-element.50.st), channel_id=1, source_target_pairs={{1,2},{2,1},{3,4},{4,3},{5,6},{6,5},{7,8},{8,7},{9,10},{10,9},{11,... | collective-permute-start | bytes 147464 | tf_op jit(solution)/shard_map/ppermute | solution.py:460
  103.0 6.4 %copy-start.3 = (bf16[1,256,1536]{2,1,0:T(8,128)(2,1)S(1)}, bf16[1,256,1536]{2,1,0:T(8,128)(2,1)}, u32[]{:S(2)}) copy-start(bf16[1,256,1536]{2,1,0:T(8,128)(2,1)} %param.9) | copy-start | bytes 2359300
  103.0 6.4 %copy-start.6 = (bf16[256,1536]{1,0:T(8,128)(2,1)S(1)}, bf16[256,1536]{1,0:T(8,128)(2,1)}, u32[]{:S(2)}) copy-start(bf16[256,1536]{1,0:T(8,128)(2,1)} %copy-done.4) | copy-start | bytes 2359300
  103.0 32.4 %collective-permute-start.9 = (bf16[1536,256]{1,0:T(8,128)(2,1)S(1)}, bf16[1536,256]{1,0:T(8,128)(2,1)S(1)}, u32[]{:S(2)}, u32[]{:S(2)}) collective-permute-start(bf16[1536,256]{1,0:T(8,128)(2,1)S(1)} %get-tuple-element.46), channel_id=1, source_target_pairs={{0,1},{1,0},{2,3},{3,2},{4,5},{5,4},{6,7},{7,6},{8,9},{9,8},{10,11... | collective-permute-start | bytes 2359304 | tf_op jit(solution)/shard_map/ppermute | solution.py:457
  107.2 58.0 %collective-permute-start.13 = (bf16[1536,256]{1,0:T(8,128)(2,1)S(1)}, bf16[1536,256]{1,0:T(8,128)(2,1)S(1)}, u32[]{:S(2)}, u32[]{:S(2)}) collective-permute-start(bf16[1536,256]{1,0:T(8,128)(2,1)S(1)} %get-tuple-element.51._), channel_id=1, source_target_pairs={{0,1},{1,0},{2,3},{3,2},{4,5},{5,4},{6,7},{7,6},{8,9},{9,8},{10,11... | collective-permute-start | bytes 2359304 | tf_op jit(solution)/shard_map/ppermute | solution.py:457
  117.3 20.4 %collective-permute-start.14 = (bf16[512,512]{1,0:T(8,128)(2,1)S(1)}, bf16[512,512]{1,0:T(8,128)(2,1)S(1)}, u32[]{:S(2)}, u32[]{:S(2)}) collective-permute-start(bf16[512,512]{1,0:T(8,128)(2,1)S(1)} %get-tuple-element.56), channel_id=1, source_target_pairs={{1,2},{2,1},{3,4},{4,3},{5,6},{6,5},{7,8},{8,7},{9,10},{10,9},{11,... | collective-permute-start | bytes 1572872 | tf_op jit(solution)/shard_map/ppermute | solution.py:460
  121.9 27.1 %collective-permute-start.15 = (bf16[512,512]{1,0:T(8,128)(2,1)S(1)}, bf16[512,512]{1,0:T(8,128)(2,1)S(1)}, u32[]{:S(2)}, u32[]{:S(2)}) collective-permute-start(bf16[512,512]{1,0:T(8,128)(2,1)S(1)} %get-tuple-element.57), channel_id=1, source_target_pairs={{1,2},{2,1},{3,4},{4,3},{5,6},{6,5},{7,8},{8,7},{9,10},{10,9},{11,... | collective-permute-start | bytes 1572872 | tf_op jit(solution)/shard_map/ppermute | solution.py:460
  130.9 24.2 %collective-permute-start.16 = (bf16[512,512]{1,0:T(8,128)(2,1)S(1)}, bf16[512,512]{1,0:T(8,128)(2,1)S(1)}, u32[]{:S(2)}, u32[]{:S(2)}) collective-permute-start(bf16[512,512]{1,0:T(8,128)(2,1)S(1)} %get-tuple-element.58), channel_id=1, source_target_pairs={{1,2},{2,1},{3,4},{4,3},{5,6},{6,5},{7,8},{8,7},{9,10},{10,9},{11,... | collective-permute-start | bytes 1572872 | tf_op jit(solution)/shard_map/ppermute | solution.py:460
  137.7 1.1 copy-start.12
  141.1 30.9 %collective-permute-start.17 = (bf16[512,512]{1,0:T(8,128)(2,1)S(1)}, bf16[512,512]{1,0:T(8,128)(2,1)S(1)}, u32[]{:S(2)}, u32[]{:S(2)}) collective-permute-start(bf16[512,512]{1,0:T(8,128)(2,1)S(1)} %partner_far_grads.3._), channel_id=1, source_target_pairs={{0,1},{1,0},{2,3},{3,2},{4,5},{5,4},{6,7},{7,6},{8,9},{9,8},{10,11... | collective-permute-start | bytes 1572872 | tf_op jit(solution)/shard_map/ppermute | solution.py:457
  151.2 20.8 %collective-permute-start.18 = (bf16[512,512]{1,0:T(8,128)(2,1)S(1)}, bf16[512,512]{1,0:T(8,128)(2,1)S(1)}, u32[]{:S(2)}, u32[]{:S(2)}) collective-permute-start(bf16[512,512]{1,0:T(8,128)(2,1)S(1)} %partner_far_grads.4._), channel_id=1, source_target_pairs={{0,1},{1,0},{2,3},{3,2},{4,5},{5,4},{6,7},{7,6},{8,9},{9,8},{10,11... | collective-permute-start | bytes 1572872 | tf_op jit(solution)/shard_map/ppermute | solution.py:457
  157.3 14.7 %collective-permute-start.19 = (bf16[512,512]{1,0:T(8,128)(2,1)S(1)}, bf16[512,512]{1,0:T(8,128)(2,1)S(1)}, u32[]{:S(2)}, u32[]{:S(2)}) collective-permute-start(bf16[512,512]{1,0:T(8,128)(2,1)S(1)} %partner_far_grads.5.refs_3_), channel_id=1, source_target_pairs={{0,1},{1,0},{2,3},{3,2},{4,5},{5,4},{6,7},{7,6},{8,9},{9,8},{10,11... | collective-permute-start | bytes 1572872 | tf_op jit(solution)/shard_map/ppermute | solution.py:457
  157.6 7.5 %copy-start.8 = (bf16[1,256,1536]{2,1,0:T(8,128)(2,1)S(1)}, bf16[1,256,1536]{2,1,0:T(8,128)(2,1)}, u32[]{:S(2)}) copy-start(bf16[1,256,1536]{2,1,0:T(8,128)(2,1)} %param.7) | copy-start | bytes 2359300
  165.2 6.8 %copy-start.10 = (bf16[1,256,1536]{2,1,0:T(8,128)(2,1)S(1)}, bf16[1,256,1536]{2,1,0:T(8,128)(2,1)}, u32[]{:S(2)}) copy-start(bf16[1,256,1536]{2,1,0:T(8,128)(2,1)} %param.8) | copy-start | bytes 2359300
  (3 other events, 2.9 us)

commit v4 on v3

--- a/solution.py
+++ b/solution.py
@@ -23,7 +23,8 @@
         "own_query_grads",
     ),
     0,
-)
+) | {"partner_near_grads": 5_000_000_000}
+CHUNKS = ((0, 2), (4, 4), (8, 4), (2, 2))
 OTHER = 20_000_000_000
 SCALE = math.log2(math.e) / math.sqrt(128)
 BF = jnp.bfloat16
@@ -125,14 +126,14 @@
     return units
 
 
-def backward_units(permit, kn, v, qn, do, st, use, half=0, first=None, heads=None):
+def backward_units(permit, kn, v, qn, do, st, use, half=0, first=None, heads=None, n=HB):
     if heads is None:
         heads = pl.num_programs(0) * HB
     if first is None:
         first = pl.program_id(0) * HB
     base = 2 * half * heads
     units = []
-    for j in range(HB):
+    for j in range(n):
         def scores(c=cols(j)):
             return dot(kn[:, c], qn[:, c], NT), dot(v[:, c], do[:, c], NT)
 
@@ -281,7 +282,8 @@
                 sh_ref[heads:] = w2
 
 
-def merge(acc_ref, sh, o_ret, _, att_ref):
+def merge(acc_ref, sh, o_ret, qs, ds, _, att_ref, both_out):
+    stack(both_out, qs, ds)
     step = pl.program_id(0)
     heads = pl.num_programs(0) * HB
     for j in range(HB):
@@ -342,7 +344,7 @@
     dv_ref[...] = dv[...].astype(BF)
 
 
-def partner_far_grads(chunk, heads, sc, knp, vp, both, st, dk0, dv0, _, out, dk, dv):
+def partner_far_grads(start, n, heads, sc, knp, vp, both, st, dk0, dv0, _, __, out, dk, dv):
     me, partner, near, far = around(sc)
     dk[...] = dk0[...].astype(F32)
     dv[...] = dv0[...].astype(F32)
@@ -350,7 +352,7 @@
     use = partial(key_use, qn, do, dk, dv)
     emit(
         backward_units(
-            allowed(sc, far, partner), knp, vp, qn, do, st, use, 1, chunk * HB, heads
+            allowed(sc, far, partner), knp, vp, qn, do, st, use, 1, start, heads, n
         )
     )
     out[:ROWS] = dk[...].astype(BF)
@@ -369,12 +371,19 @@
         backward_units(allowed(sc, partner, me), knx, v, qnp, dop, st, own, 1)
         + backward_units(allowed(sc, near, me), knx, v, qne, doe, ste, use)
     )
-    for chunk, both in enumerate(chunks):
-        @pl.when(pl.program_id(0) == chunk)
-        def _(both=both):
+    for (start, n), both in zip(CHUNKS, chunks):
+        @pl.when(pl.program_id(0) == start // HB)
+        def _(start=start, n=n, both=both):
+            part = pl.ds(start % HB * HD, n * HD)
             qn, do = both.at[pl.ds(0, ROWS)], both.at[pl.ds(ROWS, ROWS)]
-            last = partial(key_use, qn, do, dk, dv)
-            emit(backward_units(allowed(sc, far, me), knx, v, qn, do, ste, last, 1))
+            last = partial(key_use, qn, do, dk.at[:, part], dv.at[:, part])
+            heads = pl.num_programs(0) * HB
+            emit(
+                backward_units(
+                    allowed(sc, far, me), knx.at[:, part], v.at[:, part], qn, do, ste, last,
+                    1, start, heads, n,
+                )
+            )
 
 
 def finish_queries(g, dqt, dqr, q, _, dq_out):
@@ -388,14 +397,14 @@
 def finish_keys(g, k, dk, dv, *refs):
     dk_out, dv_out = refs[-2:]
     scale = 1.0 / math.sqrt(HD)
-    for chunk, back in enumerate(refs[:-2]):
-        @pl.when(pl.program_id(0) == chunk)
-        def _(back=back):
-            for j in range(HB):
-                c = cols(j)
-                total = (dk[:, c] + back[:ROWS, c].astype(F32)) * scale
+    for (start, n), back in zip(CHUNKS, refs[:-2]):
+        @pl.when(pl.program_id(0) == start // HB)
+        def _(start=start, n=n, back=back):
+            for j in range(n):
+                c, b = cols(start % HB + j), cols(j)
+                total = (dk[:, c] + back[:ROWS, b].astype(F32)) * scale
                 dk_out[:, c] = denormed(k[:, c], g[1:2, :], total)
-            dv_out[...] = (dv[...] + back[ROWS:].astype(F32)).astype(BF)
+                dv_out[:, c] = (dv[:, c] + back[ROWS:, b].astype(F32)).astype(BF)
 
 
 WIDE = "wide"
@@ -409,8 +418,9 @@
         return pl.BlockSpec((ROWS, HB * HD), lambda i, *_: (0, i))
     if kind == TALL:
         return pl.BlockSpec((HB * HD, ROWS), lambda i, *_: (i, 0))
-    if isinstance(kind, int):
-        return pl.BlockSpec((ROWS, HB * HD), lambda i, *_: (0, kind))
+    if isinstance(kind, tuple):
+        start, n = kind
+        return pl.BlockSpec((ROWS, n * HD), lambda i, *_: (0, start // n))
     if kind == ORDER:
         return pl.BlockSpec(memory_space=pl.ANY)
     return pl.BlockSpec(arr.shape, lambda i, *_: (0,) * len(arr.shape))
@@ -478,7 +488,7 @@
     scalars = (jnp.concatenate([place, tile_device, neighbours.reshape(-1)]),)
     gain = [(FULL, g)]
     chunks = features // (HB * HD)
-    pair = (FULL, (2 * ROWS, HB * HD), BF)
+    pairs = [(FULL, (2 * ROWS, n * HD), BF) for _, n in CHUNKS]
 
     qn, knx, do2 = run(prepare, (), gain + wide(q, k, do), [wide_bf] * 3)
     kf, vf = beyond(kp, vp)
@@ -508,46 +518,55 @@
     (o_ret,) = across(op)
 
     def send(i):
-        return [(i, qnp), (i, dop)]
+        return [(CHUNKS[i], qnp), (CHUNKS[i], dop)]
 
     dqp, sent0 = run(
         partner_query_grads, scalars,
         wide(qnp, dop) + [(FULL, st)] + wide(kne, ve, knf, vf) + send(0),
-        [tall_bf, pair], (acc_t,),
+        [tall_bf, pairs[0]], (acc_t,),
     )
     (dqr,) = across(dqp)
     dqt, dk, dv, sent1 = run(
         own_query_grads, scalars,
         wide(qn, do) + [(FULL, st)] + wide(knx, v, knp, vp, kne, ve, knf, vf) + send(1)
         + [(ORDER, dqp)],
-        [tall_f, wide_f, wide_f, pair],
+        [tall_f, wide_f, wide_f, pairs[1]],
     )
     dkp, dvp, sent2 = run(
         partner_near_grads, scalars,
         wide(knp, vp, qne, doe) + [(FULL, ste)] + send(2) + [(ORDER, dqt)],
-        [wide_bf, wide_bf, pair], (acc_w, acc_w),
+        [wide_bf, wide_bf, pairs[2]], (acc_w, acc_w),
     )
     far = beyond(sent0, sent1, sent2)
-    (att,) = run(
-        merge, (), [(TALL, acc), (FULL, shares), (TALL, o_ret), (ORDER, dkp)], [wide_bf], (), chunks,
-    )
-    last, back = att, []
-    for i in range(chunks):
+    last, back = dkp, []
+    for i, (start, n) in enumerate(CHUNKS):
+        at = (start, n)
+        wait = o_ret if i == 0 else last
+        acc_n = pltpu.VMEM((ROWS, n * HD), F32)
         (last,) = run(
-            partial(partner_far_grads, i, heads), scalars,
-            [(i, knp), (i, vp), (FULL, far[i]), (FULL, ste), (i, dkp), (i, dvp), (ORDER, last)],
-            [pair], (acc_w, acc_w), 1, "partner_far_grads",
+            partial(partner_far_grads, start, n, heads), scalars,
+            [(at, knp), (at, vp), (FULL, far[i]), (FULL, ste), (at, dkp), (at, dvp), (ORDER, last), (ORDER, wait)],
+            [pairs[i]], (acc_n, acc_n), 1, "partner_far_grads",
         )
         back += across(last)
+        if i == 0:
+            att, sent3 = run(
+                merge, (), [(TALL, acc), (FULL, shares), (TALL, o_ret)] + send(3) + [(ORDER, last)],
+                [wide_bf, pairs[3]], (), chunks,
+            )
+            far += beyond(sent3)
+            last = att
+        if i == 1:
+            (dq_out,) = run(
+                finish_queries, (),
+                gain + [(TALL, dqt), (TALL, dqr)] + wide(q) + [(ORDER, last)], [wide_bf],
+            )
+            last = dq_out
     dk, dv = run(
         own_key_grads, scalars,
         wide(knx, v, qnp, dop) + [(FULL, st)] + wide(qne, doe) + [(FULL, ste)]
         + wide(dk, dv) + [(FULL, part) for part in far] + [(ORDER, last)],
         [wide_f, wide_f],
-    )
-    (dq_out,) = run(
-        finish_queries, (), gain + [(TALL, dqt), (TALL, dqr)] + wide(q) + [(ORDER, dk)],
-        [wide_bf],
     )
     dk_out, dv_out = run(
         finish_keys, (), gain + wide(k, dk, dv) + [(FULL, part) for part in back], [wide_bf] * 2

time: 176 us -> 176 us (level)
  waiting for transfers between devices: 35.6 us -> 28.3 us
  starting transfers between devices: 55.4 us -> 60.6 us
  Pallas kernels: 53.2 us -> 55 us
    ppermute x10 -> x11, waiting for transfers between devices: 20.9 us -> 12.7 us  [beyond(): return [lax.ppermute(value, 'ctx', outer) for value in values]]
    ppermute x10 -> x11, starting transfers between devices: 48.3 us -> 53.4 us  [beyond(): return [lax.ppermute(value, 'ctx', outer) for value in values]]
    pallas_call x15 -> x16, Pallas kernels: 53.2 us -> 55 us  [run(): pl.pallas_call(body, name=name or body.__name__, grid_spec=grid_spec, out...]
    unnamed x32 -> x34, local copies, waits for them, and re-layouts: 8.75 us -> 9.87 us
    ppermute x10 -> x11, waiting for transfers between devices: 14.7 us -> 15.6 us  [across(): return [lax.ppermute(value, 'ctx', inner) for value in values]]
    ppermute x10 -> x11, starting transfers between devices: 7.11 us -> 7.22 us  [across(): return [lax.ppermute(value, 'ctx', inner) for value in values]]
  transfers between devices with their start and end apart: 20 -> 22, of which waited for: 7 -> 5; matrix products, arithmetic and copies ran while one was open for 0% -> 0% of each run, Pallas kernels for 29% -> 30%
where the time goes in v4:
time: 176 us
  starting transfers between devices  60.6 us (34%)
  Pallas kernels  55 us (31%)
  waiting for transfers between devices  28.3 us (16%)
  blocking collectives  20.6 us (12%)
  local copies, waits for them, and re-layouts  9.96 us (6%)
    pallas_call x16, Pallas kernels, run(): pl.pallas_call(body, name=name or body.__name__, grid_spec=grid_spec, out...  55 us
    ppermute x11, starting transfers between devices, beyond(): return [lax.ppermute(value, 'ctx', outer) for value in values]  53.4 us
    all_gather x1, blocking collectives, local(): g = lax.all_gather(gains, 'fsdp', axis=1, tiled=True)  20.6 us
    ppermute x11, waiting for transfers between devices, across(): return [lax.ppermute(value, 'ctx', inner) for value in values]  15.6 us
    ppermute x11, waiting for transfers between devices, beyond(): return [lax.ppermute(value, 'ctx', outer) for value in values]  12.7 us
    unnamed x34, local copies, waits for them, and re-layouts  9.87 us
    ppermute x11, starting transfers between devices, across(): return [lax.ppermute(value, 'ctx', inner) for value in values]  7.22 us
  transfers between devices with their start and end apart: 22, of which 5 were waited for; matrix products, arithmetic and copies ran while one was open for 0% of the time, Pallas kernels for 30%

profile of v4, /device:TPU:16, one launch (start us, length us, event | category | flops | bytes accessed | tf_op | source)
XLA Modules:
  0.0 175.6 jit_solution(14724960790083783810)
XLA Ops:
  0.6 2.0 %collective-permute-start.2 = (bf16[256,1536]{1,0:T(8,128)(2,1)}, bf16[256,1536]{1,0:T(8,128)(2,1)}, u32[]{:S(2)}, u32[]{:S(2)}) collective-permute-start(bf16[256,1536]{1,0:T(8,128)(2,1)} %bitcast.19), channel_id=1, source_target_pairs={{0,1},{1,0},{2,3},{3,2},{4,5},{5,4},{6,7},{7,6},{8,9},{9,8},{10,11... | collective-permute-start | bytes 2359304 | tf_op jit(solution)/shard_map/ppermute | solution.py:467
  2.6 6.6 %collective-permute-start.4 = (bf16[256,1536]{1,0:T(8,128)(2,1)}, bf16[256,1536]{1,0:T(8,128)(2,1)S(1)}, u32[]{:S(2)}, u32[]{:S(2)}) collective-permute-start(bf16[256,1536]{1,0:T(8,128)(2,1)} %bitcast.20), channel_id=1, source_target_pairs={{1,2},{2,1},{3,4},{4,3},{5,6},{6,5},{7,8},{8,7},{9,10},{10,9},{11,... | collective-permute-start | bytes 2359304 | tf_op jit(solution)/shard_map/ppermute | solution.py:470
  9.4 3.9 %collective-permute-start.3 = (bf16[256,1536]{1,0:T(8,128)(2,1)}, bf16[256,1536]{1,0:T(8,128)(2,1)}, u32[]{:S(2)}, u32[]{:S(2)}) collective-permute-start(bf16[256,1536]{1,0:T(8,128)(2,1)} %bitcast.32), channel_id=1, source_target_pairs={{1,2},{2,1},{3,4},{4,3},{5,6},{6,5},{7,8},{8,7},{9,10},{10,9},{11,... | collective-permute-start | bytes 2359304 | tf_op jit(solution)/shard_map/ppermute | solution.py:470
  13.3 20.6 %all-gather = f32[16,8,2]{1,2,0:T(2,128)S(1)} all-gather(f32[1,8,2]{1,2,0:T(2,128)} %bitcast.37), channel_id=1, replica_groups=mesh['fsdp'=16,'ctx'=16] {'fsdp'}, dimensions={0}, use_global_device_ids=true | all-gather | bytes 1088 | tf_op jit(solution)/shard_map/all_gather | solution.py:486
  42.9 4.9 %collective-permute-start.6 = (bf16[256,1536]{1,0:T(8,128)(2,1)}, bf16[256,1536]{1,0:T(8,128)(2,1)S(1)}, u32[]{:S(2)}, u32[]{:S(2)}) collective-permute-start(bf16[256,1536]{1,0:T(8,128)(2,1)} %collective-permute-done.2.vp), channel_id=1, source_target_pairs={{1,2},{2,1},{3,4},{4,3},{5,6},{6,5},{7,8},{8,7},{9,10},{10,9},{11,... | collective-permute-start | bytes 2359304 | tf_op jit(solution)/shard_map/ppermute | solution.py:470
  47.8 4.5 %collective-permute-start.5 = (bf16[256,1536]{1,0:T(8,128)(2,1)}, bf16[256,1536]{1,0:T(8,128)(2,1)S(1)}, u32[]{:S(2)}, u32[]{:S(2)}) collective-permute-start(bf16[256,1536]{1,0:T(8,128)(2,1)} %collective-permute-done.1.kp), channel_id=1, source_target_pairs={{1,2},{2,1},{3,4},{4,3},{5,6},{6,5},{7,8},{8,7},{9,10},{10,9},{11,... | collective-permute-start | bytes 2359304 | tf_op jit(solution)/shard_map/ppermute | solution.py:470
  54.6 6.9 %own_forward.1 = (f32[1536,256]{1,0:T(8,128)S(1)}, f32[24,256]{1,0:T(8,128)S(1)}, bf16[256,1536]{1,0:T(8,128)(2,1)S(1)}, bf16[256,1536]{1,0:T(8,128)(2,1)S(1)}, ...) custom-call(s32[114]{0:T(128)S(1)} %pad_add_fusion.sc, f32[2,128]{1,0:T(2,128)S(1)} %bitcast.25, ...), custom_call_target="tpu_custom_call" | custom-call | flops 20000000000 | bytes 20000000000 | tf_op jit(solution)/shard_map/own_forward/pallas_call | solution.py:440
  61.5 5.0 %collective-permute-start.12 = (bf16[256,1536]{1,0:T(8,128)(2,1)S(1)}, bf16[256,1536]{1,0:T(8,128)(2,1)S(1)}, u32[]{:S(2)}, u32[]{:S(2)}) collective-permute-start(bf16[256,1536]{1,0:T(8,128)(2,1)S(1)} %get-tuple-element.52), channel_id=1, source_target_pairs={{1,2},{2,1},{3,4},{4,3},{5,6},{6,5},{7,8},{8,7},{9,10},{10,9},{11,... | collective-permute-start | bytes 2359304 | tf_op jit(solution)/shard_map/ppermute | solution.py:470
  66.5 4.5 %collective-permute-start.13 = (bf16[256,1536]{1,0:T(8,128)(2,1)S(1)}, bf16[256,1536]{1,0:T(8,128)(2,1)S(1)}, u32[]{:S(2)}, u32[]{:S(2)}) collective-permute-start(bf16[256,1536]{1,0:T(8,128)(2,1)S(1)} %get-tuple-element.53), channel_id=1, source_target_pairs={{1,2},{2,1},{3,4},{4,3},{5,6},{6,5},{7,8},{8,7},{9,10},{10,9},{11,... | collective-permute-start | bytes 2359304 | tf_op jit(solution)/shard_map/ppermute | solution.py:470
  71.0 6.1 %collective-permute-done.7.do.ds.dop = bf16[256,1536]{1,0:T(8,128)(2,1)S(1)} collective-permute-done((bf16[256,1536]{1,0:T(8,128)(2,1)}, bf16[256,1536]{1,0:T(8,128)(2,1)S(1)}, u32[]{:S(2)}, u32[]{:S(2)}) %collective-permute-start.7) | collective-permute-done | bytes 786464 | tf_op jit(solution)/shard_map/ppermute | solution.py:467
  77.1 8.7 %collective-permute-done.5.kf = bf16[256,1536]{1,0:T(8,128)(2,1)S(1)} collective-permute-done((bf16[256,1536]{1,0:T(8,128)(2,1)}, bf16[256,1536]{1,0:T(8,128)(2,1)S(1)}, u32[]{:S(2)}, u32[]{:S(2)}) %collective-permute-start.5) | collective-permute-done | bytes 786464 | tf_op jit(solution)/shard_map/ppermute | solution.py:470
  85.9 4.6 %partner_forward.1 = (bf16[1536,256]{1,0:T(8,128)(2,1)S(1)}, f32[36,256]{1,0:T(8,128)S(1)}, bf16[256,1536]{1,0:T(8,128)(2,1)S(1)}) custom-call(s32[114]{0:T(128)S(1)} %pad_add_fusion.sc, f32[2,128]{1,0:T(2,128)S(1)} %bitcast.26, bf16[256,1536]{1,0:T(8,128)(2,1)S(1)} %collective-permute-done.qn.qs.qnp, bf16[256,1536]{1,0:T(8,128)(2,1)S(1)} %get-tuple-element.38.kne, ...), custom_call_target="tpu_custom_call" | custom-call | tf_op jit(solution)/shard_map/partner_forward/pallas_call | solution.py:440
  90.4 3.0 %own_forward_far.1 = (f32[1536,256]{1,0:T(8,128)S(1)}, f32[72,256]{1,0:T(8,128)S(1)}) custom-call(s32[114]{0:T(128)S(1)} %pad_add_fusion.sc, bf16[256,1536]{1,0:T(8,128)(2,1)S(1)} %get-tuple-element.36.qn, bf16[256,1536]{1,0:T(8,128)(2,1)S(1)} %get-tuple-element.40.knf, bf16[256,1536]{1,0:T(8,128)(2,1)S(1)} %collective-permute-done.6.vf, ...), custom_call_target="tpu_custom_call" | custom-call | tf_op jit(solution)/shard_map/own_forward_far/pallas_call | solution.py:440
  93.5 4.8 %collective-permute-done.8.got = f32[72,256]{1,0:T(8,128)S(1)} collective-permute-done((f32[72,256]{1,0:T(8,128)S(1)}, f32[72,256]{1,0:T(8,128)S(1)}, u32[]{:S(2)}, u32[]{:S(2)}) %collective-permute-start.8) | collective-permute-done | bytes 73760 | tf_op jit(solution)/shard_map/ppermute | solution.py:467
  98.6 5.1 %collective-permute-start.11 = (f32[48,256]{1,0:T(8,128)S(1)}, f32[48,256]{1,0:T(8,128)S(1)}, u32[]{:S(2)}, u32[]{:S(2)}) collective-permute-start(f32[48,256]{1,0:T(8,128)S(1)} %get-tuple-element.50.st), channel_id=1, source_target_pairs={{1,2},{2,1},{3,4},{4,3},{5,6},{6,5},{7,8},{8,7},{9,10},{10,9},{11,... | collective-permute-start | bytes 147464 | tf_op jit(solution)/shard_map/ppermute | solution.py:470
  103.7 4.0 %partner_query_grads.1 = (bf16[1536,256]{1,0:T(8,128)(2,1)S(1)}, bf16[512,256]{1,0:T(8,128)(2,1)S(1)}) custom-call(s32[114]{0:T(128)S(1)} %pad_add_fusion.sc, bf16[256,1536]{1,0:T(8,128)(2,1)S(1)} %collective-permute-done.qn.qs.qnp, bf16[256,1536]{1,0:T(8,128)(2,1)S(1)} %collective-permute-done.7.do.ds.dop, f32[48,256]{1,0:T(8,128)S(1)} %get-tuple-element.50.st, ...), custom_call_target="tpu_custom_call" | custom-call | tf_op jit(solution)/shard_map/partner_query_grads/pallas_call | solution.py:440
  108.0 7.9 %own_query_grads.1 = (f32[1536,256]{1,0:T(8,128)S(1)}, f32[256,1536]{1,0:T(8,128)S(1)}, f32[256,1536]{1,0:T(8,128)S(1)}, bf16[512,512]{1,0:T(8,128)(2,1)S(1)}) custom-call(s32[114]{0:T(128)S(1)} %pad_add_fusion.sc, bf16[256,1536]{1,0:T(8,128)(2,1)S(1)} %get-tuple-element.36.qn, bf16[256,1536]{1,0:T(8,128)(2,1)S(1)} %bitcast.18, ...), custom_call_target="tpu_custom_call" | custom-call | tf_op jit(solution)/shard_map/own_query_grads/pallas_call | solution.py:440
  115.9 4.5 %collective-permute-start.10 = (bf16[512,256]{1,0:T(8,128)(2,1)S(1)}, bf16[512,256]{1,0:T(8,128)(2,1)S(1)}, u32[]{:S(2)}, u32[]{:S(2)}) collective-permute-start(bf16[512,256]{1,0:T(8,128)(2,1)S(1)} %get-tuple-element.51), channel_id=1, source_target_pairs={{1,2},{2,1},{3,4},{4,3},{5,6},{6,5},{7,8},{8,7},{9,10},{10,9},{11,... | collective-permute-start | bytes 786440 | tf_op jit(solution)/shard_map/ppermute | solution.py:470
  120.4 5.0 %collective-permute-start.15 = (bf16[512,512]{1,0:T(8,128)(2,1)S(1)}, bf16[512,512]{1,0:T(8,128)(2,1)S(1)}, u32[]{:S(2)}, u32[]{:S(2)}) collective-permute-start(bf16[512,512]{1,0:T(8,128)(2,1)S(1)} %get-tuple-element.59), channel_id=1, source_target_pairs={{1,2},{2,1},{3,4},{4,3},{5,6},{6,5},{7,8},{8,7},{9,10},{10,9},{11,... | collective-permute-start | bytes 1572872 | tf_op jit(solution)/shard_map/ppermute | solution.py:470
  125.4 4.1 %partner_near_grads.1 = (bf16[256,1536]{1,0:T(8,128)(2,1)S(1)}, bf16[256,1536]{1,0:T(8,128)(2,1)S(1)}, bf16[512,512]{1,0:T(8,128)(2,1)S(1)}) custom-call(s32[114]{0:T(128)S(1)} %pad_add_fusion.sc, bf16[256,1536]{1,0:T(8,128)(2,1)S(1)} %get-tuple-element.49.knp, bf16[256,1536]{1,0:T(8,128)(2,1)} %collective-permute-done.2.vp, ...), custom_call_target="tpu_custom_call" | custom-call | flops 5000000000 | bytes 5000000000 | tf_op jit(solution)/shard_map/partner_near_grads/pallas_call | solution.py:440
  129.5 4.5 %collective-permute-start.16 = (bf16[512,512]{1,0:T(8,128)(2,1)S(1)}, bf16[512,512]{1,0:T(8,128)(2,1)S(1)}, u32[]{:S(2)}, u32[]{:S(2)}) collective-permute-start(bf16[512,512]{1,0:T(8,128)(2,1)S(1)} %get-tuple-element.62), channel_id=1, source_target_pairs={{1,2},{2,1},{3,4},{4,3},{5,6},{6,5},{7,8},{8,7},{9,10},{10,9},{11,... | collective-permute-start | bytes 1572872 | tf_op jit(solution)/shard_map/ppermute | solution.py:470
  134.0 1.9 %partner_far_grads.4._ = bf16[512,256]{1,0:T(8,128)(2,1)S(1)} custom-call(s32[114]{0:T(128)S(1)} %pad_add_fusion.sc, bf16[256,1536]{1,0:T(8,128)(2,1)S(1)} %get-tuple-element.49.knp, bf16[256,1536]{1,0:T(8,128)(2,1)} %collective-permute-done.2.vp, bf16[512,256]{1,0:T(8,128)(2,1)S(1)} %collective-permute-done.10.both.refs_0_, ...), custom_call_target="tpu_custom_call" | custom-call | flops 20000000000 | bytes 20000000000 | tf_op jit(solution)/shard_map/partner_far_grads/pallas_call | solution.py:440
  137.8 4.9 %collective-permute-start.17 = (bf16[512,256]{1,0:T(8,128)(2,1)S(1)}, bf16[512,256]{1,0:T(8,128)(2,1)S(1)}, u32[]{:S(2)}, u32[]{:S(2)}) collective-permute-start(bf16[512,256]{1,0:T(8,128)(2,1)S(1)} %get-tuple-element.63), channel_id=1, source_target_pairs={{1,2},{2,1},{3,4},{4,3},{5,6},{6,5},{7,8},{8,7},{9,10},{10,9},{11,... | collective-permute-start | bytes 786440 | tf_op jit(solution)/shard_map/ppermute | solution.py:470
  143.9 2.2 %partner_far_grads.5._ = bf16[512,512]{1,0:T(8,128)(2,1)S(1)} custom-call(s32[114]{0:T(128)S(1)} %pad_add_fusion.sc, bf16[256,1536]{1,0:T(8,128)(2,1)S(1)} %get-tuple-element.49.knp, bf16[256,1536]{1,0:T(8,128)(2,1)} %collective-permute-done.2.vp, bf16[512,512]{1,0:T(8,128)(2,1)S(1)} %collective-permute-done.15.both.refs_1_, ...), custom_call_target="tpu_custom_call" | custom-call | flops 20000000000 | bytes 20000000000 | tf_op jit(solution)/shard_map/partner_far_grads/pallas_call | solution.py:440
  146.3 2.5 %finish_queries.1._.__ = bf16[256,1536]{1,0:T(8,128)(2,1)} custom-call(f32[2,128]{1,0:T(2,128)S(1)} %bitcast.27, f32[1536,256]{1,0:T(8,128)S(1)} %get-tuple-element.55._.dqt, bf16[1536,256]{1,0:T(8,128)(2,1)S(1)} %collective-permute-done.14.dqr, bf16[256,1536]{1,0:T(8,128)(2,1)S(1)} %bitcast.30, bf16[512,512]{1,0:T(8,128)(2,1)S(1)} %partner_far_grads.5._), custom_call_target="tpu_custom_call" | custom-call | flops 20000000000 | bytes 20000000000 | tf_op jit(solution)/shard_map/finish_queries/pallas_call | solution.py:440
  148.7 4.0 %collective-permute-done.16.both.refs_2_ = bf16[512,512]{1,0:T(8,128)(2,1)S(1)} collective-permute-done((bf16[512,512]{1,0:T(8,128)(2,1)S(1)}, bf16[512,512]{1,0:T(8,128)(2,1)S(1)}, u32[]{:S(2)}, u32[]{:S(2)}) %collective-permute-start.16) | collective-permute-done | bytes 524320 | tf_op jit(solution)/shard_map/ppermute | solution.py:470
  153.9 2.2 %partner_far_grads.6._.__ = bf16[512,512]{1,0:T(8,128)(2,1)S(1)} custom-call(s32[114]{0:T(128)S(1)} %pad_add_fusion.sc, bf16[256,1536]{1,0:T(8,128)(2,1)S(1)} %get-tuple-element.49.knp, bf16[256,1536]{1,0:T(8,128)(2,1)} %collective-permute-done.2.vp, bf16[512,512]{1,0:T(8,128)(2,1)S(1)} %collective-permute-done.16.both.refs_2_, ...), custom_call_target="tpu_custom_call" | custom-call | flops 20000000000 | bytes 20000000000 | tf_op jit(solution)/shard_map/partner_far_grads/pallas_call | solution.py:440
  156.2 1.9 %partner_far_grads.7.refs_4_ = bf16[512,256]{1,0:T(8,128)(2,1)S(1)} custom-call(s32[114]{0:T(128)S(1)} %pad_add_fusion.sc, bf16[256,1536]{1,0:T(8,128)(2,1)S(1)} %get-tuple-element.49.knp, bf16[256,1536]{1,0:T(8,128)(2,1)} %collective-permute-done.2.vp, bf16[512,256]{1,0:T(8,128)(2,1)S(1)} %collective-permute-done.17.both.refs_3_, ...), custom_call_target="tpu_custom_call" | custom-call | flops 20000000000 | bytes 20000000000 | tf_op jit(solution)/shard_map/partner_far_grads/pallas_call | solution.py:440
  158.1 2.3 %collective-permute-start.21 = (bf16[512,256]{1,0:T(8,128)(2,1)S(1)}, bf16[512,256]{1,0:T(8,128)(2,1)S(1)}, u32[]{:S(2)}, u32[]{:S(2)}) collective-permute-start(bf16[512,256]{1,0:T(8,128)(2,1)S(1)} %partner_far_grads.7.refs_4_), channel_id=1, source_target_pairs={{0,1},{1,0},{2,3},{3,2},{4,5},{5,4},{6,7},{7,6},{8,9},{9,8},{10,11... | collective-permute-start | bytes 786440 | tf_op jit(solution)/shard_map/ppermute | solution.py:467
  160.5 7.7 %own_key_grads.1 = (f32[256,1536]{1,0:T(8,128)S(1)}, f32[256,1536]{1,0:T(8,128)S(1)}) custom-call(s32[114]{0:T(128)S(1)} %pad_add_fusion.sc, bf16[256,1536]{1,0:T(8,128)(2,1)S(1)} %copy-done.6, bf16[256,1536]{1,0:T(8,128)(2,1)S(1)} %bitcast.23, bf16[256,1536]{1,0:T(8,128)(2,1)S(1)} %collective-permute-done.qn.qs.qnp, ...), custom_call_target="tpu_custom_call" | custom-call | flops 20000000000 | bytes 20000000000 | tf_op jit(solution)/shard_map/own_key_grads/pallas_call | solution.py:440
  168.2 4.7 %collective-permute-done.21.refs_3_ = bf16[512,256]{1,0:T(8,128)(2,1)S(1)} collective-permute-done((bf16[512,256]{1,0:T(8,128)(2,1)S(1)}, bf16[512,256]{1,0:T(8,128)(2,1)S(1)}, u32[]{:S(2)}, u32[]{:S(2)}) %collective-permute-start.21) | collective-permute-done | bytes 262176 | tf_op jit(solution)/shard_map/ppermute | solution.py:467
  172.8 2.7 %finish_keys.1 = (bf16[256,1536]{1,0:T(8,128)(2,1)}, bf16[256,1536]{1,0:T(8,128)(2,1)}) custom-call(f32[2,128]{1,0:T(2,128)S(1)} %bitcast.28, bf16[256,1536]{1,0:T(8,128)(2,1)S(1)} %bitcast.34, f32[256,1536]{1,0:T(8,128)S(1)} %get-tuple-element.64.dk, f32[256,1536]{1,0:T(8,128)S(1)} %get-tuple-element.65.dv, ...), custom_call_target="tpu_custom_call" | custom-call | flops 20000000000 | bytes 20000000000 | tf_op jit(solution)/shard_map/finish_keys/pallas_call | solution.py:440
  (66 shorter events, 16.3 us)
Async XLA Ops:
  0.6 40.5 %collective-permute-start.2 = (bf16[256,1536]{1,0:T(8,128)(2,1)}, bf16[256,1536]{1,0:T(8,128)(2,1)}, u32[]{:S(2)}, u32[]{:S(2)}) collective-permute-start(bf16[256,1536]{1,0:T(8,128)(2,1)} %bitcast.19), channel_id=1, source_target_pairs={{0,1},{1,0},{2,3},{3,2},{4,5},{5,4},{6,7},{7,6},{8,9},{9,8},{10,11... | collective-permute-start | bytes 2359304 | tf_op jit(solution)/shard_map/ppermute | solution.py:467
  2.6 40.2 %collective-permute-start.4 = (bf16[256,1536]{1,0:T(8,128)(2,1)}, bf16[256,1536]{1,0:T(8,128)(2,1)S(1)}, u32[]{:S(2)}, u32[]{:S(2)}) collective-permute-start(bf16[256,1536]{1,0:T(8,128)(2,1)} %bitcast.20), channel_id=1, source_target_pairs={{1,2},{2,1},{3,4},{4,3},{5,6},{6,5},{7,8},{8,7},{9,10},{10,9},{11,... | collective-permute-start | bytes 2359304 | tf_op jit(solution)/shard_map/ppermute | solution.py:470
  9.3 38.5 %collective-permute-start.1 = (bf16[256,1536]{1,0:T(8,128)(2,1)}, bf16[256,1536]{1,0:T(8,128)(2,1)}, u32[]{:S(2)}, u32[]{:S(2)}) collective-permute-start(bf16[256,1536]{1,0:T(8,128)(2,1)} %bitcast.31), channel_id=1, source_target_pairs={{0,1},{1,0},{2,3},{3,2},{4,5},{5,4},{6,7},{7,6},{8,9},{9,8},{10,11... | collective-permute-start | bytes 2359304 | tf_op jit(solution)/shard_map/ppermute | solution.py:467
  9.4 43.0 %collective-permute-start.3 = (bf16[256,1536]{1,0:T(8,128)(2,1)}, bf16[256,1536]{1,0:T(8,128)(2,1)}, u32[]{:S(2)}, u32[]{:S(2)}) collective-permute-start(bf16[256,1536]{1,0:T(8,128)(2,1)} %bitcast.32), channel_id=1, source_target_pairs={{1,2},{2,1},{3,4},{4,3},{5,6},{6,5},{7,8},{8,7},{9,10},{10,9},{11,... | collective-permute-start | bytes 2359304 | tf_op jit(solution)/shard_map/ppermute | solution.py:470
  33.9 1.1 copy-start
  37.3 3.6 %copy-start.14 = (s32[16,6]{0,1:T(8,128)S(1)}, s32[16,6]{0,1:T(8,128)}, u32[]{:S(2)}) copy-start(s32[16,6]{0,1:T(8,128)} %param.13) | copy-start | bytes 1156
  37.3 3.7 %copy-start.15 = (s32[16]{0:T(128)S(1)}, s32[16]{0:T(128)}, u32[]{:S(2)}) copy-start(s32[16]{0:T(128)} %param.12) | copy-start | bytes 196
  37.3 15.0 %copy-start.1 = (bf16[1,256,1536]{2,1,0:T(8,128)(2,1)S(1)}, bf16[1,256,1536]{2,1,0:T(8,128)(2,1)}, u32[]{:S(2)}) copy-start(bf16[1,256,1536]{2,1,0:T(8,128)(2,1)} %param.10) | copy-start | bytes 2359300
  40.5 26.0 %collective-permute-start = (bf16[256,1536]{1,0:T(8,128)(2,1)S(1)}, bf16[256,1536]{1,0:T(8,128)(2,1)S(1)}, u32[]{:S(2)}, u32[]{:S(2)}) collective-permute-start(bf16[256,1536]{1,0:T(8,128)(2,1)S(1)} %get-tuple-element.36.qn), channel_id=1, source_target_pairs={{0,1},{1,0},{2,3},{3,2},{4,5},{5,4},{6,7},{7,6},{8,9},{9,8},{10,11... | collective-permute-start | bytes 2359304 | tf_op jit(solution)/shard_map/ppermute | solution.py:467
  41.1 36.0 %collective-permute-start.7 = (bf16[256,1536]{1,0:T(8,128)(2,1)}, bf16[256,1536]{1,0:T(8,128)(2,1)S(1)}, u32[]{:S(2)}, u32[]{:S(2)}) collective-permute-start(bf16[256,1536]{1,0:T(8,128)(2,1)} %copy-done.11), channel_id=1, source_target_pairs={{0,1},{1,0},{2,3},{3,2},{4,5},{5,4},{6,7},{7,6},{8,9},{9,8},{10,11... | collective-permute-start | bytes 2359304 | tf_op jit(solution)/shard_map/ppermute | solution.py:467
  42.9 34.3 %collective-permute-start.6 = (bf16[256,1536]{1,0:T(8,128)(2,1)}, bf16[256,1536]{1,0:T(8,128)(2,1)S(1)}, u32[]{:S(2)}, u32[]{:S(2)}) collective-permute-start(bf16[256,1536]{1,0:T(8,128)(2,1)} %collective-permute-done.2.vp), channel_id=1, source_target_pairs={{1,2},{2,1},{3,4},{4,3},{5,6},{6,5},{7,8},{8,7},{9,10},{10,9},{11,... | collective-permute-start | bytes 2359304 | tf_op jit(solution)/shard_map/ppermute | solution.py:470
  47.8 38.0 %collective-permute-start.5 = (bf16[256,1536]{1,0:T(8,128)(2,1)}, bf16[256,1536]{1,0:T(8,128)(2,1)S(1)}, u32[]{:S(2)}, u32[]{:S(2)}) collective-permute-start(bf16[256,1536]{1,0:T(8,128)(2,1)} %collective-permute-done.1.kp), channel_id=1, source_target_pairs={{1,2},{2,1},{3,4},{4,3},{5,6},{6,5},{7,8},{8,7},{9,10},{10,9},{11,... | collective-permute-start | bytes 2359304 | tf_op jit(solution)/shard_map/ppermute | solution.py:470
  52.3 1.1 copy-start.2
  61.5 54.3 %collective-permute-start.12 = (bf16[256,1536]{1,0:T(8,128)(2,1)S(1)}, bf16[256,1536]{1,0:T(8,128)(2,1)S(1)}, u32[]{:S(2)}, u32[]{:S(2)}) collective-permute-start(bf16[256,1536]{1,0:T(8,128)(2,1)S(1)} %get-tuple-element.52), channel_id=1, source_target_pairs={{1,2},{2,1},{3,4},{4,3},{5,6},{6,5},{7,8},{8,7},{9,10},{10,9},{11,... | collective-permute-start | bytes 2359304 | tf_op jit(solution)/shard_map/ppermute | solution.py:470
  66.5 53.9 %collective-permute-start.13 = (bf16[256,1536]{1,0:T(8,128)(2,1)S(1)}, bf16[256,1536]{1,0:T(8,128)(2,1)S(1)}, u32[]{:S(2)}, u32[]{:S(2)}) collective-permute-start(bf16[256,1536]{1,0:T(8,128)(2,1)S(1)} %get-tuple-element.53), channel_id=1, source_target_pairs={{1,2},{2,1},{3,4},{4,3},{5,6},{6,5},{7,8},{8,7},{9,10},{10,9},{11,... | collective-permute-start | bytes 2359304 | tf_op jit(solution)/shard_map/ppermute | solution.py:470
  93.4 4.9 %collective-permute-start.8 = (f32[72,256]{1,0:T(8,128)S(1)}, f32[72,256]{1,0:T(8,128)S(1)}, u32[]{:S(2)}, u32[]{:S(2)}) collective-permute-start(f32[72,256]{1,0:T(8,128)S(1)} %get-tuple-element.45.mine), channel_id=1, source_target_pairs={{0,1},{1,0},{2,3},{3,2},{4,5},{5,4},{6,7},{7,6},{8,9},{9,8},{10,11... | collective-permute-start | bytes 221192 | tf_op jit(solution)/shard_map/ppermute | solution.py:467
  98.5 35.5 %collective-permute-start.9 = (bf16[1536,256]{1,0:T(8,128)(2,1)S(1)}, bf16[1536,256]{1,0:T(8,128)(2,1)S(1)}, u32[]{:S(2)}, u32[]{:S(2)}) collective-permute-start(bf16[1536,256]{1,0:T(8,128)(2,1)S(1)} %get-tuple-element.48), channel_id=1, source_target_pairs={{0,1},{1,0},{2,3},{3,2},{4,5},{5,4},{6,7},{7,6},{8,9},{9,8},{10,11... | collective-permute-start | bytes 2359304 | tf_op jit(solution)/shard_map/ppermute | solution.py:467
  98.6 9.4 %copy-start.3 = (bf16[1,256,1536]{2,1,0:T(8,128)(2,1)S(1)}, bf16[1,256,1536]{2,1,0:T(8,128)(2,1)}, u32[]{:S(2)}) copy-start(bf16[1,256,1536]{2,1,0:T(8,128)(2,1)} %param.9) | copy-start | bytes 2359300
  98.6 9.4 %copy-start.6 = (bf16[256,1536]{1,0:T(8,128)(2,1)S(1)}, bf16[256,1536]{1,0:T(8,128)(2,1)}, u32[]{:S(2)}) copy-start(bf16[256,1536]{1,0:T(8,128)(2,1)} %copy-done.4) | copy-start | bytes 2359300
  98.6 26.8 %collective-permute-start.11 = (f32[48,256]{1,0:T(8,128)S(1)}, f32[48,256]{1,0:T(8,128)S(1)}, u32[]{:S(2)}, u32[]{:S(2)}) collective-permute-start(f32[48,256]{1,0:T(8,128)S(1)} %get-tuple-element.50.st), channel_id=1, source_target_pairs={{1,2},{2,1},{3,4},{4,3},{5,6},{6,5},{7,8},{8,7},{9,10},{10,9},{11,... | collective-permute-start | bytes 147464 | tf_op jit(solution)/shard_map/ppermute | solution.py:470
  107.7 38.5 %collective-permute-start.14 = (bf16[1536,256]{1,0:T(8,128)(2,1)S(1)}, bf16[1536,256]{1,0:T(8,128)(2,1)S(1)}, u32[]{:S(2)}, u32[]{:S(2)}) collective-permute-start(bf16[1536,256]{1,0:T(8,128)(2,1)S(1)} %get-tuple-element.54._), channel_id=1, source_target_pairs={{0,1},{1,0},{2,3},{3,2},{4,5},{5,4},{6,7},{7,6},{8,9},{9,8},{10,11... | collective-permute-start | bytes 2359304 | tf_op jit(solution)/shard_map/ppermute | solution.py:467
  115.9 18.1 %collective-permute-start.10 = (bf16[512,256]{1,0:T(8,128)(2,1)S(1)}, bf16[512,256]{1,0:T(8,128)(2,1)S(1)}, u32[]{:S(2)}, u32[]{:S(2)}) collective-permute-start(bf16[512,256]{1,0:T(8,128)(2,1)S(1)} %get-tuple-element.51), channel_id=1, source_target_pairs={{1,2},{2,1},{3,4},{4,3},{5,6},{6,5},{7,8},{8,7},{9,10},{10,9},{11,... | collective-permute-start | bytes 786440 | tf_op jit(solution)/shard_map/ppermute | solution.py:470
  120.4 22.3 %collective-permute-start.15 = (bf16[512,512]{1,0:T(8,128)(2,1)S(1)}, bf16[512,512]{1,0:T(8,128)(2,1)S(1)}, u32[]{:S(2)}, u32[]{:S(2)}) collective-permute-start(bf16[512,512]{1,0:T(8,128)(2,1)S(1)} %get-tuple-element.59), channel_id=1, source_target_pairs={{1,2},{2,1},{3,4},{4,3},{5,6},{6,5},{7,8},{8,7},{9,10},{10,9},{11,... | collective-permute-start | bytes 1572872 | tf_op jit(solution)/shard_map/ppermute | solution.py:470
  129.5 23.3 %collective-permute-start.16 = (bf16[512,512]{1,0:T(8,128)(2,1)S(1)}, bf16[512,512]{1,0:T(8,128)(2,1)S(1)}, u32[]{:S(2)}, u32[]{:S(2)}) collective-permute-start(bf16[512,512]{1,0:T(8,128)(2,1)S(1)} %get-tuple-element.62), channel_id=1, source_target_pairs={{1,2},{2,1},{3,4},{4,3},{5,6},{6,5},{7,8},{8,7},{9,10},{10,9},{11,... | collective-permute-start | bytes 1572872 | tf_op jit(solution)/shard_map/ppermute | solution.py:470
  135.9 32.3 %collective-permute-start.18 = (bf16[512,256]{1,0:T(8,128)(2,1)S(1)}, bf16[512,256]{1,0:T(8,128)(2,1)S(1)}, u32[]{:S(2)}, u32[]{:S(2)}) collective-permute-start(bf16[512,256]{1,0:T(8,128)(2,1)S(1)} %partner_far_grads.4._), channel_id=1, source_target_pairs={{0,1},{1,0},{2,3},{3,2},{4,5},{5,4},{6,7},{7,6},{8,9},{9,8},{10,11... | collective-permute-start | bytes 786440 | tf_op jit(solution)/shard_map/ppermute | solution.py:467
  137.8 18.5 %collective-permute-start.17 = (bf16[512,256]{1,0:T(8,128)(2,1)S(1)}, bf16[512,256]{1,0:T(8,128)(2,1)S(1)}, u32[]{:S(2)}, u32[]{:S(2)}) collective-permute-start(bf16[512,256]{1,0:T(8,128)(2,1)S(1)} %get-tuple-element.63), channel_id=1, source_target_pairs={{1,2},{2,1},{3,4},{4,3},{5,6},{6,5},{7,8},{8,7},{9,10},{10,9},{11,... | collective-permute-start | bytes 786440 | tf_op jit(solution)/shard_map/ppermute | solution.py:470
  142.7 1.1 copy-start.12
  143.9 2.4 %copy-start.8 = (bf16[1,256,1536]{2,1,0:T(8,128)(2,1)S(1)}, bf16[1,256,1536]{2,1,0:T(8,128)(2,1)}, u32[]{:S(2)}) copy-start(bf16[1,256,1536]{2,1,0:T(8,128)(2,1)} %param.7) | copy-start | bytes 2359300
  146.1 26.7 %collective-permute-start.19 = (bf16[512,512]{1,0:T(8,128)(2,1)S(1)}, bf16[512,512]{1,0:T(8,128)(2,1)S(1)}, u32[]{:S(2)}, u32[]{:S(2)}) collective-permute-start(bf16[512,512]{1,0:T(8,128)(2,1)S(1)} %partner_far_grads.5._), channel_id=1, source_target_pairs={{0,1},{1,0},{2,3},{3,2},{4,5},{5,4},{6,7},{7,6},{8,9},{9,8},{10,11... | collective-permute-start | bytes 1572872 | tf_op jit(solution)/shard_map/ppermute | solution.py:467
  156.1 16.7 %collective-permute-start.20 = (bf16[512,512]{1,0:T(8,128)(2,1)S(1)}, bf16[512,512]{1,0:T(8,128)(2,1)S(1)}, u32[]{:S(2)}, u32[]{:S(2)}) collective-permute-start(bf16[512,512]{1,0:T(8,128)(2,1)S(1)} %partner_far_grads.6._.__), channel_id=1, source_target_pairs={{0,1},{1,0},{2,3},{3,2},{4,5},{5,4},{6,7},{7,6},{8,9},{9,8},{10,11... | collective-permute-start | bytes 1572872 | tf_op jit(solution)/shard_map/ppermute | solution.py:467
  158.1 14.7 %collective-permute-start.21 = (bf16[512,256]{1,0:T(8,128)(2,1)S(1)}, bf16[512,256]{1,0:T(8,128)(2,1)S(1)}, u32[]{:S(2)}, u32[]{:S(2)}) collective-permute-start(bf16[512,256]{1,0:T(8,128)(2,1)S(1)} %partner_far_grads.7.refs_4_), channel_id=1, source_target_pairs={{0,1},{1,0},{2,3},{3,2},{4,5},{5,4},{6,7},{7,6},{8,9},{9,8},{10,11... | collective-permute-start | bytes 786440 | tf_op jit(solution)/shard_map/ppermute | solution.py:467
  160.4 12.4 %copy-start.10 = (bf16[1,256,1536]{2,1,0:T(8,128)(2,1)S(1)}, bf16[1,256,1536]{2,1,0:T(8,128)(2,1)}, u32[]{:S(2)}) copy-start(bf16[1,256,1536]{2,1,0:T(8,128)(2,1)} %param.8) | copy-start | bytes 2359300
  (6 other events, 6.3 us)

commit v5 on v4

--- a/solution.py
+++ b/solution.py
@@ -282,8 +282,8 @@
                 sh_ref[heads:] = w2
 
 
-def merge(acc_ref, sh, o_ret, qs, ds, _, att_ref, both_out):
-    stack(both_out, qs, ds)
+def merge(acc_ref, sh, o_ret, _, att_ref, token):
+    clear(token)
     step = pl.program_id(0)
     heads = pl.num_programs(0) * HB
     for j in range(HB):
@@ -386,7 +386,8 @@
             )
 
 
-def finish_queries(g, dqt, dqr, q, _, dq_out):
+def finish_queries(g, dqt, dqr, q, qs, ds, _, dq_out, both_out):
+    stack(both_out, qs, ds)
     scale = 1.0 / math.sqrt(HD)
     for j in range(HB):
         c = cols(j)
@@ -550,18 +551,18 @@
         )
         back += across(last)
         if i == 0:
-            att, sent3 = run(
-                merge, (), [(TALL, acc), (FULL, shares), (TALL, o_ret)] + send(3) + [(ORDER, last)],
-                [wide_bf, pairs[3]], (), chunks,
+            att, last = run(
+                merge, (), [(TALL, acc), (FULL, shares), (TALL, o_ret), (ORDER, last)],
+                [wide_bf, (FULL, (8, HD), F32)], (), chunks,
+            )
+        if i == 1:
+            dq_out, sent3 = run(
+                finish_queries, (),
+                gain + [(TALL, dqt), (TALL, dqr)] + wide(q) + send(3) + [(ORDER, last)],
+                [wide_bf, pairs[3]],
             )
             far += beyond(sent3)
-            last = att
-        if i == 1:
-            (dq_out,) = run(
-                finish_queries, (),
-                gain + [(TALL, dqt), (TALL, dqr)] + wide(q) + [(ORDER, last)], [wide_bf],
-            )
-            last = dq_out
+            last = sent3
     dk, dv = run(
         own_key_grads, scalars,
         wide(knx, v, qnp, dop) + [(FULL, st)] + wide(qne, doe) + [(FULL, ste)]

time: 176 us -> 174 us (0.989)
  starting transfers between devices: 60.6 us -> 57.9 us
  waiting for transfers between devices: 28.3 us -> 31 us
  local copies, waits for them, and re-layouts: 9.96 us -> 7.7 us
    ppermute x11, waiting for transfers between devices: 12.7 us -> 17.9 us  [beyond(): return [lax.ppermute(value, 'ctx', outer) for value in values]]
    ppermute x11, waiting for transfers between devices: 15.6 us -> 13.1 us  [across(): return [lax.ppermute(value, 'ctx', inner) for value in values]]
    unnamed x34 -> x30, local copies, waits for them, and re-layouts: 9.87 us -> 7.61 us
    ppermute x11, starting transfers between devices: 7.22 us -> 5.21 us  [across(): return [lax.ppermute(value, 'ctx', inner) for value in values]]
  transfers between devices with their start and end apart: 22 -> 22, of which waited for: 5 -> 7; matrix products, arithmetic and copies ran while one was open for 0% -> 0% of each run, Pallas kernels for 30% -> 30%
where the time goes in v5:
time: 174 us; the launch traced here: 173 us
  starting transfers between devices  57.9 us (33%)
  Pallas kernels  54.9 us (32%)
  waiting for transfers between devices  31 us (18%)
  blocking collectives  20.6 us (12%)
  local copies, waits for them, and re-layouts  7.7 us (4%)
    pallas_call x16, Pallas kernels, run(): pl.pallas_call(body, name=name or body.__name__, grid_spec=grid_spec, out...  54.9 us
    ppermute x11, starting transfers between devices, beyond(): return [lax.ppermute(value, 'ctx', outer) for value in values]  52.7 us
    all_gather x1, blocking collectives, local(): g = lax.all_gather(gains, 'fsdp', axis=1, tiled=True)  20.6 us
    ppermute x11, waiting for transfers between devices, beyond(): return [lax.ppermute(value, 'ctx', outer) for value in values]  17.9 us
    ppermute x11, waiting for transfers between devices, across(): return [lax.ppermute(value, 'ctx', inner) for value in values]  13.1 us
    unnamed x30, local copies, waits for them, and re-layouts  7.61 us
    ppermute x11, starting transfers between devices, across(): return [lax.ppermute(value, 'ctx', inner) for value in values]  5.21 us
  transfers between devices with their start and end apart: 22, of which 7 were waited for; matrix products, arithmetic and copies ran while one was open for 0% of the time, Pallas kernels for 30%

profile of v5, /device:TPU:16, one launch (start us, length us, event | category | flops | bytes accessed | tf_op | source)
XLA Modules:
  0.0 173.2 jit_solution(18163382956122449512)
XLA Ops:
  0.6 2.0 %collective-permute-start.2 = (bf16[256,1536]{1,0:T(8,128)(2,1)}, bf16[256,1536]{1,0:T(8,128)(2,1)}, u32[]{:S(2)}, u32[]{:S(2)}) collective-permute-start(bf16[256,1536]{1,0:T(8,128)(2,1)} %bitcast.19), channel_id=1, source_target_pairs={{0,1},{1,0},{2,3},{3,2},{4,5},{5,4},{6,7},{7,6},{8,9},{9,8},{10,11... | collective-permute-start | bytes 2359304 | tf_op jit(solution)/shard_map/ppermute | solution.py:468
  2.6 6.6 %collective-permute-start.4 = (bf16[256,1536]{1,0:T(8,128)(2,1)}, bf16[256,1536]{1,0:T(8,128)(2,1)S(1)}, u32[]{:S(2)}, u32[]{:S(2)}) collective-permute-start(bf16[256,1536]{1,0:T(8,128)(2,1)} %bitcast.20), channel_id=1, source_target_pairs={{1,2},{2,1},{3,4},{4,3},{5,6},{6,5},{7,8},{8,7},{9,10},{10,9},{11,... | collective-permute-start | bytes 2359304 | tf_op jit(solution)/shard_map/ppermute | solution.py:471
  9.4 3.9 %collective-permute-start.3 = (bf16[256,1536]{1,0:T(8,128)(2,1)}, bf16[256,1536]{1,0:T(8,128)(2,1)}, u32[]{:S(2)}, u32[]{:S(2)}) collective-permute-start(bf16[256,1536]{1,0:T(8,128)(2,1)} %bitcast.32), channel_id=1, source_target_pairs={{1,2},{2,1},{3,4},{4,3},{5,6},{6,5},{7,8},{8,7},{9,10},{10,9},{11,... | collective-permute-start | bytes 2359304 | tf_op jit(solution)/shard_map/ppermute | solution.py:471
  13.3 20.6 %all-gather = f32[16,8,2]{1,2,0:T(2,128)S(1)} all-gather(f32[1,8,2]{1,2,0:T(2,128)} %bitcast.35), channel_id=1, replica_groups=mesh['fsdp'=16,'ctx'=16] {'fsdp'}, dimensions={0}, use_global_device_ids=true | all-gather | bytes 1088 | tf_op jit(solution)/shard_map/all_gather | solution.py:487
  42.9 4.9 %collective-permute-start.6 = (bf16[256,1536]{1,0:T(8,128)(2,1)}, bf16[256,1536]{1,0:T(8,128)(2,1)S(1)}, u32[]{:S(2)}, u32[]{:S(2)}) collective-permute-start(bf16[256,1536]{1,0:T(8,128)(2,1)} %collective-permute-done.2.vp), channel_id=1, source_target_pairs={{1,2},{2,1},{3,4},{4,3},{5,6},{6,5},{7,8},{8,7},{9,10},{10,9},{11,... | collective-permute-start | bytes 2359304 | tf_op jit(solution)/shard_map/ppermute | solution.py:471
  47.8 4.5 %collective-permute-start.5 = (bf16[256,1536]{1,0:T(8,128)(2,1)}, bf16[256,1536]{1,0:T(8,128)(2,1)S(1)}, u32[]{:S(2)}, u32[]{:S(2)}) collective-permute-start(bf16[256,1536]{1,0:T(8,128)(2,1)} %collective-permute-done.1.kp), channel_id=1, source_target_pairs={{1,2},{2,1},{3,4},{4,3},{5,6},{6,5},{7,8},{8,7},{9,10},{10,9},{11,... | collective-permute-start | bytes 2359304 | tf_op jit(solution)/shard_map/ppermute | solution.py:471
  54.6 7.0 %own_forward.1 = (f32[1536,256]{1,0:T(8,128)S(1)}, f32[24,256]{1,0:T(8,128)S(1)}, bf16[256,1536]{1,0:T(8,128)(2,1)S(1)}, bf16[256,1536]{1,0:T(8,128)(2,1)S(1)}, ...) custom-call(s32[114]{0:T(128)S(1)} %pad_add_fusion.sc, f32[2,128]{1,0:T(2,128)S(1)} %bitcast.25, ...), custom_call_target="tpu_custom_call" | custom-call | flops 20000000000 | bytes 20000000000 | tf_op jit(solution)/shard_map/own_forward/pallas_call | solution.py:441
  61.6 5.0 %collective-permute-start.12 = (bf16[256,1536]{1,0:T(8,128)(2,1)S(1)}, bf16[256,1536]{1,0:T(8,128)(2,1)S(1)}, u32[]{:S(2)}, u32[]{:S(2)}) collective-permute-start(bf16[256,1536]{1,0:T(8,128)(2,1)S(1)} %get-tuple-element.54), channel_id=1, source_target_pairs={{1,2},{2,1},{3,4},{4,3},{5,6},{6,5},{7,8},{8,7},{9,10},{10,9},{11,... | collective-permute-start | bytes 2359304 | tf_op jit(solution)/shard_map/ppermute | solution.py:471
  66.6 4.5 %collective-permute-start.13 = (bf16[256,1536]{1,0:T(8,128)(2,1)S(1)}, bf16[256,1536]{1,0:T(8,128)(2,1)S(1)}, u32[]{:S(2)}, u32[]{:S(2)}) collective-permute-start(bf16[256,1536]{1,0:T(8,128)(2,1)S(1)} %get-tuple-element.55), channel_id=1, source_target_pairs={{1,2},{2,1},{3,4},{4,3},{5,6},{6,5},{7,8},{8,7},{9,10},{10,9},{11,... | collective-permute-start | bytes 2359304 | tf_op jit(solution)/shard_map/ppermute | solution.py:471
  71.1 6.1 %collective-permute-done.7.do.ds.dop = bf16[256,1536]{1,0:T(8,128)(2,1)S(1)} collective-permute-done((bf16[256,1536]{1,0:T(8,128)(2,1)}, bf16[256,1536]{1,0:T(8,128)(2,1)S(1)}, u32[]{:S(2)}, u32[]{:S(2)}) %collective-permute-start.7) | collective-permute-done | bytes 786464 | tf_op jit(solution)/shard_map/ppermute | solution.py:468
  77.1 8.7 %collective-permute-done.5.kf = bf16[256,1536]{1,0:T(8,128)(2,1)S(1)} collective-permute-done((bf16[256,1536]{1,0:T(8,128)(2,1)}, bf16[256,1536]{1,0:T(8,128)(2,1)S(1)}, u32[]{:S(2)}, u32[]{:S(2)}) %collective-permute-start.5) | collective-permute-done | bytes 786464 | tf_op jit(solution)/shard_map/ppermute | solution.py:471
  85.9 4.6 %partner_forward.1 = (bf16[1536,256]{1,0:T(8,128)(2,1)S(1)}, f32[36,256]{1,0:T(8,128)S(1)}, bf16[256,1536]{1,0:T(8,128)(2,1)S(1)}) custom-call(s32[114]{0:T(128)S(1)} %pad_add_fusion.sc, f32[2,128]{1,0:T(2,128)S(1)} %bitcast.26, bf16[256,1536]{1,0:T(8,128)(2,1)S(1)} %collective-permute-done.qn.qs.qnp, bf16[256,1536]{1,0:T(8,128)(2,1)S(1)} %get-tuple-element.40.kne, ...), custom_call_target="tpu_custom_call" | custom-call | tf_op jit(solution)/shard_map/partner_forward/pallas_call | solution.py:441
  90.4 3.0 %own_forward_far.1 = (f32[1536,256]{1,0:T(8,128)S(1)}, f32[72,256]{1,0:T(8,128)S(1)}) custom-call(s32[114]{0:T(128)S(1)} %pad_add_fusion.sc, bf16[256,1536]{1,0:T(8,128)(2,1)S(1)} %get-tuple-element.38.qn, bf16[256,1536]{1,0:T(8,128)(2,1)S(1)} %get-tuple-element.42.knf, bf16[256,1536]{1,0:T(8,128)(2,1)S(1)} %collective-permute-done.6.vf, ...), custom_call_target="tpu_custom_call" | custom-call | tf_op jit(solution)/shard_map/own_forward_far/pallas_call | solution.py:441
  93.6 4.8 %collective-permute-done.8.got = f32[72,256]{1,0:T(8,128)S(1)} collective-permute-done((f32[72,256]{1,0:T(8,128)S(1)}, f32[72,256]{1,0:T(8,128)S(1)}, u32[]{:S(2)}, u32[]{:S(2)}) %collective-permute-start.8) | collective-permute-done | bytes 73760 | tf_op jit(solution)/shard_map/ppermute | solution.py:468
  98.6 5.1 %collective-permute-start.11 = (f32[48,256]{1,0:T(8,128)S(1)}, f32[48,256]{1,0:T(8,128)S(1)}, u32[]{:S(2)}, u32[]{:S(2)}) collective-permute-start(f32[48,256]{1,0:T(8,128)S(1)} %get-tuple-element.52.st), channel_id=1, source_target_pairs={{1,2},{2,1},{3,4},{4,3},{5,6},{6,5},{7,8},{8,7},{9,10},{10,9},{11,... | collective-permute-start | bytes 147464 | tf_op jit(solution)/shard_map/ppermute | solution.py:471
  103.7 4.0 %partner_query_grads.1 = (bf16[1536,256]{1,0:T(8,128)(2,1)S(1)}, bf16[512,256]{1,0:T(8,128)(2,1)S(1)}) custom-call(s32[114]{0:T(128)S(1)} %pad_add_fusion.sc, bf16[256,1536]{1,0:T(8,128)(2,1)S(1)} %collective-permute-done.qn.qs.qnp, bf16[256,1536]{1,0:T(8,128)(2,1)S(1)} %collective-permute-done.7.do.ds.dop, f32[48,256]{1,0:T(8,128)S(1)} %get-tuple-element.52.st, ...), custom_call_target="tpu_custom_call" | custom-call | tf_op jit(solution)/shard_map/partner_query_grads/pallas_call | solution.py:441
  108.0 7.9 %own_query_grads.1 = (f32[1536,256]{1,0:T(8,128)S(1)}, f32[256,1536]{1,0:T(8,128)S(1)}, f32[256,1536]{1,0:T(8,128)S(1)}, bf16[512,512]{1,0:T(8,128)(2,1)S(1)}) custom-call(s32[114]{0:T(128)S(1)} %pad_add_fusion.sc, bf16[256,1536]{1,0:T(8,128)(2,1)S(1)} %get-tuple-element.38.qn, bf16[256,1536]{1,0:T(8,128)(2,1)S(1)} %bitcast.18, ...), custom_call_target="tpu_custom_call" | custom-call | tf_op jit(solution)/shard_map/own_query_grads/pallas_call | solution.py:441
  115.9 4.5 %collective-permute-start.10 = (bf16[512,256]{1,0:T(8,128)(2,1)S(1)}, bf16[512,256]{1,0:T(8,128)(2,1)S(1)}, u32[]{:S(2)}, u32[]{:S(2)}) collective-permute-start(bf16[512,256]{1,0:T(8,128)(2,1)S(1)} %get-tuple-element.53), channel_id=1, source_target_pairs={{1,2},{2,1},{3,4},{4,3},{5,6},{6,5},{7,8},{8,7},{9,10},{10,9},{11,... | collective-permute-start | bytes 786440 | tf_op jit(solution)/shard_map/ppermute | solution.py:471
  120.5 4.9 %collective-permute-start.15 = (bf16[512,512]{1,0:T(8,128)(2,1)S(1)}, bf16[512,512]{1,0:T(8,128)(2,1)S(1)}, u32[]{:S(2)}, u32[]{:S(2)}) collective-permute-start(bf16[512,512]{1,0:T(8,128)(2,1)S(1)} %get-tuple-element.61), channel_id=1, source_target_pairs={{1,2},{2,1},{3,4},{4,3},{5,6},{6,5},{7,8},{8,7},{9,10},{10,9},{11,... | collective-permute-start | bytes 1572872 | tf_op jit(solution)/shard_map/ppermute | solution.py:471
  125.4 4.1 %partner_near_grads.1 = (bf16[256,1536]{1,0:T(8,128)(2,1)S(1)}, bf16[256,1536]{1,0:T(8,128)(2,1)S(1)}, bf16[512,512]{1,0:T(8,128)(2,1)S(1)}) custom-call(s32[114]{0:T(128)S(1)} %pad_add_fusion.sc, bf16[256,1536]{1,0:T(8,128)(2,1)S(1)} %get-tuple-element.51.knp, bf16[256,1536]{1,0:T(8,128)(2,1)} %collective-permute-done.2.vp, ...), custom_call_target="tpu_custom_call" | custom-call | flops 5000000000 | bytes 5000000000 | tf_op jit(solution)/shard_map/partner_near_grads/pallas_call | solution.py:441
  129.5 4.5 %collective-permute-start.16 = (bf16[512,512]{1,0:T(8,128)(2,1)S(1)}, bf16[512,512]{1,0:T(8,128)(2,1)S(1)}, u32[]{:S(2)}, u32[]{:S(2)}) collective-permute-start(bf16[512,512]{1,0:T(8,128)(2,1)S(1)} %get-tuple-element.66), channel_id=1, source_target_pairs={{1,2},{2,1},{3,4},{4,3},{5,6},{6,5},{7,8},{8,7},{9,10},{10,9},{11,... | collective-permute-start | bytes 1572872 | tf_op jit(solution)/shard_map/ppermute | solution.py:471
  134.1 1.9 %partner_far_grads.4._ = bf16[512,256]{1,0:T(8,128)(2,1)S(1)} custom-call(s32[114]{0:T(128)S(1)} %pad_add_fusion.sc, bf16[256,1536]{1,0:T(8,128)(2,1)S(1)} %get-tuple-element.51.knp, bf16[256,1536]{1,0:T(8,128)(2,1)} %collective-permute-done.2.vp, bf16[512,256]{1,0:T(8,128)(2,1)S(1)} %collective-permute-done.10.both.refs_0_, ...), custom_call_target="tpu_custom_call" | custom-call | flops 20000000000 | bytes 20000000000 | tf_op jit(solution)/shard_map/partner_far_grads/pallas_call | solution.py:441
  137.8 3.8 %collective-permute-done.15.both.refs_1_ = bf16[512,512]{1,0:T(8,128)(2,1)S(1)} collective-permute-done((bf16[512,512]{1,0:T(8,128)(2,1)S(1)}, bf16[512,512]{1,0:T(8,128)(2,1)S(1)}, u32[]{:S(2)}, u32[]{:S(2)}) %collective-permute-start.15) | collective-permute-done | bytes 524320 | tf_op jit(solution)/shard_map/ppermute | solution.py:471
  141.6 2.2 %partner_far_grads.5._ = bf16[512,512]{1,0:T(8,128)(2,1)S(1)} custom-call(s32[114]{0:T(128)S(1)} %pad_add_fusion.sc, bf16[256,1536]{1,0:T(8,128)(2,1)S(1)} %get-tuple-element.51.knp, bf16[256,1536]{1,0:T(8,128)(2,1)} %collective-permute-done.2.vp, bf16[512,512]{1,0:T(8,128)(2,1)S(1)} %collective-permute-done.15.both.refs_1_, ...), custom_call_target="tpu_custom_call" | custom-call | flops 20000000000 | bytes 20000000000 | tf_op jit(solution)/shard_map/partner_far_grads/pallas_call | solution.py:441
  143.9 2.5 %finish_queries.1 = (bf16[256,1536]{1,0:T(8,128)(2,1)}, bf16[512,256]{1,0:T(8,128)(2,1)S(1)}) custom-call(f32[2,128]{1,0:T(2,128)S(1)} %bitcast.27, f32[1536,256]{1,0:T(8,128)S(1)} %get-tuple-element.57._.dqt, bf16[1536,256]{1,0:T(8,128)(2,1)S(1)} %collective-permute-done.14.dqr, bf16[256,1536]{1,0:T(8,128)(2,1)S(1)} %bitcast.30, ...), custom_call_target="tpu_custom_call" | custom-call | flops 20000000000 | bytes 20000000000 | tf_op jit(solution)/shard_map/finish_queries/pallas_call | solution.py:441
  146.5 4.2 %collective-permute-start.17 = (bf16[512,256]{1,0:T(8,128)(2,1)S(1)}, bf16[512,256]{1,0:T(8,128)(2,1)S(1)}, u32[]{:S(2)}, u32[]{:S(2)}) collective-permute-start(bf16[512,256]{1,0:T(8,128)(2,1)S(1)} %get-tuple-element.67._.__), channel_id=1, source_target_pairs={{1,2},{2,1},{3,4},{4,3},{5,6},{6,5},{7,8},{8,7},{9,10},{10,9},{11,... | collective-permute-start | bytes 786440 | tf_op jit(solution)/shard_map/ppermute | solution.py:471
  150.9 2.2 %partner_far_grads.6._.__ = bf16[512,512]{1,0:T(8,128)(2,1)S(1)} custom-call(s32[114]{0:T(128)S(1)} %pad_add_fusion.sc, bf16[256,1536]{1,0:T(8,128)(2,1)S(1)} %get-tuple-element.51.knp, bf16[256,1536]{1,0:T(8,128)(2,1)} %collective-permute-done.2.vp, bf16[512,512]{1,0:T(8,128)(2,1)S(1)} %collective-permute-done.16.both.refs_2_, ...), custom_call_target="tpu_custom_call" | custom-call | flops 20000000000 | bytes 20000000000 | tf_op jit(solution)/shard_map/partner_far_grads/pallas_call | solution.py:441
  153.2 5.1 %collective-permute-done.17.both.refs_3_ = bf16[512,256]{1,0:T(8,128)(2,1)S(1)} collective-permute-done((bf16[512,256]{1,0:T(8,128)(2,1)S(1)}, bf16[512,256]{1,0:T(8,128)(2,1)S(1)}, u32[]{:S(2)}, u32[]{:S(2)}) %collective-permute-start.17) | collective-permute-done | bytes 262176 | tf_op jit(solution)/shard_map/ppermute | solution.py:471
  158.3 1.9 %partner_far_grads.7.refs_4_ = bf16[512,256]{1,0:T(8,128)(2,1)S(1)} custom-call(s32[114]{0:T(128)S(1)} %pad_add_fusion.sc, bf16[256,1536]{1,0:T(8,128)(2,1)S(1)} %get-tuple-element.51.knp, bf16[256,1536]{1,0:T(8,128)(2,1)} %collective-permute-done.2.vp, bf16[512,256]{1,0:T(8,128)(2,1)S(1)} %collective-permute-done.17.both.refs_3_, ...), custom_call_target="tpu_custom_call" | custom-call | flops 20000000000 | bytes 20000000000 | tf_op jit(solution)/shard_map/partner_far_grads/pallas_call | solution.py:441
  160.6 7.7 %own_key_grads.1 = (f32[256,1536]{1,0:T(8,128)S(1)}, f32[256,1536]{1,0:T(8,128)S(1)}) custom-call(s32[114]{0:T(128)S(1)} %pad_add_fusion.sc, bf16[256,1536]{1,0:T(8,128)(2,1)S(1)} %copy-done.6, bf16[256,1536]{1,0:T(8,128)(2,1)S(1)} %bitcast.23, bf16[256,1536]{1,0:T(8,128)(2,1)S(1)} %collective-permute-done.qn.qs.qnp, ...), custom_call_target="tpu_custom_call" | custom-call | flops 20000000000 | bytes 20000000000 | tf_op jit(solution)/shard_map/own_key_grads/pallas_call | solution.py:441
  168.3 2.2 %collective-permute-done.21.refs_3_ = bf16[512,256]{1,0:T(8,128)(2,1)S(1)} collective-permute-done((bf16[512,256]{1,0:T(8,128)(2,1)S(1)}, bf16[512,256]{1,0:T(8,128)(2,1)S(1)}, u32[]{:S(2)}, u32[]{:S(2)}) %collective-permute-start.21) | collective-permute-done | bytes 262176 | tf_op jit(solution)/shard_map/ppermute | solution.py:468
  170.5 2.7 %finish_keys.1 = (bf16[256,1536]{1,0:T(8,128)(2,1)}, bf16[256,1536]{1,0:T(8,128)(2,1)}) custom-call(f32[2,128]{1,0:T(2,128)S(1)} %bitcast.28, bf16[256,1536]{1,0:T(8,128)(2,1)S(1)} %bitcast.34, f32[256,1536]{1,0:T(8,128)S(1)} %get-tuple-element.68.dk, f32[256,1536]{1,0:T(8,128)S(1)} %get-tuple-element.69.dv, ...), custom_call_target="tpu_custom_call" | custom-call | flops 20000000000 | bytes 20000000000 | tf_op jit(solution)/shard_map/finish_keys/pallas_call | solution.py:441
  (62 shorter events, 14.6 us)
Async XLA Ops:
  0.6 40.5 %collective-permute-start.2 = (bf16[256,1536]{1,0:T(8,128)(2,1)}, bf16[256,1536]{1,0:T(8,128)(2,1)}, u32[]{:S(2)}, u32[]{:S(2)}) collective-permute-start(bf16[256,1536]{1,0:T(8,128)(2,1)} %bitcast.19), channel_id=1, source_target_pairs={{0,1},{1,0},{2,3},{3,2},{4,5},{5,4},{6,7},{7,6},{8,9},{9,8},{10,11... | collective-permute-start | bytes 2359304 | tf_op jit(solution)/shard_map/ppermute | solution.py:468
  2.6 40.2 %collective-permute-start.4 = (bf16[256,1536]{1,0:T(8,128)(2,1)}, bf16[256,1536]{1,0:T(8,128)(2,1)S(1)}, u32[]{:S(2)}, u32[]{:S(2)}) collective-permute-start(bf16[256,1536]{1,0:T(8,128)(2,1)} %bitcast.20), channel_id=1, source_target_pairs={{1,2},{2,1},{3,4},{4,3},{5,6},{6,5},{7,8},{8,7},{9,10},{10,9},{11,... | collective-permute-start | bytes 2359304 | tf_op jit(solution)/shard_map/ppermute | solution.py:471
  9.3 38.5 %collective-permute-start.1 = (bf16[256,1536]{1,0:T(8,128)(2,1)}, bf16[256,1536]{1,0:T(8,128)(2,1)}, u32[]{:S(2)}, u32[]{:S(2)}) collective-permute-start(bf16[256,1536]{1,0:T(8,128)(2,1)} %bitcast.31), channel_id=1, source_target_pairs={{0,1},{1,0},{2,3},{3,2},{4,5},{5,4},{6,7},{7,6},{8,9},{9,8},{10,11... | collective-permute-start | bytes 2359304 | tf_op jit(solution)/shard_map/ppermute | solution.py:468
  9.4 43.0 %collective-permute-start.3 = (bf16[256,1536]{1,0:T(8,128)(2,1)}, bf16[256,1536]{1,0:T(8,128)(2,1)}, u32[]{:S(2)}, u32[]{:S(2)}) collective-permute-start(bf16[256,1536]{1,0:T(8,128)(2,1)} %bitcast.32), channel_id=1, source_target_pairs={{1,2},{2,1},{3,4},{4,3},{5,6},{6,5},{7,8},{8,7},{9,10},{10,9},{11,... | collective-permute-start | bytes 2359304 | tf_op jit(solution)/shard_map/ppermute | solution.py:471
  33.9 1.1 copy-start
  35.1 1.1 copy-start.7
  37.3 3.6 %copy-start.12 = (s32[16,6]{0,1:T(8,128)S(1)}, s32[16,6]{0,1:T(8,128)}, u32[]{:S(2)}) copy-start(s32[16,6]{0,1:T(8,128)} %param.13) | copy-start | bytes 1156
  37.3 3.7 %copy-start.13 = (s32[16]{0:T(128)S(1)}, s32[16]{0:T(128)}, u32[]{:S(2)}) copy-start(s32[16]{0:T(128)} %param.12) | copy-start | bytes 196
  37.3 15.0 %copy-start.1 = (bf16[1,256,1536]{2,1,0:T(8,128)(2,1)S(1)}, bf16[1,256,1536]{2,1,0:T(8,128)(2,1)}, u32[]{:S(2)}) copy-start(bf16[1,256,1536]{2,1,0:T(8,128)(2,1)} %param.10) | copy-start | bytes 2359300
  40.5 26.0 %collective-permute-start = (bf16[256,1536]{1,0:T(8,128)(2,1)S(1)}, bf16[256,1536]{1,0:T(8,128)(2,1)S(1)}, u32[]{:S(2)}, u32[]{:S(2)}) collective-permute-start(bf16[256,1536]{1,0:T(8,128)(2,1)S(1)} %get-tuple-element.38.qn), channel_id=1, source_target_pairs={{0,1},{1,0},{2,3},{3,2},{4,5},{5,4},{6,7},{7,6},{8,9},{9,8},{10,11... | collective-permute-start | bytes 2359304 | tf_op jit(solution)/shard_map/ppermute | solution.py:468
  41.1 36.0 %collective-permute-start.7 = (bf16[256,1536]{1,0:T(8,128)(2,1)}, bf16[256,1536]{1,0:T(8,128)(2,1)S(1)}, u32[]{:S(2)}, u32[]{:S(2)}) collective-permute-start(bf16[256,1536]{1,0:T(8,128)(2,1)} %copy-done.11), channel_id=1, source_target_pairs={{0,1},{1,0},{2,3},{3,2},{4,5},{5,4},{6,7},{7,6},{8,9},{9,8},{10,11... | collective-permute-start | bytes 2359304 | tf_op jit(solution)/shard_map/ppermute | solution.py:468
  42.9 34.3 %collective-permute-start.6 = (bf16[256,1536]{1,0:T(8,128)(2,1)}, bf16[256,1536]{1,0:T(8,128)(2,1)S(1)}, u32[]{:S(2)}, u32[]{:S(2)}) collective-permute-start(bf16[256,1536]{1,0:T(8,128)(2,1)} %collective-permute-done.2.vp), channel_id=1, source_target_pairs={{1,2},{2,1},{3,4},{4,3},{5,6},{6,5},{7,8},{8,7},{9,10},{10,9},{11,... | collective-permute-start | bytes 2359304 | tf_op jit(solution)/shard_map/ppermute | solution.py:471
  47.8 38.0 %collective-permute-start.5 = (bf16[256,1536]{1,0:T(8,128)(2,1)}, bf16[256,1536]{1,0:T(8,128)(2,1)S(1)}, u32[]{:S(2)}, u32[]{:S(2)}) collective-permute-start(bf16[256,1536]{1,0:T(8,128)(2,1)} %collective-permute-done.1.kp), channel_id=1, source_target_pairs={{1,2},{2,1},{3,4},{4,3},{5,6},{6,5},{7,8},{8,7},{9,10},{10,9},{11,... | collective-permute-start | bytes 2359304 | tf_op jit(solution)/shard_map/ppermute | solution.py:471
  52.3 1.1 copy-start.2
  61.6 54.3 %collective-permute-start.12 = (bf16[256,1536]{1,0:T(8,128)(2,1)S(1)}, bf16[256,1536]{1,0:T(8,128)(2,1)S(1)}, u32[]{:S(2)}, u32[]{:S(2)}) collective-permute-start(bf16[256,1536]{1,0:T(8,128)(2,1)S(1)} %get-tuple-element.54), channel_id=1, source_target_pairs={{1,2},{2,1},{3,4},{4,3},{5,6},{6,5},{7,8},{8,7},{9,10},{10,9},{11,... | collective-permute-start | bytes 2359304 | tf_op jit(solution)/shard_map/ppermute | solution.py:471
  66.6 53.9 %collective-permute-start.13 = (bf16[256,1536]{1,0:T(8,128)(2,1)S(1)}, bf16[256,1536]{1,0:T(8,128)(2,1)S(1)}, u32[]{:S(2)}, u32[]{:S(2)}) collective-permute-start(bf16[256,1536]{1,0:T(8,128)(2,1)S(1)} %get-tuple-element.55), channel_id=1, source_target_pairs={{1,2},{2,1},{3,4},{4,3},{5,6},{6,5},{7,8},{8,7},{9,10},{10,9},{11,... | collective-permute-start | bytes 2359304 | tf_op jit(solution)/shard_map/ppermute | solution.py:471
  93.5 4.9 %collective-permute-start.8 = (f32[72,256]{1,0:T(8,128)S(1)}, f32[72,256]{1,0:T(8,128)S(1)}, u32[]{:S(2)}, u32[]{:S(2)}) collective-permute-start(f32[72,256]{1,0:T(8,128)S(1)} %get-tuple-element.47.mine), channel_id=1, source_target_pairs={{0,1},{1,0},{2,3},{3,2},{4,5},{5,4},{6,7},{7,6},{8,9},{9,8},{10,11... | collective-permute-start | bytes 221192 | tf_op jit(solution)/shard_map/ppermute | solution.py:468
  98.5 35.5 %collective-permute-start.9 = (bf16[1536,256]{1,0:T(8,128)(2,1)S(1)}, bf16[1536,256]{1,0:T(8,128)(2,1)S(1)}, u32[]{:S(2)}, u32[]{:S(2)}) collective-permute-start(bf16[1536,256]{1,0:T(8,128)(2,1)S(1)} %get-tuple-element.50), channel_id=1, source_target_pairs={{0,1},{1,0},{2,3},{3,2},{4,5},{5,4},{6,7},{7,6},{8,9},{9,8},{10,11... | collective-permute-start | bytes 2359304 | tf_op jit(solution)/shard_map/ppermute | solution.py:468
  98.6 9.4 %copy-start.3 = (bf16[1,256,1536]{2,1,0:T(8,128)(2,1)S(1)}, bf16[1,256,1536]{2,1,0:T(8,128)(2,1)}, u32[]{:S(2)}) copy-start(bf16[1,256,1536]{2,1,0:T(8,128)(2,1)} %param.9) | copy-start | bytes 2359300
  98.6 9.4 %copy-start.6 = (bf16[256,1536]{1,0:T(8,128)(2,1)S(1)}, bf16[256,1536]{1,0:T(8,128)(2,1)}, u32[]{:S(2)}) copy-start(bf16[256,1536]{1,0:T(8,128)(2,1)} %copy-done.4) | copy-start | bytes 2359300
  98.6 26.8 %collective-permute-start.11 = (f32[48,256]{1,0:T(8,128)S(1)}, f32[48,256]{1,0:T(8,128)S(1)}, u32[]{:S(2)}, u32[]{:S(2)}) collective-permute-start(f32[48,256]{1,0:T(8,128)S(1)} %get-tuple-element.52.st), channel_id=1, source_target_pairs={{1,2},{2,1},{3,4},{4,3},{5,6},{6,5},{7,8},{8,7},{9,10},{10,9},{11,... | collective-permute-start | bytes 147464 | tf_op jit(solution)/shard_map/ppermute | solution.py:471
  107.7 36.2 %collective-permute-start.14 = (bf16[1536,256]{1,0:T(8,128)(2,1)S(1)}, bf16[1536,256]{1,0:T(8,128)(2,1)S(1)}, u32[]{:S(2)}, u32[]{:S(2)}) collective-permute-start(bf16[1536,256]{1,0:T(8,128)(2,1)S(1)} %get-tuple-element.56._), channel_id=1, source_target_pairs={{0,1},{1,0},{2,3},{3,2},{4,5},{5,4},{6,7},{7,6},{8,9},{9,8},{10,11... | collective-permute-start | bytes 2359304 | tf_op jit(solution)/shard_map/ppermute | solution.py:468
  115.9 18.1 %collective-permute-start.10 = (bf16[512,256]{1,0:T(8,128)(2,1)S(1)}, bf16[512,256]{1,0:T(8,128)(2,1)S(1)}, u32[]{:S(2)}, u32[]{:S(2)}) collective-permute-start(bf16[512,256]{1,0:T(8,128)(2,1)S(1)} %get-tuple-element.53), channel_id=1, source_target_pairs={{1,2},{2,1},{3,4},{4,3},{5,6},{6,5},{7,8},{8,7},{9,10},{10,9},{11,... | collective-permute-start | bytes 786440 | tf_op jit(solution)/shard_map/ppermute | solution.py:471
  120.5 21.1 %collective-permute-start.15 = (bf16[512,512]{1,0:T(8,128)(2,1)S(1)}, bf16[512,512]{1,0:T(8,128)(2,1)S(1)}, u32[]{:S(2)}, u32[]{:S(2)}) collective-permute-start(bf16[512,512]{1,0:T(8,128)(2,1)S(1)} %get-tuple-element.61), channel_id=1, source_target_pairs={{1,2},{2,1},{3,4},{4,3},{5,6},{6,5},{7,8},{8,7},{9,10},{10,9},{11,... | collective-permute-start | bytes 1572872 | tf_op jit(solution)/shard_map/ppermute | solution.py:471
  129.5 21.4 %collective-permute-start.16 = (bf16[512,512]{1,0:T(8,128)(2,1)S(1)}, bf16[512,512]{1,0:T(8,128)(2,1)S(1)}, u32[]{:S(2)}, u32[]{:S(2)}) collective-permute-start(bf16[512,512]{1,0:T(8,128)(2,1)S(1)} %get-tuple-element.66), channel_id=1, source_target_pairs={{1,2},{2,1},{3,4},{4,3},{5,6},{6,5},{7,8},{8,7},{9,10},{10,9},{11,... | collective-permute-start | bytes 1572872 | tf_op jit(solution)/shard_map/ppermute | solution.py:471
  135.9 32.3 %collective-permute-start.18 = (bf16[512,256]{1,0:T(8,128)(2,1)S(1)}, bf16[512,256]{1,0:T(8,128)(2,1)S(1)}, u32[]{:S(2)}, u32[]{:S(2)}) collective-permute-start(bf16[512,256]{1,0:T(8,128)(2,1)S(1)} %partner_far_grads.4._), channel_id=1, source_target_pairs={{0,1},{1,0},{2,3},{3,2},{4,5},{5,4},{6,7},{7,6},{8,9},{9,8},{10,11... | collective-permute-start | bytes 786440 | tf_op jit(solution)/shard_map/ppermute | solution.py:468
  141.6 2.3 %copy-start.8 = (bf16[1,256,1536]{2,1,0:T(8,128)(2,1)S(1)}, bf16[1,256,1536]{2,1,0:T(8,128)(2,1)}, u32[]{:S(2)}) copy-start(bf16[1,256,1536]{2,1,0:T(8,128)(2,1)} %param.7) | copy-start | bytes 2359300
  143.8 26.7 %collective-permute-start.19 = (bf16[512,512]{1,0:T(8,128)(2,1)S(1)}, bf16[512,512]{1,0:T(8,128)(2,1)S(1)}, u32[]{:S(2)}, u32[]{:S(2)}) collective-permute-start(bf16[512,512]{1,0:T(8,128)(2,1)S(1)} %partner_far_grads.5._), channel_id=1, source_target_pairs={{0,1},{1,0},{2,3},{3,2},{4,5},{5,4},{6,7},{7,6},{8,9},{9,8},{10,11... | collective-permute-start | bytes 1572872 | tf_op jit(solution)/shard_map/ppermute | solution.py:468
  146.5 11.9 %collective-permute-start.17 = (bf16[512,256]{1,0:T(8,128)(2,1)S(1)}, bf16[512,256]{1,0:T(8,128)(2,1)S(1)}, u32[]{:S(2)}, u32[]{:S(2)}) collective-permute-start(bf16[512,256]{1,0:T(8,128)(2,1)S(1)} %get-tuple-element.67._.__), channel_id=1, source_target_pairs={{1,2},{2,1},{3,4},{4,3},{5,6},{6,5},{7,8},{8,7},{9,10},{10,9},{11,... | collective-permute-start | bytes 786440 | tf_op jit(solution)/shard_map/ppermute | solution.py:471
  153.1 17.4 %collective-permute-start.20 = (bf16[512,512]{1,0:T(8,128)(2,1)S(1)}, bf16[512,512]{1,0:T(8,128)(2,1)S(1)}, u32[]{:S(2)}, u32[]{:S(2)}) collective-permute-start(bf16[512,512]{1,0:T(8,128)(2,1)S(1)} %partner_far_grads.6._.__), channel_id=1, source_target_pairs={{0,1},{1,0},{2,3},{3,2},{4,5},{5,4},{6,7},{7,6},{8,9},{9,8},{10,11... | collective-permute-start | bytes 1572872 | tf_op jit(solution)/shard_map/ppermute | solution.py:468
  160.2 10.3 %collective-permute-start.21 = (bf16[512,256]{1,0:T(8,128)(2,1)S(1)}, bf16[512,256]{1,0:T(8,128)(2,1)S(1)}, u32[]{:S(2)}, u32[]{:S(2)}) collective-permute-start(bf16[512,256]{1,0:T(8,128)(2,1)S(1)} %partner_far_grads.7.refs_4_), channel_id=1, source_target_pairs={{0,1},{1,0},{2,3},{3,2},{4,5},{5,4},{6,7},{7,6},{8,9},{9,8},{10,11... | collective-permute-start | bytes 786440 | tf_op jit(solution)/shard_map/ppermute | solution.py:468
  160.6 10.0 %copy-start.10 = (bf16[1,256,1536]{2,1,0:T(8,128)(2,1)S(1)}, bf16[1,256,1536]{2,1,0:T(8,128)(2,1)}, u32[]{:S(2)}) copy-start(bf16[1,256,1536]{2,1,0:T(8,128)(2,1)} %param.8) | copy-start | bytes 2359300
  (4 other events, 4.0 us)
